TPU v7x, 32 devices: a whole 2x2x4 slice. The times are simulated.
32 devices in a mesh: groups: 2 (over x), rows: 2 (over core), cols: 8 (over z, y).
Axes of the slice: x: 2, y: 2, z: 4, core: 2. Of those that a mesh axis runs over, the one named last changes fastest.
Arguments:
- feats: bfloat16 [16, 256, 256], P(('groups', 'rows'), 'cols'), parts along dimension 0, may hold values from -6 to 6
- w_in: bfloat16 [256, 512], replicated, may hold values from -0.375 to 0.375
- conv_w: float32 [9, 256], replicated, may hold values from -2 to 2
- conv_b: float32 [256], replicated, may hold values from -3 to 3
- w_proj: bfloat16 [4, 256, 144], replicated, may hold values from -0.375 to 0.375
- dt_bias: float32 [4, 16], replicated, may hold values from -4 to 1
- a_rate: float32 [4, 16], replicated, may hold values from 0.0001953125 to 0.1
- d_skip: float32 [4, 16], replicated, may hold values from 0.5 to 1.5
- norm_gain: float32 [256], replicated, may hold values from 0.1 to 1.9
- w_out: bfloat16 [256, 256], replicated, may hold values from -0.375 to 0.375
Outputs:
- mixed: bfloat16 [16, 256, 256], P(('groups', 'rows'), 'cols'), parts along dimension 0
There are 2 independent parts, one for each index of `groups`. A program takes and returns all parts, laid end to end along the dimension named above; an argument that names none is the same for every part. Nothing has to cross between parts.
All inputs are finite; a program needn't handle non-finite values.
Results may differ from a plain program's by a relative error of at most 0.0097.
Values may be sent and summed in bfloat16 or wider, within the bound.
No kernel may reach another device: no remote copies, remote signals or barrier semaphores. Data moves between devices by JAX's collectives and lax.ppermute only.
A program may use at most 128 MiB of HBM per device.

v0:
```python
import math

import jax
import jax.numpy as jnp
from jax import lax
from jax.sharding import PartitionSpec as P

norm_eps = 1e-05


def entering(value, axis, join, neutral, backward):
    count, mine = (lax.axis_size(axis), lax.axis_index(axis))
    pieces = jax.tree.map(lambda part: lax.all_gather(part, axis), value)
    if backward:
        pieces = jax.tree.map(lambda part: part[::-1], pieces)
        mine = count - 1 - mine
    so_far = jax.tree.map(
        lambda part, zero: jnp.full_like(part, 0) + jnp.asarray(zero, part.dtype), value, neutral
    )

    def turn(position, so_far):
        longer = join(so_far, jax.tree.map(lambda part: part[position], pieces))
        return jax.tree.map(lambda new, old: jnp.where(position < mine, new, old), longer, so_far)

    return lax.fori_loop(0, count - 1, turn, so_far)


def padded_2(block, sides, width):
    for axis, dim in sides:
        count = lax.axis_size(axis)
        forward = [(i, i + 1) for i in range(count - 1)]
        backward = [(target, source) for source, target in forward]
        low = lax.ppermute(
            lax.slice_in_dim(block, block.shape[dim] - width, None, axis=dim), axis, forward
        )
        high = lax.ppermute(lax.slice_in_dim(block, 0, width, axis=dim), axis, backward)
        block = jnp.concatenate([low, block, high], axis=dim)
    return block


def block_terms(inputs, step_sizes, write_vec, read_vec, rates, skips):
    seq_count, length, features = inputs.shape
    head_count = rates.shape[0]
    head_size = features // head_count
    cumul = jnp.cumsum(-step_sizes * rates, axis=1)
    scores = jnp.einsum("rtn,rsn->rts", read_vec, write_vec, preferred_element_type=jnp.float32)
    places = jnp.arange(length)
    lower = places[:, None] >= places[None, :]
    cum_heads = jnp.swapaxes(cumul, 1, 2)
    gaps = cum_heads[:, :, :, None] - cum_heads[:, :, None, :]
    decays = jnp.where(lower, jnp.exp(jnp.minimum(gaps, 0.0)), 0.0)
    steps_heads = jnp.swapaxes(step_sizes, 1, 2)
    weights = (scores[:, None, :, :] * decays * steps_heads[:, :, None, :]).astype(jnp.bfloat16)
    per_head = inputs.reshape(seq_count, length, head_count, head_size)
    within = jnp.einsum("rhts,rshp->rthp", weights, per_head, preferred_element_type=jnp.float32)
    within = within + skips[:, None] * per_head.astype(jnp.float32)
    to_end = jnp.exp(cumul[:, -1:, :] - cumul) * step_sizes
    scaled = (per_head.astype(jnp.float32) * to_end[..., None]).astype(jnp.bfloat16)
    states = jnp.einsum("rsn,rshp->rnhp", write_vec, scaled, preferred_element_type=jnp.float32)
    nstate = write_vec.shape[2]
    return (
        within.reshape(seq_count, length, features),
        states.reshape(seq_count, nstate, features),
        jnp.exp(cumul[:, -1, :]),
        cumul,
    )


def grouped_terms(inputs, step_sizes, write_vec, read_vec, rates, skips):
    seq_count = inputs.shape[0]
    group = math.gcd(seq_count, 8)

    def split_rows(array):
        return array.reshape((seq_count // group, group) + array.shape[1:])

    def one_group(pieces):
        return block_terms(pieces[0], pieces[1], pieces[2], pieces[3], rates, skips)

    results = lax.map(
        one_group,
        (split_rows(inputs), split_rows(step_sizes), split_rows(write_vec), split_rows(read_vec)),
    )
    return tuple((part.reshape((seq_count,) + part.shape[2:]) for part in results))


def correction(read_vec, cumul, carried):
    seq_count, length, nstate = read_vec.shape
    features = carried.shape[-1]
    head_count = cumul.shape[-1]
    reads = jnp.einsum(
        "rtn,rnd->rtd", read_vec.astype(jnp.float32), carried, precision=lax.Precision.HIGHEST
    )
    reads = (
        reads.reshape(seq_count, length, head_count, features // head_count)
        * jnp.exp(cumul)[..., None]
    )
    return reads.reshape(seq_count, length, features)


def advance_state(carried, decays, added):
    seq_count, nstate, features = carried.shape
    head_count = decays.shape[-1]
    kept = (
        carried.reshape(seq_count, nstate, head_count, features // head_count)
        * decays[:, None, :, None]
    )
    return kept.reshape(seq_count, nstate, features) + added


def chain(earlier, later):
    return (earlier[0] * later[0], advance_state(earlier[1], later[0], later[1]))


def direction_inputs(seqs, weight, bias, head_count):
    seq_count, length, features = seqs.shape
    projected = jnp.dot(seqs.reshape(-1, features), weight, preferred_element_type=jnp.float32)
    projected = projected.reshape(seq_count, length, -1)
    nstate = (projected.shape[-1] - head_count) // 2
    step_sizes = jax.nn.softplus(projected[..., :head_count] + bias)
    write_vec = projected[..., head_count : head_count + nstate].astype(jnp.bfloat16)
    read_vec = projected[..., head_count + nstate :].astype(jnp.bfloat16)
    return (step_sizes, write_vec, read_vec)


def horizontal(mixed_in, weight, bias, rates, skips, backward):
    seqs = jnp.flip(mixed_in, 1) if backward else mixed_in
    step_sizes, write_vec, read_vec = direction_inputs(seqs, weight, bias, rates.shape[0])
    within, added, decays, cumul = grouped_terms(
        seqs, step_sizes, write_vec, read_vec, rates, skips
    )
    neutral = (jnp.ones_like(decays), jnp.zeros_like(added))
    if backward:
        incoming = entering((decays, added), "cols", chain, neutral, True)
    else:
        incoming = entering((decays, added), "cols", chain, neutral, False)
    results = within + correction(read_vec, cumul, incoming[1])
    return jnp.flip(results, 1) if backward else results


def column_pass(columns, weight, bias, rates, skips, backward):
    seqs = jnp.flip(columns, 1) if backward else columns
    step_sizes, write_vec, read_vec = direction_inputs(seqs, weight, bias, rates.shape[0])
    within, added, decays, cumul = grouped_terms(
        seqs, step_sizes, write_vec, read_vec, rates, skips
    )
    neutral = (jnp.ones_like(decays), jnp.zeros_like(added))
    if backward:
        incoming = entering((decays, added), "rows", chain, neutral, True)
    else:
        incoming = entering((decays, added), "rows", chain, neutral, False)
    results = within + correction(read_vec, cumul, incoming[1])
    return jnp.flip(results, 1) if backward else results


def shards(feats, w_in, conv_w, conv_b, w_proj, dt_bias, a_rate, d_skip, norm_gain, w_out):
    tile_rows, tile_cols, features = feats.shape
    both = jnp.dot(feats.reshape(-1, features), w_in, preferred_element_type=jnp.float32)
    both = both.reshape(tile_rows, tile_cols, 2 * features)
    pre_conv = both[..., :features].astype(jnp.bfloat16)
    gate_in = both[..., features:]
    padded = padded_2(pre_conv, (("rows", 0), ("cols", 1)), 1)
    conv_sum = conv_b + jnp.zeros((tile_rows, tile_cols, features), jnp.float32)
    for offset in range(9):
        top = offset // 3
        left = offset % 3
        conv_sum = conv_sum + conv_w[offset] * padded[
            top : top + tile_rows, left : left + tile_cols
        ].astype(jnp.float32)
    mixed_in = jax.nn.silu(conv_sum).astype(jnp.bfloat16)
    across = horizontal(mixed_in, w_proj[0], dt_bias[0], a_rate[0], d_skip[0], False)
    across = across + horizontal(mixed_in, w_proj[1], dt_bias[1], a_rate[1], d_skip[1], True)
    columns = jnp.swapaxes(mixed_in, 0, 1)
    down = column_pass(columns, w_proj[2], dt_bias[2], a_rate[2], d_skip[2], False)
    down = down + column_pass(columns, w_proj[3], dt_bias[3], a_rate[3], d_skip[3], True)
    vertical = jnp.swapaxes(down, 0, 1).astype(jnp.bfloat16)
    combined = across + vertical.astype(jnp.float32)
    centre = combined - jnp.mean(combined, axis=-1, keepdims=True)
    normed = (
        centre * lax.rsqrt(jnp.mean(centre * centre, axis=-1, keepdims=True) + norm_eps) * norm_gain
    )
    gated = (normed * jax.nn.silu(gate_in)).astype(jnp.bfloat16)
    output = jnp.dot(gated.reshape(-1, features), w_out, preferred_element_type=jnp.float32)
    return output.reshape(tile_rows, tile_cols, features).astype(jnp.bfloat16)


def solution(mesh):
    in_specs = (P(("groups", "rows"), "cols", None), P(), P(), P(), P(), P(), P(), P(), P(), P())
    out_specs = P(("groups", "rows"), "cols", None)
    return jax.shard_map(shards, mesh=mesh, in_specs=in_specs, out_specs=out_specs, check_vma=False)
```

profile of v0, /device:TPU:0, one launch (start us, length us, event | category | flops | bytes accessed | tf_op | source)
XLA Modules:
  0.0 201.7 jit_solution(17799183301293330654)
XLA Ops:
  7.5 1.7 fusion.135
  9.2 1.3 collective-permute-start.1
  10.5 3.0 %collective-permute-start = (bf16[1,32,256]{2,1,0:T(8,128)(2,1)S(1)}, bf16[1,32,256]{2,1,0:T(8,128)(2,1)S(1)}, u32[]{:S(2)}, u32[]{:S(2)}) collective-permute-start(bf16[1,32,256]{2,1,0:T(8,128)(2,1)S(1)} %get-tuple-element.625), channel_id=1, source_target_pairs={{0,8},{1,9},{2,10},{3,11},{4,12},{5,13},{6,14},{7,15},{16,24},{17,... | collective-permute-start | bytes 49160 | tf_op jit(solution)/shard_map/ppermute | solution.py:33
  15.4 4.9 %collective-permute-start.2 = (bf16[6,1,256]{2,1,0:T(2,128)(2,1)S(1)}, bf16[6,1,256]{2,1,0:T(2,128)(2,1)S(1)}, u32[]{:S(2)}, u32[]{:S(2)}) collective-permute-start(bf16[6,1,256]{2,1,0:T(2,128)(2,1)S(1)} %get-tuple-element.629), channel_id=1, source_target_pairs={{0,1},{1,2},{2,3},{3,4},{4,5},{5,6},{6,7},{8,9},{9,10},{10,11},{11... | collective-permute-start | bytes 9224 | tf_op jit(solution)/shard_map/ppermute | solution.py:33
  20.3 1.3 collective-permute-start.3
  21.6 1.4 fusion.134
  23.1 2.8 %collective-permute-done.3 = bf16[6,1,256]{2,1,0:T(2,128)(2,1)S(1)} collective-permute-done((bf16[6,1,256]{2,1,0:T(2,128)(2,1)S(1)}, bf16[6,1,256]{2,1,0:T(2,128)(2,1)S(1)}, u32[]{:S(2)}, u32[]{:S(2)}) %collective-permute-start.3) | collective-permute-done | bytes 3104 | tf_op jit(solution)/shard_map/ppermute | solution.py:36
  37.1 1.6 broadcast.117.clone2.1
  39.9 30.9 %while.15 = (s32[]{:T(128)}, f32[4,8,4,256]{3,1,0,2:T(8,128)}, f32[4,8,64,256]{3,2,1,0:T(8,128)}, f32[4,8,16]{2,1,0:T(8,128)}, f32[4,8,4,16]{3,1,2,0:T(8,128)}, ...) while((s32[]{:T(128)}, f32[4,8,4,256]{3,1,0,2:T(8,128)}, ...), condition=%wide.region_11.12_spmd, body=%wide.region_9.11_spmd.sunk | while | flops 1195538 | bytes 3050233 | solution.py:79
  40.0 1.2 bitcast_dynamic-update-slice_fusion.15
  47.8 1.2 bitcast_dynamic-update-slice_fusion.15
  55.5 1.2 bitcast_dynamic-update-slice_fusion.15
  70.8 1.6 fusion.129
  73.1 1.5 broadcast.117.clone2
  75.3 25.8 %while.14 = (s32[]{:T(128)}, f32[4,8,4,256]{3,1,0,2:T(8,128)}, f32[4,8,64,256]{3,2,1,0:T(8,128)}, f32[4,8,16]{2,1,0:T(8,128)}, f32[4,8,4,16]{3,1,2,0:T(8,128)S(1...) while((s32[]{:T(128)}, f32[4,8,4,256]{3,1,0,2:T(8,128)}, ...), condition=%wide.region_8.9_spmd, body=%wide.region_6.8_spmd.sunk | while | flops 1195538 | bytes 3064121 | solution.py:79
  102.8 1.8 all_gather.28
  107.2 1.8 all_gather.30
  112.4 26.8 %all-gather.1 = f32[32,1,16]{2,1,0:T(1,128)S(1)} all-gather(f32[4,1,16]{2,1,0:T(1,128)S(1)} %copy-done.18), channel_id=3, replica_groups=mesh['groups'=2,'rows'=2,'cols'=8] {'cols'}, dimensions={0}, use_global_device_ids=true | all-gather | bytes 2304 | tf_op jit(solution)/shard_map/all_gather | solution.py:13
  141.1 26.3 %all-gather = f32[32,1,16]{2,1,0:T(1,128)S(1)} all-gather(f32[4,1,16]{2,1,0:T(1,128)S(1)} %copy-done.19), channel_id=2, replica_groups=mesh['groups'=2,'rows'=2,'cols'=8] {'cols'}, dimensions={0}, use_global_device_ids=true | all-gather | bytes 2304 | tf_op jit(solution)/shard_map/all_gather | solution.py:13
  167.5 1.8 rev.26
  169.3 7.0 %while.17 = (s32[]{:T(128)}, f32[4,64,256]{2,1,0:T(8,128)S(1)}, s32[]{:T(128)}, f32[8,4,16]{2,1,0:T(4,128)}, f32[8,4,64,256]{3,2,1,0:T(8,128)S(1)}, /*index=5*/s32[]{:T(128)}, s32[]{:T(128)}) while((s32[]{:T(128)}, f32[4,64,256]{2,1,0:T(8,128)S(1)}, s32[]{:T(128)}, f32[8,4,16]{2,1,0:T(4,128)}, f32[8,4,64,256]{3,2,1,0:T(8,128)S(1)}, ...), condition=%wide.region_5.6_spmd.clone, body=%wide.region_4.5_spmd.clone.sunk | while | flops 262148 | bytes 803697 | solution.py:25
  177.6 8.9 %while.16 = (s32[]{:T(128)}, f32[4,64,256]{2,1,0:T(8,128)S(1)}, s32[]{:T(128)}, f32[8,4,16]{2,1,0:T(4,128)S(1)}, f32[8,4,64,256]{3,2,1,0:T(8,128)}, /*index=5*/s32[]{:T(128)}, s32[]{:T(128)}) while((s32[]{:T(128)}, f32[4,64,256]{2,1,0:T(8,128)S(1)}, s32[]{:T(128)}, f32[8,4,16]{2,1,0:T(4,128)S(1)}, f32[8,4,64,256]{3,2,1,0:T(8,128)}, ...), condition=%wide.region_2.3_spmd.clone, body=%wide.region_1.2_spmd.clone.sunk | while | flops 262148 | bytes 803697 | solution.py:25
  186.6 2.6 %fusion.54 = f32[32,4,256]{2,1,0:T(4,128)S(1)} fusion(f32[2,32,64,256]{3,2,1,0:T(8,128)} %all-gather.13.cloned.1.call-done, f32[32,256]{1,0:T(8,128)S(1)} %copy-done.16, pred[]{:T(512)S(6)} %lt.61, bf16[32,4,64]{2,0,1:T(8,128)(2,1)S(1)} %copy-done.13), kind=kOutput, calls=%fused_computation.89 | convolution fusion | flops 26214400 | bytes 2277377 | tf_op jit(solution)/shard_map/rtn,rnd->rtd/dot_general | solution.py:90
  190.2 2.5 %fusion.58 = f32[32,4,256]{2,1,0:T(4,128)S(1)} fusion(f32[2,32,64,256]{3,2,1,0:T(8,128)} %all-gather.11.cloned.1.call-done, f32[32,256]{1,0:T(8,128)S(1)} %copy-done.15, pred[]{:T(512)S(6)} %lt.60, bf16[32,4,64]{2,0,1:T(8,128)(2,1)S(1)} %copy-done.14), kind=kOutput, calls=%fused_computation.93 | convolution fusion | flops 26214400 | bytes 2277377 | tf_op jit(solution)/shard_map/rtn,rnd->rtd/dot_general | solution.py:90
  (363 shorter events, 99.0 us)
Async XLA Ops:
  6.5 20.5 %copy-start.7 = (bf16[4,256,144]{1,2,0:T(8,128)(2,1)S(1)}, bf16[4,256,144]{1,2,0:T(8,128)(2,1)}, u32[]{:S(2)}) copy-start(bf16[4,256,144]{1,2,0:T(8,128)(2,1)} %param.22) | copy-start | bytes 884740
  6.5 160.9 %all-gather.9.cloned.1.call-start = ((), (), s32[]{:S(2)}) async-start(), calls=%async_computation.1 | async-start | bytes 2359296 | tf_op jit(solution)/shard_map/all_gather | solution.py:13
  9.2 6.2 %collective-permute-start.1 = (bf16[1,32,256]{2,1,0:T(8,128)(2,1)S(1)}, bf16[1,32,256]{2,1,0:T(8,128)(2,1)S(1)}, u32[]{:S(2)}, u32[]{:S(2)}) collective-permute-start(bf16[1,32,256]{2,1,0:T(8,128)(2,1)S(1)} %get-tuple-element.626), channel_id=1, source_target_pairs={{8,0},{9,1},{10,2},{11,3},{12,4},{13,5},{14,6},{15,7},{24,16},{25,... | collective-permute-start | bytes 49160 | tf_op jit(solution)/shard_map/ppermute | solution.py:36
  10.5 4.9 %collective-permute-start = (bf16[1,32,256]{2,1,0:T(8,128)(2,1)S(1)}, bf16[1,32,256]{2,1,0:T(8,128)(2,1)S(1)}, u32[]{:S(2)}, u32[]{:S(2)}) collective-permute-start(bf16[1,32,256]{2,1,0:T(8,128)(2,1)S(1)} %get-tuple-element.625), channel_id=1, source_target_pairs={{0,8},{1,9},{2,10},{3,11},{4,12},{5,13},{6,14},{7,15},{16,24},{17,... | collective-permute-start | bytes 49160 | tf_op jit(solution)/shard_map/ppermute | solution.py:33
  15.4 7.6 %collective-permute-start.2 = (bf16[6,1,256]{2,1,0:T(2,128)(2,1)S(1)}, bf16[6,1,256]{2,1,0:T(2,128)(2,1)S(1)}, u32[]{:S(2)}, u32[]{:S(2)}) collective-permute-start(bf16[6,1,256]{2,1,0:T(2,128)(2,1)S(1)} %get-tuple-element.629), channel_id=1, source_target_pairs={{0,1},{1,2},{2,3},{3,4},{4,5},{5,6},{6,7},{8,9},{9,10},{10,11},{11... | collective-permute-start | bytes 9224 | tf_op jit(solution)/shard_map/ppermute | solution.py:33
  20.3 5.5 %collective-permute-start.3 = (bf16[6,1,256]{2,1,0:T(2,128)(2,1)S(1)}, bf16[6,1,256]{2,1,0:T(2,128)(2,1)S(1)}, u32[]{:S(2)}, u32[]{:S(2)}) collective-permute-start(bf16[6,1,256]{2,1,0:T(2,128)(2,1)S(1)} %get-tuple-element.630), channel_id=1, source_target_pairs={{1,0},{2,1},{3,2},{4,3},{5,4},{6,5},{7,6},{9,8},{10,9},{11,10},{12... | collective-permute-start | bytes 9224 | tf_op jit(solution)/shard_map/ppermute | solution.py:36
  23.1 7.7 %copy-start.21 = (f32[4,16]{1,0:T(4,128)S(1)}, f32[4,16]{1,0:T(4,128)}, u32[]{:S(2)}) copy-start(f32[4,16]{1,0:T(4,128)} %param.25) | copy-start | bytes 772
  30.0 147.5 %all-gather.7.cloned.1.call-start = ((), (), s32[]{:S(2)}) async-start(), calls=%async_computation | async-start | bytes 2359296 | tf_op jit(solution)/shard_map/all_gather | solution.py:13
  36.3 150.2 %all-gather.13.cloned.1.call-start = ((), (), s32[]{:S(2)}) async-start(), calls=%async_computation.3 | async-start | bytes 6291456 | tf_op jit(solution)/shard_map/all_gather | solution.py:13
  72.4 117.8 %all-gather.11.cloned.1.call-start = ((), (), s32[]{:S(2)}) async-start(), calls=%async_computation.2 | async-start | bytes 6291456 | tf_op jit(solution)/shard_map/all_gather | solution.py:13
  101.0 6.1 %copy-start.17 = (f32[4,8,16]{2,1,0:T(8,128)S(1)}, f32[4,8,16]{2,1,0:T(8,128)}, u32[]{:S(2)}) copy-start(f32[4,8,16]{2,1,0:T(8,128)} %get-tuple-element.422) | copy-start | bytes 6148
  101.0 8.7 %copy-start.9 = (f32[4,16,32]{1,2,0:T(8,128)S(1)}, f32[4,16,32]{1,2,0:T(8,128)}, u32[]{:S(2)}) copy-start(f32[4,16,32]{1,2,0:T(8,128)} %get-tuple-element.624) | copy-start | bytes 24580
  101.0 8.8 %copy-start.2 = (bf16[4,32,144]{2,1,0:T(8,128)(2,1)S(1)}, bf16[4,32,144]{2,1,0:T(8,128)(2,1)}, u32[]{:S(2)}) copy-start(bf16[4,32,144]{2,1,0:T(8,128)(2,1)} %copy-done.1) | copy-start | bytes 110596
  101.0 9.1 %copy-start.20 = (pred[32,32]{1,0:T(8,128)(4,1)S(1)}, pred[32,32]{1,0:T(8,128)(4,1)}, u32[]{:S(2)}) copy-start(pred[32,32]{1,0:T(8,128)(4,1)} %iota_compare_fusion.2) | copy-start | bytes 3076
  101.0 9.1 %copy-start.23 = (f32[16]{0:T(128)S(1)}, f32[16]{0:T(128)}, u32[]{:S(2)}) copy-start(f32[16]{0:T(128)} %get-tuple-element.653) | copy-start | bytes 196
  106.3 5.2 %copy-start.8 = (f32[4,32,16]{2,1,0:T(8,128)S(1)}, f32[4,32,16]{2,1,0:T(8,128)}, u32[]{:S(2)}) copy-start(f32[4,32,16]{2,1,0:T(8,128)} %get-tuple-element.640) | copy-start | bytes 24580
  110.1 29.7 %copy-start.11 = (f32[4,16,32]{1,2,0:T(8,128)S(1)}, f32[4,16,32]{1,2,0:T(8,128)}, u32[]{:S(2)}) copy-start(f32[4,16,32]{1,2,0:T(8,128)} %get-tuple-element.622) | copy-start | bytes 24580
  110.1 30.0 %copy-start.22 = (f32[16]{0:T(128)S(1)}, f32[16]{0:T(128)}, u32[]{:S(2)}) copy-start(f32[16]{0:T(128)} %get-tuple-element.654) | copy-start | bytes 196
  111.6 29.3 %copy-start.10 = (f32[4,32,16]{2,1,0:T(8,128)S(1)}, f32[4,32,16]{2,1,0:T(8,128)}, u32[]{:S(2)}) copy-start(f32[4,32,16]{2,1,0:T(8,128)} %get-tuple-element.637) | copy-start | bytes 24580
  169.2 7.0 %copy-start.3 = (bf16[4,32,144]{2,1,0:T(8,128)(2,1)S(1)}, bf16[4,32,144]{2,1,0:T(8,128)(2,1)}, u32[]{:S(2)}) copy-start(bf16[4,32,144]{2,1,0:T(8,128)(2,1)} %copy-done.1) | copy-start | bytes 110596
  169.2 7.0 %copy-start.6 = (f32[4,32,256]{2,1,0:T(8,128)S(1)}, f32[4,32,256]{2,1,0:T(8,128)}, u32[]{:S(2)}) copy-start(f32[4,32,256]{2,1,0:T(8,128)} %copy.198) | copy-start | bytes 393220
  177.6 9.0 %copy-start.13 = (bf16[32,4,64]{2,0,1:T(8,128)(2,1)S(1)}, bf16[32,4,64]{2,0,1:T(8,128)(2,1)}, u32[]{:S(2)}) copy-start(bf16[32,4,64]{2,0,1:T(8,128)(2,1)} %get-tuple-element.631) | copy-start | bytes 49156
  177.6 9.0 %copy-start.16 = (f32[32,256]{1,0:T(8,128)S(1)}, f32[32,256]{1,0:T(8,128)}, u32[]{:S(2)}) copy-start(f32[32,256]{1,0:T(8,128)} %copy.218) | copy-start | bytes 98308
  186.6 6.2 %copy-start.4 = (f32[32,4,256]{2,0,1:T(8,128)S(1)}, f32[32,4,256]{2,0,1:T(8,128)}, u32[]{:S(2)}) copy-start(f32[32,4,256]{2,0,1:T(8,128)} %copy.211) | copy-start | bytes 393220
  (10 other events, 33.9 us)
Sparse Core Ops, SparseCore 0:
  30.2 50.2 all-gather.8
  82.5 47.7 all-gather.6
  131.9 12.2 all-gather.12
  167.6 11.2 all-gather.10
where the time goes:
time: 203 us; the launch traced here: 202 us
  local copies, waits for them, and re-layouts  66 us (33%)
  blocking collectives  56.7 us (28%)
  matrix products  29.4 us (14%)
  other arithmetic  21.7 us (11%)
  between operations  13.7 us (7%)
  starting transfers between devices  10.6 us (5%)
  waiting for transfers between devices  2.96 us (1%)
    all_gather x4, blocking collectives, entering(): pieces = jax.tree.map(lambda part: lax.all_gather(part, axis), value)  56.7 us
    dynamic_update_slice x32, local copies, waits for them, and re-layouts, grouped_terms(): lax.map(one_group, (split_rows(inputs), split_rows(step_sizes), split_row...  19 us
    dot_general x10, matrix products, block_terms(): jnp.einsum('rhts,rshp->rthp', weights, per_head, preferred_element_type=j...  8.98 us
    dynamic_slice x16, local copies, waits for them, and re-layouts, grouped_terms(): lax.map(one_group, (split_rows(inputs), split_rows(step_sizes), split_row...  8.63 us
    select_n x14, other arithmetic, turn(): jnp.where(position < mine, new, old)  8.48 us
    mul x46, local copies, waits for them, and re-layouts, advance_state(): carried.reshape(seq_count, nstate, head_count, features // head_count)  8.48 us
    ppermute x2, starting transfers between devices, padded_2(): lax.ppermute(lax.slice_in_dim(block, block.shape[dim] - width, None, axis...  7.93 us
    another operation x10, other arithmetic, block_terms(): cumul = jnp.cumsum(-step_sizes * rates, axis=1)  7.7 us
  transfers between devices with their start and end apart: 8, of which 1 were waited for; matrix products, arithmetic and copies ran while one was open for 52% of the time, Pallas kernels for 0%

commit v1 on v0

v1 whole, which is shorter than its diff:
```python
import functools

import jax
import jax.numpy as jnp
from jax import lax
from jax.experimental import pallas as pl
from jax.experimental.pallas import tpu as pltpu
from jax.sharding import PartitionSpec as P

norm_eps = 1e-05
f32, bf16 = jnp.float32, jnp.bfloat16
TH, TW, D, NH, NS = 4, 32, 256, 16, 64
HALO = 176


def dot(a, b):
    return jnp.dot(a, b, preferred_element_type=f32)


def dot_t(a, b):
    return lax.dot_general(a, b, (((1,), (1,)), ((), ())), preferred_element_type=f32)


def split(a):
    high = a.astype(bf16)
    return high, (a - high.astype(f32)).astype(bf16)


def dot_wide(a, mask):
    high, low = split(a)
    return dot(high, mask) + dot(low, mask)


def wide_dot(mask, b):
    high, low = split(b)
    return dot(mask, high) + dot(mask, low)


def softplus(x):
    return jnp.maximum(x, 0.0) + jnp.log1p(jnp.exp(-jnp.abs(x)))


def silu(x):
    return x * jax.nn.sigmoid(x)


def iotas(rows, lanes):
    return (
        lax.broadcasted_iota(jnp.int32, (rows, lanes), 0),
        lax.broadcasted_iota(jnp.int32, (rows, lanes), 1),
    )


def ones_where(mask):
    return jnp.where(mask, 1.0, 0.0).astype(bf16)


def at(g, j):
    start = g * (8 * TW) + TW * j
    return pl.ds(start if isinstance(start, int) else pl.multiple_of(start, TW), TW)


def each(count, body):
    if count == 1:
        body(0)
    else:
        lax.fori_loop(0, count, lambda i, carry: (body(i), carry)[1], 0)


def kernel(nb, gathered, place, *refs):
    count = 1 if gathered else nb
    blocks, refs = refs[:count], refs[count:]
    own_block, far, w_in, conv_w, conv_b, w_proj, dt_bias, a_rate, d_skip, gain, w_out, out = refs[:12]
    pre, strip, mixed, la_all, dt_all, totals, writes, scaled = refs[12:]
    row, col = place[0], place[1]
    lower = row == 1
    ng = nb // 8
    w_x = w_in[:, :D]

    def pre_conv(tokens):
        return dot(tokens, w_x).astype(bf16).astype(f32)

    pre[:, 0:8, :] = jnp.zeros((5, 8, D), f32)
    pre[:, 8 + nb * TW :, :] = jnp.zeros((5, 8, D), f32)

    def place_block(tokens, position):
        rows = pre_conv(tokens)
        base = pl.multiple_of(position * TW + 8, 8)
        for q in range(5):
            pre[q, pl.ds(base, TW), :] = rows[q * TW : (q + 1) * TW]

    if gathered:
        each(nb, lambda j: place_block(blocks[0][j, 0:160, :], j))
        left = blocks[0][jnp.maximum(col - 1, 0), 160:176, :]
        right = blocks[0][jnp.minimum(col + 1, nb - 1), 160:176, :]
    else:
        for step in range(nb):
            place_block(blocks[step][0:160, :], lax.rem(col - step + nb, nb))
        left, right = blocks[1][160:176, :], blocks[nb - 1][160:176, :]
    left = pre_conv(left) * jnp.where(col > 0, 1.0, 0.0)
    right = pre_conv(right) * jnp.where(col < nb - 1, 1.0, 0.0)
    far_pre = pre_conv(far[...])
    for i in range(3):
        strip[i, 8:40, :] = far_pre[i * TW : (i + 1) * TW]
        strip[i, 7:8, :] = left[8 + i : 9 + i]
        strip[i, 40:41, :] = right[i : i + 1]
    window = pl.multiple_of(col * TW, 32)
    for q in range(5):
        strip[3 + q] = pre[q, pl.ds(window, 48), :]

    taps = [
        [
            jnp.where(lower, conv_w[3 * a + b : 3 * a + b + 1, :], conv_w[3 * (2 - a) + b : 3 * (2 - a) + b + 1, :])
            for b in range(3)
        ]
        for a in range(3)
    ]
    bias = conv_b[...]

    def filtered(ref, count, q, base):
        total = jnp.broadcast_to(bias, (TW, D))
        for a in range(3):
            if 0 <= q + a - 1 < count:
                if not isinstance(base, int):
                    cells = ref[q + a - 1, pl.ds(pl.multiple_of(base - 8, 8), TW + 16), :]
                for b in range(3):
                    if isinstance(base, int):
                        value = ref[q + a - 1, base + b - 1 : base + b - 1 + TW, :]
                    else:
                        value = cells[7 + b : 7 + b + TW]
                    total = total + taps[a][b] * value
        return silu(total).astype(bf16)

    strip_mixed = [filtered(strip, 8, q, 8) for q in range(8)]
    own = jnp.concatenate(strip_mixed[4:], axis=0)
    column_tokens = jnp.concatenate(strip_mixed, axis=0)

    head_lane = ones_where(iotas(NH, 128)[1] % NH == iotas(NH, 128)[0])
    expand = ones_where(iotas(NH, D)[1] // NH == iotas(NH, D)[0])
    tok_r, tok_c = iotas(128, 128)
    same_row = tok_r // TW == tok_c // TW
    after = ones_where(same_row & (tok_c > tok_r))
    before = ones_where(same_row & (tok_c < tok_r))
    upto = ones_where(same_row & (tok_c <= tok_r))
    onward = ones_where(same_row & (tok_c >= tok_r))
    row_ones = ones_where(same_row)

    lane = lax.broadcasted_iota(jnp.int32, (1, 128), 1)
    bias_2 = dot_wide(dt_bias[0:2, :], head_lane)
    rate_2 = dot_wide(a_rate[0:2, :], head_lane)
    w_step = [dot(w_proj[k, :, 0:NH], head_lane) for k in range(2)]
    w_write = jnp.concatenate([w_proj[0, :, NH : NH + NS], w_proj[1, :, NH : NH + NS]], axis=1)

    def first_pass(g):
        group = lane // NH + g * 8
        is_left = group < col
        w_both = jnp.concatenate([jnp.where(is_left, w_step[0], w_step[1]).astype(bf16), w_write], axis=1)
        raw = jnp.zeros((128, 128), f32)
        for j in range(8):
            base = g * (8 * TW) + (8 + TW * j)
            for q in range(1, 5):
                mixed[g * 8 + j, (q - 1) * TW : q * TW, :] = filtered(pre, 5, q, base)
            result = dot(mixed[g * 8 + j], w_both)
            raw = jnp.where(lane // NH == j, result[:, :128], raw)
            block = g * 8 + j
            keep = jnp.where(lane < NS, jnp.where(block < col, 1.0, 0.0), jnp.where(block > col, 1.0, 0.0))
            vectors = (result[:, 128:] * keep).astype(bf16)
            for q in range(4):
                writes[q, at(g, j), :] = vectors[q * TW : (q + 1) * TW]
        steps = softplus(raw + jnp.where(is_left, bias_2[0:1], bias_2[1:2]))
        steps = jnp.where(group == col, 0.0, steps)
        logs = -steps * jnp.where(is_left, rate_2[0:1], rate_2[1:2])
        dt_all[g] = steps
        la_all[g] = logs
        totals[g] = wide_dot(row_ones, logs)

    each(ng, first_pass)

    both_ways = jnp.concatenate([after, before], axis=1)

    def second_pass(g):
        group = lane // NH + g * 8
        logs = la_all[g]
        stacked = jnp.concatenate([jnp.where(group < col, logs, 0.0), jnp.where(group > col, logs, 0.0)], axis=0)
        reach = wide_dot(both_ways, stacked)

        def add_group(other, total):
            source, target = other * 8 + tok_r // NH, g * 8 + tok_c // NH
            nearer = ((source > target) & (source < col)) | ((source < target) & (source > col))
            nearer = nearer & (tok_r % NH == tok_c % NH)
            return total + dot_wide(totals[other], ones_where(nearer))

        if ng == 1:
            reach = add_group(0, reach)
        else:
            reach = lax.fori_loop(0, ng, add_group, reach)
        weight = jnp.concatenate(split(jnp.exp(reach) * dt_all[g]), axis=1)
        expand_r, expand_c = iotas(256, D)
        for j in range(8):
            pick = ones_where((expand_r % 128) == j * NH + expand_c // NH)
            factor = dot(weight, pick)
            values = (mixed[g * 8 + j].astype(f32) * factor).astype(bf16)
            for q in range(4):
                scaled[q, at(g, j), :] = values[q * TW : (q + 1) * TW]

    each(ng, second_pass)

    projected = [dot(own, w_proj[k]) for k in range(2)]
    steps = [softplus(projected[k][:, :NH] + dt_bias[k : k + 1, :]) for k in range(2)]
    logs = [-steps[k] * a_rate[k : k + 1, :] for k in range(2)]
    write = [projected[k][:, NH : NH + NS].astype(bf16) for k in range(2)]
    read = [projected[k][:, NH + NS :].astype(bf16) for k in range(2)]
    from_edge = [
        dot_wide(jnp.exp(wide_dot(mask, logs[k])), expand) for k, mask in enumerate((upto, onward))
    ]
    pair_r, pair_c = iotas(NH, NH * TW)
    spread = ones_where(pair_c // TW == pair_r)
    inner_r, inner_c = iotas(128, NH * TW)
    inner_u, inner_s = inner_r % TW, inner_c % TW
    parts = []
    for k, keep in enumerate((inner_u > inner_s, inner_u < inner_s)):
        for part in split(logs[k]):
            parts.append(jnp.where(keep, dot(part, spread), 0.0).astype(bf16))
    step_parts = [jnp.where(inner_u == inner_s, dot_wide(steps[k], spread), 0.0) for k in range(2)]
    time_r, time_c = iotas(TW, TW)
    first, second = ones_where(time_c <= time_r), ones_where(time_c >= time_r)
    walk = jnp.concatenate([first, first, second, second], axis=1)
    local_t, local_s = iotas(TW, NH * TW)
    local_s = local_s % TW
    feature = lax.broadcasted_iota(jnp.int32, (TW, D), 1) // NH
    zeros = jnp.zeros((TW, NS), bf16)
    across = []
    for q in range(4):
        rows = slice(q * TW, (q + 1) * TW)
        gaps = dot(walk, jnp.concatenate([part[rows] for part in parts], axis=0))
        weights = jnp.zeros((TW, NH * TW), f32)
        for k, keep in enumerate((local_s <= local_t, local_s >= local_t)):
            scores = dot_t(read[k][rows], jnp.concatenate([write[k][rows]] * NH, axis=0))
            step_row = jnp.sum(step_parts[k][rows], axis=0, keepdims=True)
            weights = weights + jnp.where(keep, scores * step_row, 0.0)
        weights = (weights * jnp.exp(gaps)).astype(bf16)
        values = own[rows]
        spread_values = jnp.concatenate(
            [jnp.where(feature == h, values, jnp.zeros_like(values)) for h in range(NH)], axis=0
        )
        result = dot(weights, spread_values)
        state = lax.dot_general(writes[q], scaled[q], (((0,), (0,)), ((), ())), preferred_element_type=f32)
        reads = jnp.concatenate(
            [
                jnp.concatenate([read[0][rows], zeros], axis=1),
                jnp.concatenate([zeros, read[1][rows]], axis=1),
            ],
            axis=0,
        )
        entered = wide_dot(reads, state)
        result = result + entered[:TW] * from_edge[0][rows] + entered[TW:] * from_edge[1][rows]
        across.append(result)
    across = jnp.concatenate(across, axis=0)

    k_in = jnp.where(lower, 2, 3)
    k_out = jnp.where(lower, 3, 2)

    def pick_row(ref, k):
        return jnp.where(k == 2, ref[2:3, :], ref[3:4, :])

    project_in = dot(column_tokens, w_proj[k_in])
    project_out = dot(own, w_proj[k_out])
    steps_in = softplus(project_in[:, :NH] + pick_row(dt_bias, k_in))
    steps_out = softplus(project_out[:, :NH] + pick_row(dt_bias, k_out))
    logs_in = -steps_in * pick_row(a_rate, k_in)
    logs_out = -steps_out * pick_row(a_rate, k_out)
    write_in = project_in[:, NH : NH + NS].astype(bf16)
    write_out = project_out[:, NH : NH + NS].astype(bf16)
    read_in = project_in[128:, NH + NS :].astype(bf16)
    read_out = project_out[:, NH + NS :].astype(bf16)
    t_r, s_c = iotas(128, 256)
    same_col = (t_r % TW) == (s_c % TW)
    meet_in = ones_where(same_col)
    walk_in = ones_where(same_col & (s_c // TW <= t_r // TW + 4))
    meet_out = ones_where(tok_r % TW == tok_c % TW)
    walk_out = ones_where((tok_r % TW == tok_c % TW) & (tok_c >= tok_r))
    source_r, source_c = iotas(256, 128)
    source_u, source_s = source_r // TW, source_c // NH
    select = ones_where(source_u == source_s)
    scores_in = dot_wide(jnp.where(same_col, dot_t(read_in, write_in), 0.0), select)
    same_out = tok_r % TW == tok_c % TW
    scores_out = dot_wide(jnp.where(same_out, dot_t(read_out, write_out), 0.0), select[128:])
    out_u = tok_r // TW + 4
    out_s = tok_c // NH
    gap = jnp.zeros((128, 128), f32)
    for part in split(logs_in):
        gap = gap + dot(walk_in, jnp.where(source_u > source_s, dot(part, head_lane), 0.0).astype(bf16))
    for part in split(logs_out):
        gap = gap + dot(walk_out, jnp.where(out_u < out_s, dot(part, head_lane), 0.0).astype(bf16))
    lane_in = jnp.zeros((128, 128), f32)
    for part in split(steps_in):
        lane_in = lane_in + dot(meet_in, jnp.where(source_u == source_s, dot(part, head_lane), 0.0).astype(bf16))
    lane_out = jnp.zeros((128, 128), f32)
    for part in split(steps_out):
        lane_out = lane_out + dot(meet_out, jnp.where(out_u == out_s, dot(part, head_lane), 0.0).astype(bf16))
    weights = jnp.where(out_s <= out_u, scores_in * lane_in, 0.0) + jnp.where(out_s >= out_u, scores_out * lane_out, 0.0)
    weights = (weights * jnp.exp(gap)).astype(bf16)
    skips = dot_wide(d_skip[...], expand)
    own_wide = own.astype(f32)
    pick_r, pick_c = iotas(128, D)
    vertical = (skips[2:3] + skips[3:4]) * own_wide
    for s in range(8):
        factor = dot(weights, ones_where(pick_r == s * NH + pick_c // NH))
        values = strip_mixed[s].astype(f32)
        vertical = vertical + factor * jnp.concatenate([values] * 4, axis=0)
    combined = across + (skips[0:1] + skips[1:2]) * own_wide + vertical.astype(bf16).astype(f32)

    centre = combined - jnp.mean(combined, axis=-1, keepdims=True)
    normed = centre * lax.rsqrt(jnp.mean(centre * centre, axis=-1, keepdims=True) + norm_eps) * gain[...]
    gate_in = dot(own_block[TW:160, :], w_in[:, D:])
    gated = (normed * silu(gate_in)).astype(bf16)
    result = dot(gated, w_out[...]).astype(bf16)
    for i in range(4):
        out[jnp.where(lower, i, 3 - i)] = result[i * TW : (i + 1) * TW]


def shards(feats, w_in, conv_w, conv_b, w_proj, dt_bias, a_rate, d_skip, norm_gain, w_out):
    nb = lax.axis_size("cols")
    row, col = lax.axis_index("rows"), lax.axis_index("cols")
    partner = lax.ppermute(feats, "rows", [(0, 1), (1, 0)])
    ordered = jnp.concatenate([partner, feats], axis=0)
    turned = jnp.concatenate([partner[::-1], feats[::-1]], axis=0)
    ordered = jnp.where(row == 1, ordered, turned)
    far = ordered[:3]
    pad = jnp.zeros((5, D), bf16)
    sent = jnp.concatenate([ordered[3:].reshape(160, D), far[:, 0], pad, far[:, TW - 1], pad], axis=0)
    if nb == 8:
        blocks = [sent]
        for step in range(1, nb):
            blocks.append(lax.ppermute(sent, "cols", [(i, (i + step) % nb) for i in range(nb)]))
    else:
        blocks = [lax.all_gather(sent, "cols")]
    operands = [
        *blocks,
        sent,
        far.reshape(96, D),
        w_in,
        conv_w,
        conv_b[None],
        w_proj,
        dt_bias,
        a_rate,
        d_skip,
        norm_gain[None],
        w_out,
    ]
    vmem = pl.BlockSpec(memory_space=pltpu.VMEM)
    return pl.pallas_call(
        functools.partial(kernel, nb, nb != 8),
        out_shape=jax.ShapeDtypeStruct((TH, TW, D), bf16),
        in_specs=[pl.BlockSpec(memory_space=pltpu.SMEM)] + [vmem] * len(operands),
        out_specs=vmem,
        scratch_shapes=[
            pltpu.VMEM((5, nb * TW + 16, D), f32),
            pltpu.VMEM((8, 48, D), f32),
            pltpu.VMEM((nb, 128, D), bf16),
            pltpu.VMEM((nb // 8, 128, 128), f32),
            pltpu.VMEM((nb // 8, 128, 128), f32),
            pltpu.VMEM((nb // 8, 128, 128), f32),
            pltpu.VMEM((4, nb * TW, 128), bf16),
            pltpu.VMEM((4, nb * TW, D), bf16),
        ],
        cost_estimate=pl.CostEstimate(flops=2_000_000_000, bytes_accessed=4_000_000, transcendentals=1_000_000),
    )(jnp.stack([row, col]).astype(jnp.int32), *operands)


def solution(mesh):
    in_specs = (P(("groups", "rows"), "cols", None), P(), P(), P(), P(), P(), P(), P(), P(), P())
    out_specs = P(("groups", "rows"), "cols", None)
    return jax.shard_map(shards, mesh=mesh, in_specs=in_specs, out_specs=out_specs, check_vma=False)
```

time: 203 us -> 37.2 us (0.18)
  local copies, waits for them, and re-layouts: 66 us -> 3.73 us
  blocking collectives: 56.7 us -> 0 us
  matrix products: 29.4 us -> 0 us
  other arithmetic: 21.7 us -> 0.8 us
  between operations: 13.7 us -> 0.13 us
  Pallas kernels: 0 us -> 8.43 us
  waiting for transfers between devices: 2.96 us -> 11 us
  starting transfers between devices: 10.6 us -> 13 us
    all_gather x4 -> x0, blocking collectives: 56.7 us -> none  [entering(): pieces = jax.tree.map(lambda part: lax.all_gather(part, axis), value)]
    dot_general x38 -> x0, matrix products: 27.3 us -> none  [the longest x10 8.98 us: block_terms(): jnp.einsum('rhts,rshp->rthp', weights, per_head, preferred_element_type=j...]
    dynamic_update_slice x32 -> x0, local copies, waits for them, and re-layouts: 19 us -> none  [grouped_terms(): lax.map(one_group, (split_rows(inputs), split_rows(step_sizes), split_row...]
    mul x64 -> x0, local copies, waits for them, and re-layouts: 12.4 us -> none  [the longest x46 8.48 us: advance_state(): carried.reshape(seq_count, nstate, head_count, features // head_count)]
    dynamic_slice x16 -> x0, local copies, waits for them, and re-layouts: 8.63 us -> none  [grouped_terms(): lax.map(one_group, (split_rows(inputs), split_rows(step_sizes), split_row...]
    pallas_call x0 -> x1, Pallas kernels: none -> 8.43 us  [shards(): pl.pallas_call(functools.partial(kernel, nb, nb != 8), out_shape=jax.Shap...]
    select_n x14 -> x1, other arithmetic: 8.48 us -> 0.14 us  [shards(): ordered = jnp.where(row == 1, ordered, turned)]
    ppermute x4 -> x8, waiting for transfers between devices: 2.81 us -> 11 us  [the longest x7 10.3 us: shards(): lax.ppermute(sent, 'cols', [(i, (i + step) % nb) for i in range(nb)])]
  transfers between devices with their start and end apart: 8 -> 8, of which waited for: 1 -> 3; matrix products, arithmetic and copies ran while one was open for 52% -> 7% of each run, Pallas kernels for 0% -> 0%
where the time goes in v1:
time: 37.2 us; the launch traced here: 37 us
  starting transfers between devices  13 us (35%)
  waiting for transfers between devices  11 us (30%)
  Pallas kernels  8.43 us (23%)
  local copies, waits for them, and re-layouts  3.73 us (10%)
  other arithmetic  0.8 us (2%)
    ppermute x7, starting transfers between devices, shards(): lax.ppermute(sent, 'cols', [(i, (i + step) % nb) for i in range(nb)])  12.4 us
    ppermute x7, waiting for transfers between devices, shards(): lax.ppermute(sent, 'cols', [(i, (i + step) % nb) for i in range(nb)])  10.3 us
    pallas_call x1, Pallas kernels, shards(): pl.pallas_call(functools.partial(kernel, nb, nb != 8), out_shape=jax.Shap...  8.43 us
    unnamed x20, local copies, waits for them, and re-layouts  2.59 us
  transfers between devices with their start and end apart: 8, of which 3 were waited for; matrix products, arithmetic and copies ran while one was open for 7% of the time, Pallas kernels for 0%

profile of v1, /device:TPU:0, one launch (start us, length us, event | category | flops | bytes accessed | tf_op | source)
XLA Modules:
  0.0 37.0 jit_solution(1636727164739225605)
XLA Ops:
  0.0 0.9 %copy.16 = bf16[4,32,256]{2,0,1:T(4,128)(2,1)S(1)} copy(bf16[4,32,256]{2,1,0:T(8,128)(2,1)} %param.10) | data formatting | bytes 131072 | tf_op args[0]
  0.9 0.6 %collective-permute-start = (bf16[4,32,256]{2,0,1:T(4,128)(2,1)S(1)}, bf16[4,32,256]{2,0,1:T(4,128)(2,1)S(1)}, u32[]{:S(2)}, u32[]{:S(2)}) collective-permute-start(bf16[4,32,256]{2,0,1:T(4,128)(2,1)S(1)} %copy.16), channel_id=1, source_target_pairs={{0,8},{8,0},{1,9},{9,1},{2,10},{10,2},{3,11},{11,3},{4,12},{12,4},... | collective-permute-start | bytes 196616 | tf_op jit(solution)/shard_map/ppermute | solution.py:325
  1.5 0.2 rev.7
  1.7 0.7 %collective-permute-done = bf16[4,32,256]{2,0,1:T(4,128)(2,1)S(1)} collective-permute-done((bf16[4,32,256]{2,0,1:T(4,128)(2,1)S(1)}, bf16[4,32,256]{2,0,1:T(4,128)(2,1)S(1)}, u32[]{:S(2)}, u32[]{:S(2)}) %collective-permute-start) | collective-permute-done | bytes 65568 | tf_op jit(solution)/shard_map/ppermute | solution.py:325
  2.4 0.2 rev.6
  2.6 0.1 maximum_select_fusion
  2.7 0.0 copy-start
  2.8 0.1 concatenate.11.refs_0_.refs_8_
  2.9 5.9 %collective-permute-start.7 = (bf16[176,256]{1,0:T(8,128)(2,1)S(1)}, bf16[176,256]{1,0:T(8,128)(2,1)S(1)}, u32[]{:S(2)}, u32[]{:S(2)}) collective-permute-start(bf16[176,256]{1,0:T(8,128)(2,1)S(1)} %concatenate.11.refs_0_.refs_8_), channel_id=1, source_target_pairs={{0,7},{1,0},{2,1},{3,2},{4,3},{5,4},{6,5},{7,6},{8,15},{9,8},{10,9... | collective-permute-start | bytes 270344 | tf_op jit(solution)/shard_map/ppermute | solution.py:335
  8.8 0.4 %collective-permute-start.6 = (bf16[176,256]{1,0:T(8,128)(2,1)S(1)}, bf16[176,256]{1,0:T(8,128)(2,1)S(1)}, u32[]{:S(2)}, u32[]{:S(2)}) collective-permute-start(bf16[176,256]{1,0:T(8,128)(2,1)S(1)} %concatenate.11.refs_0_.refs_8_), channel_id=1, source_target_pairs={{0,6},{1,7},{2,0},{3,1},{4,2},{5,3},{6,4},{7,5},{8,14},{9,15},{10,... | collective-permute-start | bytes 270344 | tf_op jit(solution)/shard_map/ppermute | solution.py:335
  9.2 1.0 %copy.21.refs_13_ = bf16[4,256,144]{2,1,0:T(8,128)(2,1)} copy(bf16[4,256,144]{1,2,0:T(8,128)(2,1)S(1)} %copy-done) | data formatting | bytes 589824 | tf_op args[4]
  10.2 0.0 collective-permute-start.5
  10.2 3.0 %collective-permute-start.4 = (bf16[176,256]{1,0:T(8,128)(2,1)S(1)}, bf16[176,256]{1,0:T(8,128)(2,1)S(1)}, u32[]{:S(2)}, u32[]{:S(2)}) collective-permute-start(bf16[176,256]{1,0:T(8,128)(2,1)S(1)} %concatenate.11.refs_0_.refs_8_), channel_id=1, source_target_pairs={{0,4},{1,5},{2,6},{3,7},{4,0},{5,1},{6,2},{7,3},{8,12},{9,13},{10,... | collective-permute-start | bytes 270344 | tf_op jit(solution)/shard_map/ppermute | solution.py:335
  13.2 1.9 %collective-permute-start.2 = (bf16[176,256]{1,0:T(8,128)(2,1)S(1)}, bf16[176,256]{1,0:T(8,128)(2,1)S(1)}, u32[]{:S(2)}, u32[]{:S(2)}) collective-permute-start(bf16[176,256]{1,0:T(8,128)(2,1)S(1)} %concatenate.11.refs_0_.refs_8_), channel_id=1, source_target_pairs={{0,2},{1,3},{2,4},{3,5},{4,6},{5,7},{6,0},{7,1},{8,10},{9,11},{10,... | collective-permute-start | bytes 270344 | tf_op jit(solution)/shard_map/ppermute | solution.py:335
  15.1 0.0 collective-permute-done.6.refs_6_
  15.1 1.2 %collective-permute-start.1 = (bf16[176,256]{1,0:T(8,128)(2,1)S(1)}, bf16[176,256]{1,0:T(8,128)(2,1)S(1)}, u32[]{:S(2)}, u32[]{:S(2)}) collective-permute-start(bf16[176,256]{1,0:T(8,128)(2,1)S(1)} %concatenate.11.refs_0_.refs_8_), channel_id=1, source_target_pairs={{0,1},{1,2},{2,3},{3,4},{4,5},{5,6},{6,7},{7,0},{8,9},{9,10},{10,1... | collective-permute-start | bytes 270344 | tf_op jit(solution)/shard_map/ppermute | solution.py:335
  16.3 0.7 %pad_add_fusion.place = s32[2]{0:T(128)} fusion(s32[1]{0:T(128)} %bitcast.1, s32[1]{0:T(128)} %bitcast), kind=kLoop, calls=%fused_computation.3 | loop fusion | flops 2 | bytes 16 | tf_op jit(solution)/shard_map/stack | solution.py:369
  17.0 0.6 %copy.20 = bf16[3,32,256]{2,1,0:T(8,128)(2,1)} copy(bf16[3,32,256]{2,0,1:T(4,128)(2,1)S(1)} %slice.21) | data formatting | bytes 98304 | tf_op jit(solution)/shard_map/slice | solution.py:329
  17.6 7.2 %collective-permute-done.4.refs_4_ = bf16[176,256]{1,0:T(8,128)(2,1)S(1)} collective-permute-done((bf16[176,256]{1,0:T(8,128)(2,1)S(1)}, bf16[176,256]{1,0:T(8,128)(2,1)S(1)}, u32[]{:S(2)}, u32[]{:S(2)}) %collective-permute-start.4) | collective-permute-done | bytes 90144 | tf_op jit(solution)/shard_map/ppermute | solution.py:335
  24.8 3.1 %collective-permute-done.3.refs_3_ = bf16[176,256]{1,0:T(8,128)(2,1)S(1)} collective-permute-done((bf16[176,256]{1,0:T(8,128)(2,1)S(1)}, bf16[176,256]{1,0:T(8,128)(2,1)S(1)}, u32[]{:S(2)}, u32[]{:S(2)}) %collective-permute-start.3) | collective-permute-done | bytes 90144 | tf_op jit(solution)/shard_map/ppermute | solution.py:335
  27.9 0.6 %copy-done.6 = bf16[176,256]{1,0:T(8,128)(2,1)} copy-done((bf16[176,256]{1,0:T(8,128)(2,1)}, bf16[176,256]{1,0:T(8,128)(2,1)S(1)}, u32[]{:S(2)}) %copy-start.6) | copy-done | bytes 90136
  28.5 0.0 copy-done.7
  28.5 0.0 copy-done.8
  28.6 8.4 %shard_map.100 = bf16[4,32,256]{2,1,0:T(8,128)(2,1)} custom-call(s32[2]{0:T(128)} %pad_add_fusion.place, bf16[176,256]{1,0:T(8,128)(2,1)} %copy-done.1, bf16[176,256]{1,0:T(8,128)(2,1)} %copy-done.8, bf16[176,256]{1,0:T(8,128)(2,1)} %copy-done.7, bf16[176,256]{1,0:T(8,128)(2,1)} %copy-done.6, bf16[176,256]{1,0:T(8,128)(2,1)} %copy-done.5, ...), custom_call_target="tpu_custom_call" | custom-call | flops 2000000000 | bytes 4000000 | tf_op jit(solution)/shard_map/pallas_call | solution.py:353
  (24 shorter events, 0.1 us)
Async XLA Ops:
  0.9 1.5 %collective-permute-start = (bf16[4,32,256]{2,0,1:T(4,128)(2,1)S(1)}, bf16[4,32,256]{2,0,1:T(4,128)(2,1)S(1)}, u32[]{:S(2)}, u32[]{:S(2)}) collective-permute-start(bf16[4,32,256]{2,0,1:T(4,128)(2,1)S(1)} %copy.16), channel_id=1, source_target_pairs={{0,8},{8,0},{1,9},{9,1},{2,10},{10,2},{3,11},{11,3},{4,12},{12,4},... | collective-permute-start | bytes 196616 | tf_op jit(solution)/shard_map/ppermute | solution.py:325
  2.7 6.5 %copy-start = (bf16[4,256,144]{1,2,0:T(8,128)(2,1)S(1)}, bf16[4,256,144]{1,2,0:T(8,128)(2,1)}, u32[]{:S(2)}) copy-start(bf16[4,256,144]{1,2,0:T(8,128)(2,1)} %param.14) | copy-start | bytes 884740
  2.9 12.2 %copy-start.1 = (bf16[176,256]{1,0:T(8,128)(2,1)}, bf16[176,256]{1,0:T(8,128)(2,1)S(1)}, u32[]{:S(2)}) copy-start(bf16[176,256]{1,0:T(8,128)(2,1)S(1)} %concatenate.11.refs_0_.refs_8_) | copy-start | bytes 270340
  2.9 10.4 %collective-permute-start.7 = (bf16[176,256]{1,0:T(8,128)(2,1)S(1)}, bf16[176,256]{1,0:T(8,128)(2,1)S(1)}, u32[]{:S(2)}, u32[]{:S(2)}) collective-permute-start(bf16[176,256]{1,0:T(8,128)(2,1)S(1)} %concatenate.11.refs_0_.refs_8_), channel_id=1, source_target_pairs={{0,7},{1,0},{2,1},{3,2},{4,3},{5,4},{6,5},{7,6},{8,15},{9,8},{10,9... | collective-permute-start | bytes 270344 | tf_op jit(solution)/shard_map/ppermute | solution.py:335
  8.8 6.3 %collective-permute-start.6 = (bf16[176,256]{1,0:T(8,128)(2,1)S(1)}, bf16[176,256]{1,0:T(8,128)(2,1)S(1)}, u32[]{:S(2)}, u32[]{:S(2)}) collective-permute-start(bf16[176,256]{1,0:T(8,128)(2,1)S(1)} %concatenate.11.refs_0_.refs_8_), channel_id=1, source_target_pairs={{0,6},{1,7},{2,0},{3,1},{4,2},{5,3},{6,4},{7,5},{8,14},{9,15},{10,... | collective-permute-start | bytes 270344 | tf_op jit(solution)/shard_map/ppermute | solution.py:335
  10.2 7.4 %collective-permute-start.5 = (bf16[176,256]{1,0:T(8,128)(2,1)S(1)}, bf16[176,256]{1,0:T(8,128)(2,1)S(1)}, u32[]{:S(2)}, u32[]{:S(2)}) collective-permute-start(bf16[176,256]{1,0:T(8,128)(2,1)S(1)} %concatenate.11.refs_0_.refs_8_), channel_id=1, source_target_pairs={{0,5},{1,6},{2,7},{3,0},{4,1},{5,2},{6,3},{7,4},{8,13},{9,14},{10,... | collective-permute-start | bytes 270344 | tf_op jit(solution)/shard_map/ppermute | solution.py:335
  10.2 14.5 %collective-permute-start.4 = (bf16[176,256]{1,0:T(8,128)(2,1)S(1)}, bf16[176,256]{1,0:T(8,128)(2,1)S(1)}, u32[]{:S(2)}, u32[]{:S(2)}) collective-permute-start(bf16[176,256]{1,0:T(8,128)(2,1)S(1)} %concatenate.11.refs_0_.refs_8_), channel_id=1, source_target_pairs={{0,4},{1,5},{2,6},{3,7},{4,0},{5,1},{6,2},{7,3},{8,12},{9,13},{10,... | collective-permute-start | bytes 270344 | tf_op jit(solution)/shard_map/ppermute | solution.py:335
  13.2 14.6 %collective-permute-start.3 = (bf16[176,256]{1,0:T(8,128)(2,1)S(1)}, bf16[176,256]{1,0:T(8,128)(2,1)S(1)}, u32[]{:S(2)}, u32[]{:S(2)}) collective-permute-start(bf16[176,256]{1,0:T(8,128)(2,1)S(1)} %concatenate.11.refs_0_.refs_8_), channel_id=1, source_target_pairs={{0,3},{1,4},{2,5},{3,6},{4,7},{5,0},{6,1},{7,2},{8,11},{9,12},{10,... | collective-permute-start | bytes 270344 | tf_op jit(solution)/shard_map/ppermute | solution.py:335
  13.2 4.4 %copy-start.2 = (bf16[176,256]{1,0:T(8,128)(2,1)}, bf16[176,256]{1,0:T(8,128)(2,1)S(1)}, u32[]{:S(2)}) copy-start(bf16[176,256]{1,0:T(8,128)(2,1)S(1)} %collective-permute-done.7.refs_7_) | copy-start | bytes 270340
  13.2 14.6 %collective-permute-start.2 = (bf16[176,256]{1,0:T(8,128)(2,1)S(1)}, bf16[176,256]{1,0:T(8,128)(2,1)S(1)}, u32[]{:S(2)}, u32[]{:S(2)}) collective-permute-start(bf16[176,256]{1,0:T(8,128)(2,1)S(1)} %concatenate.11.refs_0_.refs_8_), channel_id=1, source_target_pairs={{0,2},{1,3},{2,4},{3,5},{4,6},{5,7},{6,0},{7,1},{8,10},{9,11},{10,... | collective-permute-start | bytes 270344 | tf_op jit(solution)/shard_map/ppermute | solution.py:335
  15.1 2.5 %copy-start.3 = (bf16[176,256]{1,0:T(8,128)(2,1)}, bf16[176,256]{1,0:T(8,128)(2,1)S(1)}, u32[]{:S(2)}) copy-start(bf16[176,256]{1,0:T(8,128)(2,1)S(1)} %collective-permute-done.6.refs_6_) | copy-start | bytes 270340
  15.1 12.8 %collective-permute-start.1 = (bf16[176,256]{1,0:T(8,128)(2,1)S(1)}, bf16[176,256]{1,0:T(8,128)(2,1)S(1)}, u32[]{:S(2)}, u32[]{:S(2)}) collective-permute-start(bf16[176,256]{1,0:T(8,128)(2,1)S(1)} %concatenate.11.refs_0_.refs_8_), channel_id=1, source_target_pairs={{0,1},{1,2},{2,3},{3,4},{4,5},{5,6},{6,7},{7,0},{8,9},{9,10},{10,1... | collective-permute-start | bytes 270344 | tf_op jit(solution)/shard_map/ppermute | solution.py:335
  17.6 10.3 %copy-start.4 = (bf16[176,256]{1,0:T(8,128)(2,1)}, bf16[176,256]{1,0:T(8,128)(2,1)S(1)}, u32[]{:S(2)}) copy-start(bf16[176,256]{1,0:T(8,128)(2,1)S(1)} %collective-permute-done.5.refs_5_) | copy-start | bytes 270340
  24.8 3.1 %copy-start.5 = (bf16[176,256]{1,0:T(8,128)(2,1)}, bf16[176,256]{1,0:T(8,128)(2,1)S(1)}, u32[]{:S(2)}) copy-start(bf16[176,256]{1,0:T(8,128)(2,1)S(1)} %collective-permute-done.4.refs_4_) | copy-start | bytes 270340
  27.9 0.6 %copy-start.6 = (bf16[176,256]{1,0:T(8,128)(2,1)}, bf16[176,256]{1,0:T(8,128)(2,1)S(1)}, u32[]{:S(2)}) copy-start(bf16[176,256]{1,0:T(8,128)(2,1)S(1)} %collective-permute-done.3.refs_3_) | copy-start | bytes 270340
  27.9 0.7 %copy-start.7 = (bf16[176,256]{1,0:T(8,128)(2,1)}, bf16[176,256]{1,0:T(8,128)(2,1)S(1)}, u32[]{:S(2)}) copy-start(bf16[176,256]{1,0:T(8,128)(2,1)S(1)} %collective-permute-done.2.refs_2_) | copy-start | bytes 270340
  27.9 0.7 %copy-start.8 = (bf16[176,256]{1,0:T(8,128)(2,1)}, bf16[176,256]{1,0:T(8,128)(2,1)S(1)}, u32[]{:S(2)}) copy-start(bf16[176,256]{1,0:T(8,128)(2,1)S(1)} %collective-permute-done.1.refs_1_) | copy-start | bytes 270340

commit v2 on v1

v2 whole, which is shorter than its diff:
```python
import functools

import jax
import jax.numpy as jnp
from jax import lax
from jax.experimental import pallas as pl
from jax.experimental.pallas import tpu as pltpu
from jax.sharding import PartitionSpec as P

norm_eps = 1e-05
f32, bf16 = jnp.float32, jnp.bfloat16
TH, TW, D, NH, NS = 4, 32, 256, 16, 64
HALO = 176


def dot(a, b):
    return jnp.dot(a, b, preferred_element_type=f32)


def dot_t(a, b):
    return lax.dot_general(a, b, (((1,), (1,)), ((), ())), preferred_element_type=f32)


def split(a):
    high = a.astype(bf16)
    return high, (a - high.astype(f32)).astype(bf16)


def dot_wide(a, mask):
    high, low = split(a)
    return dot(high, mask) + dot(low, mask)


def wide_dot(mask, b):
    high, low = split(b)
    return dot(mask, high) + dot(mask, low)


def softplus(x):
    return jnp.maximum(x, 0.0) + jnp.log1p(jnp.exp(-jnp.abs(x)))


def silu(x):
    return x * jax.nn.sigmoid(x)


def iotas(rows, lanes):
    return (
        lax.broadcasted_iota(jnp.int32, (rows, lanes), 0),
        lax.broadcasted_iota(jnp.int32, (rows, lanes), 1),
    )


def ones_where(mask):
    return jnp.where(mask, 1.0, 0.0).astype(bf16)


def at(g, j):
    start = g * (8 * TW) + TW * j
    return pl.ds(start if isinstance(start, int) else pl.multiple_of(start, TW), TW)


def each(count, body):
    if count == 1:
        body(0)
    else:
        lax.fori_loop(0, count, lambda i, carry: (body(i), carry)[1], 0)


def load(feats, w_in, conv_w, conv_b, w_proj, dt_bias, a_rate, d_skip, gain, w_out, *refs):
    lower = lax.axis_index("rows") == 1
    sent, outs, sems = refs[0], refs[1:-1], refs[-1]
    copies = [
        pltpu.make_async_copy(
            feats.at[jnp.where(lower, i, 3 - i)], sent.at[pl.ds(TW * (i + 1), TW), :], sems.at[i]
        )
        for i in range(4)
    ]
    weights = (w_in, conv_w, conv_b, w_proj, dt_bias, a_rate, d_skip, gain, w_out)
    copies += [
        pltpu.make_async_copy(source, target, sems.at[4 + i])
        for i, (source, target) in enumerate(zip(weights, outs))
    ]
    for copy in copies:
        copy.start()
    for copy in copies:
        copy.wait()


def pack(loaded, partner, sent, far):
    lower = lax.axis_index("rows") == 1
    own = [loaded[TW * (i + 1) : TW * (i + 2), :] for i in range(4)]
    rows = [partner[jnp.where(lower, i, 3 - i)] for i in range(4)] + own
    for i in range(3, 8):
        sent[TW * (i - 3) : TW * (i - 2), :] = rows[i]
    for i in range(3):
        far[i * TW : (i + 1) * TW, :] = rows[i]
    wide = [part.astype(f32) for part in rows]
    edges = [part[:1] for part in wide] + [part[TW - 1 :] for part in wide]
    sent[160:HALO, :] = jnp.concatenate(edges, axis=0).astype(bf16)


def direction_taps(conv_w, lower):
    return [
        [
            jnp.where(lower, conv_w[3 * a + b : 3 * a + b + 1, :], conv_w[3 * (2 - a) + b : 3 * (2 - a) + b + 1, :])
            for b in range(3)
        ]
        for a in range(3)
    ]


def filtered(ref, count, q, base, taps, bias):
    total = jnp.broadcast_to(bias, (TW, D))
    for a in range(3):
        if 0 <= q + a - 1 < count:
            if not isinstance(base, int):
                cells = ref[q + a - 1, pl.ds(pl.multiple_of(base - 8, 8), TW + 16), :]
            for b in range(3):
                if isinstance(base, int):
                    value = ref[q + a - 1, base + b - 1 : base + b - 1 + TW, :]
                else:
                    value = cells[7 + b : 7 + b + TW]
                total = total + taps[a][b] * value
    return silu(total).astype(bf16)


def local(nb, count, sent, far, *refs):
    sides, refs = refs[:count], refs[count:]
    w_in, conv_w, conv_b, w_proj, dt_bias, a_rate, d_skip = refs[:7]
    base_out, gate_out, reads_out, edge_out, strip = refs[7:]
    row, col = lax.axis_index("rows"), lax.axis_index("cols")
    lower = row == 1
    w_x = w_in[:, :D]

    def pre_conv(tokens):
        return dot(tokens, w_x).astype(bf16).astype(f32)

    if count == 1:
        left = sides[0][jnp.maximum(col - 1, 0), 160:HALO, :]
        right = sides[0][jnp.minimum(col + 1, nb - 1), 160:HALO, :]
    else:
        near, further, furthest = (side[160:HALO, :] for side in sides)
        odd = lax.rem(col, 2) == 1
        left = jnp.where(odd, near, jnp.where(col == 4, furthest, further))
        right = jnp.where(odd, jnp.where(col == 3, furthest, further), near)
    left = pre_conv(left) * jnp.where(col > 0, 1.0, 0.0)
    right = pre_conv(right) * jnp.where(col < nb - 1, 1.0, 0.0)
    far_pre, own_pre = pre_conv(far[...]), pre_conv(sent[0:160, :])
    for i in range(8):
        strip[i, 8:40, :] = far_pre[i * TW : (i + 1) * TW] if i < 3 else own_pre[(i - 3) * TW : (i - 2) * TW]
        strip[i, 7:8, :] = left[8 + i : 9 + i]
        strip[i, 40:41, :] = right[i : i + 1]
    taps, bias = direction_taps(conv_w, lower), conv_b[...]
    strip_mixed = [filtered(strip, 8, q, 8, taps, bias) for q in range(8)]
    own = jnp.concatenate(strip_mixed[4:], axis=0)
    column_tokens = jnp.concatenate(strip_mixed, axis=0)
    gate_out[...] = silu(dot(sent[TW:160, :], w_in[:, D:]))

    head_lane = ones_where(iotas(NH, 128)[1] % NH == iotas(NH, 128)[0])
    expand = ones_where(iotas(NH, D)[1] // NH == iotas(NH, D)[0])
    tok_r, tok_c = iotas(128, 128)
    same_row = tok_r // TW == tok_c // TW
    upto = ones_where(same_row & (tok_c <= tok_r))
    onward = ones_where(same_row & (tok_c >= tok_r))

    projected = [dot_t(own, w_proj[k]) for k in range(2)]
    steps = [softplus(projected[k][:, :NH] + dt_bias[k : k + 1, :]) for k in range(2)]
    logs = [-steps[k] * a_rate[k : k + 1, :] for k in range(2)]
    write = [projected[k][:, NH : NH + NS].astype(bf16) for k in range(2)]
    read = [projected[k][:, NH + NS :].astype(bf16) for k in range(2)]
    from_edge = [
        dot_wide(jnp.exp(wide_dot(mask, logs[k])), expand) for k, mask in enumerate((upto, onward))
    ]
    edge_out[0], edge_out[1] = from_edge
    pair_r, pair_c = iotas(NH, NH * TW)
    spread = ones_where(pair_c // TW == pair_r)
    inner_r, inner_c = iotas(128, NH * TW)
    inner_u, inner_s = inner_r % TW, inner_c % TW
    parts = []
    for k, keep in enumerate((inner_u > inner_s, inner_u < inner_s)):
        for part in split(logs[k]):
            parts.append(jnp.where(keep, dot(part, spread), 0.0).astype(bf16))
    step_parts = [jnp.where(inner_u == inner_s, dot_wide(steps[k], spread), 0.0) for k in range(2)]
    time_r, time_c = iotas(TW, TW)
    first, second = ones_where(time_c <= time_r), ones_where(time_c >= time_r)
    walk = jnp.concatenate([first, first, second, second], axis=1)
    local_t, local_s = iotas(TW, NH * TW)
    local_s = local_s % TW
    feature = lax.broadcasted_iota(jnp.int32, (TW, D), 1) // NH
    zeros = jnp.zeros((TW, NS), bf16)
    across = []
    for q in range(4):
        rows = slice(q * TW, (q + 1) * TW)
        gaps = dot(walk, jnp.concatenate([part[rows] for part in parts], axis=0))
        weights = jnp.zeros((TW, NH * TW), f32)
        for k, keep in enumerate((local_s <= local_t, local_s >= local_t)):
            scores = dot_t(read[k][rows], jnp.concatenate([write[k][rows]] * NH, axis=0))
            step_row = jnp.sum(step_parts[k][rows], axis=0, keepdims=True)
            weights = weights + jnp.where(keep, scores * step_row, 0.0)
        weights = (weights * jnp.exp(gaps)).astype(bf16)
        values = own[rows]
        spread_values = jnp.concatenate(
            [jnp.where(feature == h, values, jnp.zeros_like(values)) for h in range(NH)], axis=0
        )
        result = dot(weights, spread_values)
        reads = jnp.concatenate(
            [
                jnp.concatenate([read[0][rows], zeros], axis=1),
                jnp.concatenate([zeros, read[1][rows]], axis=1),
            ],
            axis=0,
        )
        reads_out[q] = reads
        across.append(result)
    across = jnp.concatenate(across, axis=0)

    k_in = jnp.where(lower, 2, 3)
    k_out = jnp.where(lower, 3, 2)

    def pick_row(ref, k):
        return jnp.where(k == 2, ref[2:3, :], ref[3:4, :])

    project_in = dot_t(column_tokens, w_proj[k_in])
    project_out = dot_t(own, w_proj[k_out])
    steps_in = softplus(project_in[:, :NH] + pick_row(dt_bias, k_in))
    steps_out = softplus(project_out[:, :NH] + pick_row(dt_bias, k_out))
    logs_in = -steps_in * pick_row(a_rate, k_in)
    logs_out = -steps_out * pick_row(a_rate, k_out)
    write_in = project_in[:, NH : NH + NS].astype(bf16)
    write_out = project_out[:, NH : NH + NS].astype(bf16)
    read_in = project_in[128:, NH + NS :].astype(bf16)
    read_out = project_out[:, NH + NS :].astype(bf16)
    t_r, s_c = iotas(128, 256)
    same_col = (t_r % TW) == (s_c % TW)
    meet_in = ones_where(same_col)
    walk_in = ones_where(same_col & (s_c // TW <= t_r // TW + 4))
    meet_out = ones_where(tok_r % TW == tok_c % TW)
    walk_out = ones_where((tok_r % TW == tok_c % TW) & (tok_c >= tok_r))
    source_r, source_c = iotas(256, 128)
    source_u, source_s = source_r // TW, source_c // NH
    select = ones_where(source_u == source_s)
    scores_in = dot_wide(jnp.where(same_col, dot_t(read_in, write_in), 0.0), select)
    same_out = tok_r % TW == tok_c % TW
    scores_out = dot_wide(jnp.where(same_out, dot_t(read_out, write_out), 0.0), select[128:])
    out_u = tok_r // TW + 4
    out_s = tok_c // NH
    gap = jnp.zeros((128, 128), f32)
    for part in split(logs_in):
        gap = gap + dot(walk_in, jnp.where(source_u > source_s, dot(part, head_lane), 0.0).astype(bf16))
    for part in split(logs_out):
        gap = gap + dot(walk_out, jnp.where(out_u < out_s, dot(part, head_lane), 0.0).astype(bf16))
    lane_in = jnp.zeros((128, 128), f32)
    for part in split(steps_in):
        lane_in = lane_in + dot(meet_in, jnp.where(source_u == source_s, dot(part, head_lane), 0.0).astype(bf16))
    lane_out = jnp.zeros((128, 128), f32)
    for part in split(steps_out):
        lane_out = lane_out + dot(meet_out, jnp.where(out_u == out_s, dot(part, head_lane), 0.0).astype(bf16))
    weights = jnp.where(out_s <= out_u, scores_in * lane_in, 0.0) + jnp.where(out_s >= out_u, scores_out * lane_out, 0.0)
    weights = (weights * jnp.exp(gap)).astype(bf16)
    skips = dot_wide(d_skip[...], expand)
    own_wide = own.astype(f32)
    pick_r, pick_c = iotas(128, D)
    vertical = (skips[2:3] + skips[3:4]) * own_wide
    for s in range(8):
        factor = dot(weights, ones_where(pick_r == s * NH + pick_c // NH))
        values = strip_mixed[s].astype(f32)
        vertical = vertical + factor * jnp.concatenate([values] * 4, axis=0)
    base_out[...] = across + (skips[0:1] + skips[1:2]) * own_wide + vertical.astype(bf16).astype(f32)


def final(nb, gathered, *refs):
    count = 1 if gathered else nb
    blocks, refs = refs[:count], refs[count:]
    base_in, gate_in, reads_in, edge_in = refs[:4]
    w_in, conv_w, conv_b, w_proj, dt_bias, a_rate, gain, w_out, out = refs[4:13]
    pre, mixed, la_all, dt_all, totals, writes, scaled = refs[13:]
    row, col = lax.axis_index("rows"), lax.axis_index("cols")
    lower = row == 1
    ng = nb // 8
    w_x = w_in[:, :D]

    def pre_conv(tokens):
        return dot(tokens, w_x).astype(bf16).astype(f32)

    pre[:, 0:8, :] = jnp.zeros((5, 8, D), f32)
    pre[:, 8 + nb * TW :, :] = jnp.zeros((5, 8, D), f32)

    def place_block(tokens, position):
        rows = pre_conv(tokens)
        base = pl.multiple_of(position * TW + 8, 8)
        for q in range(5):
            pre[q, pl.ds(base, TW), :] = rows[q * TW : (q + 1) * TW]

    if gathered:
        each(nb, lambda j: place_block(blocks[0][j, 0:160, :], j))
    else:
        for step in range(nb):
            place_block(blocks[step][0:160, :], col ^ step)
    taps, bias = direction_taps(conv_w, lower), conv_b[...]

    head_lane = ones_where(iotas(NH, 128)[1] % NH == iotas(NH, 128)[0])
    tok_r, tok_c = iotas(128, 128)
    same_row = tok_r // TW == tok_c // TW
    after = ones_where(same_row & (tok_c > tok_r))
    before = ones_where(same_row & (tok_c < tok_r))
    row_ones = ones_where(same_row)
    lane = lax.broadcasted_iota(jnp.int32, (1, 128), 1)
    bias_2 = dot_wide(dt_bias[0:2, :], head_lane)
    rate_2 = dot_wide(a_rate[0:2, :], head_lane)

    def first_pass(g):
        group = lane // NH + g * 8
        is_left = group < col
        w_both = jnp.concatenate(
            [jnp.where(g * 8 + j < col, w_proj[0, 0:NH, :], w_proj[1, 0:NH, :]) for j in range(8)]
            + [w_proj[k, NH : NH + NS, :] for k in range(2)],
            axis=0,
        )
        raw = jnp.zeros((128, 128), f32)
        for j in range(8):
            base = g * (8 * TW) + (8 + TW * j)
            for q in range(1, 5):
                mixed[g * 8 + j, (q - 1) * TW : q * TW, :] = filtered(pre, 5, q, base, taps, bias)
            result = dot_t(mixed[g * 8 + j], w_both)
            raw = jnp.where(lane // NH == j, result[:, :128], raw)
            block = g * 8 + j
            keep = jnp.where(lane < NS, jnp.where(block < col, 1.0, 0.0), jnp.where(block > col, 1.0, 0.0))
            vectors = (result[:, 128:] * keep).astype(bf16)
            for q in range(4):
                writes[q, at(g, j), :] = vectors[q * TW : (q + 1) * TW]
        steps = softplus(raw + jnp.where(is_left, bias_2[0:1], bias_2[1:2]))
        steps = jnp.where(group == col, 0.0, steps)
        logs = -steps * jnp.where(is_left, rate_2[0:1], rate_2[1:2])
        dt_all[g] = steps
        la_all[g] = logs
        totals[g] = wide_dot(row_ones, logs)

    each(ng, first_pass)

    both_ways = jnp.concatenate([after, before], axis=1)

    def second_pass(g):
        group = lane // NH + g * 8
        logs = la_all[g]
        stacked = jnp.concatenate([jnp.where(group < col, logs, 0.0), jnp.where(group > col, logs, 0.0)], axis=0)
        reach = wide_dot(both_ways, stacked)

        def add_group(other, total):
            source, target = other * 8 + tok_r // NH, g * 8 + tok_c // NH
            nearer = ((source > target) & (source < col)) | ((source < target) & (source > col))
            nearer = nearer & (tok_r % NH == tok_c % NH)
            return total + dot_wide(totals[other], ones_where(nearer))

        if ng == 1:
            reach = add_group(0, reach)
        else:
            reach = lax.fori_loop(0, ng, add_group, reach)
        weight = jnp.concatenate(split(jnp.exp(reach) * dt_all[g]), axis=1)
        expand_r, expand_c = iotas(256, D)
        for j in range(8):
            pick = ones_where((expand_r % 128) == j * NH + expand_c // NH)
            factor = dot(weight, pick)
            values = (mixed[g * 8 + j].astype(f32) * factor).astype(bf16)
            for q in range(4):
                scaled[q, at(g, j), :] = values[q * TW : (q + 1) * TW]

    each(ng, second_pass)

    entered = []
    for q in range(4):
        rows = slice(q * TW, (q + 1) * TW)
        state = lax.dot_general(writes[q], scaled[q], (((0,), (0,)), ((), ())), preferred_element_type=f32)
        both = wide_dot(reads_in[q], state)
        entered.append(both[:TW] * edge_in[0, rows, :] + both[TW:] * edge_in[1, rows, :])
    combined = base_in[...] + jnp.concatenate(entered, axis=0)

    centre = combined - jnp.mean(combined, axis=-1, keepdims=True)
    normed = centre * lax.rsqrt(jnp.mean(centre * centre, axis=-1, keepdims=True) + norm_eps) * gain[...]
    gated = (normed * gate_in[...]).astype(bf16)
    result = dot(gated, w_out[...]).astype(bf16)
    for i in range(4):
        out[jnp.where(lower, i, 3 - i)] = result[i * TW : (i + 1) * TW]


def shards(feats, w_in, conv_w, conv_b, w_proj, dt_bias, a_rate, d_skip, norm_gain, w_out):
    nb = lax.axis_size("cols")
    direct = nb == 8
    vmem, hbm = pl.BlockSpec(memory_space=pltpu.VMEM), pl.BlockSpec(memory_space=pltpu.HBM)

    def shape(*dims, dtype=f32):
        return jax.ShapeDtypeStruct(dims, dtype)

    def limit(mib):
        return pltpu.CompilerParams(vmem_limit_bytes=mib << 20)

    partner = lax.ppermute(feats, "rows", [(0, 1), (1, 0)])
    params = [w_in, conv_w, conv_b[None], jnp.swapaxes(w_proj, 1, 2), dt_bias, a_rate, d_skip, norm_gain[None], w_out]
    loaded, *params = pl.pallas_call(
        load,
        out_shape=(shape(HALO, D, dtype=bf16), *[shape(*part.shape, dtype=part.dtype) for part in params]),
        in_specs=[hbm] * 10,
        out_specs=(vmem,) * 10,
        scratch_shapes=[pltpu.SemaphoreType.DMA((13,))],
        compiler_params=limit(8),
    )(*[pltpu.with_memory_space_constraint(part, pltpu.HBM) for part in (feats, *params)])
    w_in, conv_w, conv_b, w_proj, dt_bias, a_rate, d_skip, norm_gain, w_out = params
    sent, far = pl.pallas_call(
        pack,
        out_shape=(shape(HALO, D, dtype=bf16), shape(96, D, dtype=bf16)),
        in_specs=[vmem] * 2,
        out_specs=(vmem, vmem),
        input_output_aliases={0: 0},
        compiler_params=limit(4),
    )(loaded, partner)
    if direct:

        def across(part, step):
            return lax.ppermute(part, "cols", [(i, i ^ step) for i in range(nb)])

        blocks = [sent] + [None] * 7
        for step in (6, 4, 1, 3, 2):
            blocks[step] = across(sent, step)
        blocks[7] = across(blocks[6], 1)
        blocks[5] = across(blocks[4], 1)
        sides = [blocks[1], blocks[3], blocks[7]]
    else:
        blocks = sides = [lax.all_gather(sent, "cols")]
    kept = pl.pallas_call(
        functools.partial(local, nb, len(sides)),
        out_shape=(shape(128, D), shape(128, D), shape(4, 2 * TW, 2 * NS, dtype=bf16), shape(2, 128, D)),
        in_specs=[vmem] * (9 + len(sides)),
        out_specs=(vmem,) * 4,
        scratch_shapes=[pltpu.VMEM((8, 48, D), f32)],
        compiler_params=limit(16 if direct else 40),
        cost_estimate=pl.CostEstimate(flops=1_000_000_000, bytes_accessed=4_000_000, transcendentals=1_000_000),
    )(sent, far, *sides, w_in, conv_w, conv_b, w_proj, dt_bias, a_rate, d_skip)
    operands = [*blocks, *kept, w_in, conv_w, conv_b, w_proj, dt_bias, a_rate, norm_gain, w_out]
    return pl.pallas_call(
        functools.partial(final, nb, not direct),
        out_shape=shape(TH, TW, D, dtype=bf16),
        in_specs=[vmem] * len(operands),
        out_specs=vmem,
        scratch_shapes=[
            pltpu.VMEM((5, nb * TW + 16, D), f32),
            pltpu.VMEM((nb, 128, D), bf16),
            pltpu.VMEM((nb // 8, 128, 128), f32),
            pltpu.VMEM((nb // 8, 128, 128), f32),
            pltpu.VMEM((nb // 8, 128, 128), f32),
            pltpu.VMEM((4, nb * TW, 128), bf16),
            pltpu.VMEM((4, nb * TW, D), bf16),
        ],
        compiler_params=limit(16 if direct else 48),
        cost_estimate=pl.CostEstimate(flops=1_000_000_000, bytes_accessed=4_000_000, transcendentals=1_000_000),
    )(*operands)


def solution(mesh):
    in_specs = (P(("groups", "rows"), "cols", None), P(), P(), P(), P(), P(), P(), P(), P(), P())
    out_specs = P(("groups", "rows"), "cols", None)
    return jax.shard_map(shards, mesh=mesh, in_specs=in_specs, out_specs=out_specs, check_vma=False)
```

time: 37.2 us -> 24.1 us (0.65)
  waiting for transfers between devices: 11 us -> 1.64 us
  local copies, waits for them, and re-layouts: 3.73 us -> 0 us
  other arithmetic: 0.8 us -> 0 us
  starting transfers between devices: 13 us -> 13.5 us
    ppermute x7, waiting for transfers between devices: 10.3 us -> 1.64 us  [across(): return lax.ppermute(part, 'cols', [(i, i ^ step) for i in range(nb)])]
    unnamed x20 -> x0, local copies, waits for them, and re-layouts: 2.59 us -> none
    slice x4 -> x0, local copies, waits for them, and re-layouts: 0.7 us -> none  [the longest x2 0.64 us: shards(): far = ordered[:3]]
    ppermute x1, waiting for transfers between devices: 0.7 us -> 0.01 us  [shards(): partner = lax.ppermute(feats, 'rows', [(0, 1), (1, 0)])]
    another operation x1 -> x0, other arithmetic: 0.67 us -> none  [shards(): jnp.stack([row, col]).astype(jnp.int32)]
    ppermute x7, starting transfers between devices: 12.4 us -> 13 us  [across(): return lax.ppermute(part, 'cols', [(i, i ^ step) for i in range(nb)])]
    rev x2 -> x0, local copies, waits for them, and re-layouts: 0.38 us -> none  [shards(): turned = jnp.concatenate([partner[::-1], feats[::-1]], axis=0)]
    pallas_call x1 -> x4, Pallas kernels: 8.43 us -> 8.64 us  [the longest x1 3.83 us: shards(): pl.pallas_call(functools.partial(final, nb, not direct), out_shape=shape(...]
  transfers between devices with their start and end apart: 8 -> 8, of which waited for: 3 -> 2; matrix products, arithmetic and copies ran while one was open for 7% -> 0% of each run, Pallas kernels for 0% -> 20%
where the time goes in v2:
time: 24.1 us; the launch traced here: 23.9 us
  starting transfers between devices  13.5 us (56%)
  Pallas kernels  8.64 us (36%)
  waiting for transfers between devices  1.64 us (7%)
    ppermute x7, starting transfers between devices, across(): return lax.ppermute(part, 'cols', [(i, i ^ step) for i in range(nb)])  13 us
    pallas_call x1, Pallas kernels, shards(): pl.pallas_call(functools.partial(final, nb, not direct), out_shape=shape(...  3.83 us
    pallas_call x1, Pallas kernels, shards(): pl.pallas_call(functools.partial(local, nb, len(sides)), out_shape=(shape...  3.48 us
    ppermute x7, waiting for transfers between devices, across(): return lax.ppermute(part, 'cols', [(i, i ^ step) for i in range(nb)])  1.64 us
    pallas_call x1, Pallas kernels, shards(): pl.pallas_call(load, out_shape=(shape(HALO, D, dtype=bf16), *[shape(*part...  1.3 us
    ppermute x1, starting transfers between devices, shards(): partner = lax.ppermute(feats, 'rows', [(0, 1), (1, 0)])  0.49 us
  transfers between devices with their start and end apart: 8, of which 2 were waited for; matrix products, arithmetic and copies ran while one was open for 0% of the time, Pallas kernels for 20%

profile of v2, /device:TPU:0, one launch (start us, length us, event | category | flops | bytes accessed | tf_op | source)
XLA Modules:
  0.0 23.9 jit_solution(16678217382238529747)
XLA Ops:
  0.0 0.5 %collective-permute-start = (bf16[4,32,256]{2,1,0:T(8,128)(2,1)}, bf16[4,32,256]{2,1,0:T(8,128)(2,1)S(1)}, u32[]{:S(2)}, u32[]{:S(2)}) collective-permute-start(bf16[4,32,256]{2,1,0:T(8,128)(2,1)} %feats.1), channel_id=1, source_target_pairs={{0,8},{8,0},{1,9},{9,1},{2,10},{10,2},{3,11},{11,3},{4,12},{12,4},... | collective-permute-start | bytes 196616 | tf_op jit(solution)/shard_map/ppermute | solution.py:397
  0.5 1.3 %shard_map.100 = (bf16[176,256]{1,0:T(8,128)(2,1)S(1)}, bf16[256,512]{1,0:T(8,128)(2,1)S(1)}, f32[9,256]{1,0:T(8,128)S(1)}, f32[1,256]{1,0:T(1,128)S(1)}, bf16[4...) custom-call(bf16[4,32,256]{2,1,0:T(8,128)(2,1)} %feats.1, ...), custom_call_target="tpu_custom_call" | custom-call | tf_op jit(solution)/shard_map/pallas_call | solution.py:399
  1.8 0.0 collective-permute-done.partner
  1.9 4.8 %collective-permute-start.6 = (bf16[176,256]{1,0:T(8,128)(2,1)S(1)}, bf16[176,256]{1,0:T(8,128)(2,1)S(1)}, u32[]{:S(2)}, u32[]{:S(2)}) collective-permute-start(bf16[176,256]{1,0:T(8,128)(2,1)S(1)} %get-tuple-element.22.sent.refs_0_), channel_id=1, source_target_pairs={{0,6},{1,7},{2,4},{3,5},{4,2},{5,3},{6,0},{7,1},{8,14},{9,15},{10,... | collective-permute-start | bytes 270344 | tf_op jit(solution)/shard_map/ppermute | solution.py:419
  6.6 0.0 collective-permute-start.4
  6.6 1.7 %collective-permute-start.3 = (bf16[176,256]{1,0:T(8,128)(2,1)S(1)}, bf16[176,256]{1,0:T(8,128)(2,1)S(1)}, u32[]{:S(2)}, u32[]{:S(2)}) collective-permute-start(bf16[176,256]{1,0:T(8,128)(2,1)S(1)} %get-tuple-element.22.sent.refs_0_), channel_id=1, source_target_pairs={{0,3},{1,2},{2,1},{3,0},{4,7},{5,6},{6,5},{7,4},{8,11},{9,10},{10,... | collective-permute-start | bytes 270344 | tf_op jit(solution)/shard_map/ppermute | solution.py:419
  8.4 0.4 %collective-permute-start.1 = (bf16[176,256]{1,0:T(8,128)(2,1)S(1)}, bf16[176,256]{1,0:T(8,128)(2,1)S(1)}, u32[]{:S(2)}, u32[]{:S(2)}) collective-permute-start(bf16[176,256]{1,0:T(8,128)(2,1)S(1)} %get-tuple-element.22.sent.refs_0_), channel_id=1, source_target_pairs={{0,1},{1,0},{2,3},{3,2},{4,5},{5,4},{6,7},{7,6},{8,9},{9,8},{10,11... | collective-permute-start | bytes 270344 | tf_op jit(solution)/shard_map/ppermute | solution.py:419
  8.7 1.5 %collective-permute-done.6.refs_6_ = bf16[176,256]{1,0:T(8,128)(2,1)S(1)} collective-permute-done((bf16[176,256]{1,0:T(8,128)(2,1)S(1)}, bf16[176,256]{1,0:T(8,128)(2,1)S(1)}, u32[]{:S(2)}, u32[]{:S(2)}) %collective-permute-start.6) | collective-permute-done | bytes 90144 | tf_op jit(solution)/shard_map/ppermute | solution.py:419
  10.2 1.7 %collective-permute-start.7 = (bf16[176,256]{1,0:T(8,128)(2,1)S(1)}, bf16[176,256]{1,0:T(8,128)(2,1)S(1)}, u32[]{:S(2)}, u32[]{:S(2)}) collective-permute-start(bf16[176,256]{1,0:T(8,128)(2,1)S(1)} %collective-permute-done.6.refs_6_), channel_id=1, source_target_pairs={{0,1},{1,0},{2,3},{3,2},{4,5},{5,4},{6,7},{7,6},{8,9},{9,8},{10,11... | collective-permute-start | bytes 270344 | tf_op jit(solution)/shard_map/ppermute | solution.py:419
  12.0 3.5 %collective-permute-start.2 = (bf16[176,256]{1,0:T(8,128)(2,1)S(1)}, bf16[176,256]{1,0:T(8,128)(2,1)S(1)}, u32[]{:S(2)}, u32[]{:S(2)}) collective-permute-start(bf16[176,256]{1,0:T(8,128)(2,1)S(1)} %get-tuple-element.22.sent.refs_0_), channel_id=1, source_target_pairs={{0,2},{1,3},{2,0},{3,1},{4,6},{5,7},{6,4},{7,5},{8,10},{9,11},{10,... | collective-permute-start | bytes 270344 | tf_op jit(solution)/shard_map/ppermute | solution.py:419
  15.5 0.0 collective-permute-done.4.refs_4_
  15.5 0.9 %collective-permute-start.5 = (bf16[176,256]{1,0:T(8,128)(2,1)S(1)}, bf16[176,256]{1,0:T(8,128)(2,1)S(1)}, u32[]{:S(2)}, u32[]{:S(2)}) collective-permute-start(bf16[176,256]{1,0:T(8,128)(2,1)S(1)} %collective-permute-done.4.refs_4_), channel_id=1, source_target_pairs={{0,1},{1,0},{2,3},{3,2},{4,5},{5,4},{6,7},{7,6},{8,9},{9,8},{10,11... | collective-permute-start | bytes 270344 | tf_op jit(solution)/shard_map/ppermute | solution.py:419
  16.3 0.0 collective-permute-done.3.refs_1_.refs_3_
  16.3 0.0 collective-permute-done.1.refs_0_.refs_1_
  16.4 0.0 collective-permute-done.7.refs_2_.refs_7_
  16.4 3.5 %shard_map.102 = (f32[128,256]{1,0:T(8,128)S(1)}, f32[128,256]{1,0:T(8,128)S(1)}, bf16[4,64,128]{2,1,0:T(8,128)(2,1)S(1)}, f32[2,128,256]{2,1,0:T(8,128)S(1)}) custom-call(bf16[176,256]{1,0:T(8,128)(2,1)S(1)} %get-tuple-element.22.sent.refs_0_, bf16[96,256]{1,0:T(8,128)(2,1)S(1)} %get-tuple-element.23.far, ...), custom_call_target="tpu_custom_call" | custom-call | flops 1000000000 | bytes 4000000 | tf_op jit(solution)/shard_map/pallas_call | solution.py:429
  19.8 0.0 collective-permute-done.2.refs_2_
  19.9 0.2 collective-permute-done.5.refs_5_
  20.0 3.8 %shard_map.103 = bf16[4,32,256]{2,1,0:T(8,128)(2,1)} custom-call(bf16[176,256]{1,0:T(8,128)(2,1)S(1)} %get-tuple-element.22.sent.refs_0_, bf16[176,256]{1,0:T(8,128)(2,1)S(1)} %collective-permute-done.1.refs_0_.refs_1_, bf16[176,256]{1,0:T(8,128)(2,1)S(1)} %collective-permute-done.2.refs_2_, bf16[176,256]{1,0:T(8,128)(2,1)S(1)} %collective-permute-done.3.refs_1_.refs_3_, ...), custom_call_target="tpu_custom_call" | custom-call | flops 1000000000 | bytes 4000000 | tf_op jit(solution)/shard_map/pallas_call | solution.py:439
  (1 shorter events, 0.0 us)
Async XLA Ops:
  0.0 1.8 %collective-permute-start = (bf16[4,32,256]{2,1,0:T(8,128)(2,1)}, bf16[4,32,256]{2,1,0:T(8,128)(2,1)S(1)}, u32[]{:S(2)}, u32[]{:S(2)}) collective-permute-start(bf16[4,32,256]{2,1,0:T(8,128)(2,1)} %feats.1), channel_id=1, source_target_pairs={{0,8},{8,0},{1,9},{9,1},{2,10},{10,2},{3,11},{11,3},{4,12},{12,4},... | collective-permute-start | bytes 196616 | tf_op jit(solution)/shard_map/ppermute | solution.py:397
  1.9 8.4 %collective-permute-start.6 = (bf16[176,256]{1,0:T(8,128)(2,1)S(1)}, bf16[176,256]{1,0:T(8,128)(2,1)S(1)}, u32[]{:S(2)}, u32[]{:S(2)}) collective-permute-start(bf16[176,256]{1,0:T(8,128)(2,1)S(1)} %get-tuple-element.22.sent.refs_0_), channel_id=1, source_target_pairs={{0,6},{1,7},{2,4},{3,5},{4,2},{5,3},{6,0},{7,1},{8,14},{9,15},{10,... | collective-permute-start | bytes 270344 | tf_op jit(solution)/shard_map/ppermute | solution.py:419
  6.6 8.8 %collective-permute-start.4 = (bf16[176,256]{1,0:T(8,128)(2,1)S(1)}, bf16[176,256]{1,0:T(8,128)(2,1)S(1)}, u32[]{:S(2)}, u32[]{:S(2)}) collective-permute-start(bf16[176,256]{1,0:T(8,128)(2,1)S(1)} %get-tuple-element.22.sent.refs_0_), channel_id=1, source_target_pairs={{0,4},{1,5},{2,6},{3,7},{4,0},{5,1},{6,2},{7,3},{8,12},{9,13},{10,... | collective-permute-start | bytes 270344 | tf_op jit(solution)/shard_map/ppermute | solution.py:419
  6.6 9.7 %collective-permute-start.3 = (bf16[176,256]{1,0:T(8,128)(2,1)S(1)}, bf16[176,256]{1,0:T(8,128)(2,1)S(1)}, u32[]{:S(2)}, u32[]{:S(2)}) collective-permute-start(bf16[176,256]{1,0:T(8,128)(2,1)S(1)} %get-tuple-element.22.sent.refs_0_), channel_id=1, source_target_pairs={{0,3},{1,2},{2,1},{3,0},{4,7},{5,6},{6,5},{7,4},{8,11},{9,10},{10,... | collective-permute-start | bytes 270344 | tf_op jit(solution)/shard_map/ppermute | solution.py:419
  8.4 8.0 %collective-permute-start.1 = (bf16[176,256]{1,0:T(8,128)(2,1)S(1)}, bf16[176,256]{1,0:T(8,128)(2,1)S(1)}, u32[]{:S(2)}, u32[]{:S(2)}) collective-permute-start(bf16[176,256]{1,0:T(8,128)(2,1)S(1)} %get-tuple-element.22.sent.refs_0_), channel_id=1, source_target_pairs={{0,1},{1,0},{2,3},{3,2},{4,5},{5,4},{6,7},{7,6},{8,9},{9,8},{10,11... | collective-permute-start | bytes 270344 | tf_op jit(solution)/shard_map/ppermute | solution.py:419
  10.2 6.1 %collective-permute-start.7 = (bf16[176,256]{1,0:T(8,128)(2,1)S(1)}, bf16[176,256]{1,0:T(8,128)(2,1)S(1)}, u32[]{:S(2)}, u32[]{:S(2)}) collective-permute-start(bf16[176,256]{1,0:T(8,128)(2,1)S(1)} %collective-permute-done.6.refs_6_), channel_id=1, source_target_pairs={{0,1},{1,0},{2,3},{3,2},{4,5},{5,4},{6,7},{7,6},{8,9},{9,8},{10,11... | collective-permute-start | bytes 270344 | tf_op jit(solution)/shard_map/ppermute | solution.py:419
  12.0 7.9 %collective-permute-start.2 = (bf16[176,256]{1,0:T(8,128)(2,1)S(1)}, bf16[176,256]{1,0:T(8,128)(2,1)S(1)}, u32[]{:S(2)}, u32[]{:S(2)}) collective-permute-start(bf16[176,256]{1,0:T(8,128)(2,1)S(1)} %get-tuple-element.22.sent.refs_0_), channel_id=1, source_target_pairs={{0,2},{1,3},{2,0},{3,1},{4,6},{5,7},{6,4},{7,5},{8,10},{9,11},{10,... | collective-permute-start | bytes 270344 | tf_op jit(solution)/shard_map/ppermute | solution.py:419
  15.5 4.5 %collective-permute-start.5 = (bf16[176,256]{1,0:T(8,128)(2,1)S(1)}, bf16[176,256]{1,0:T(8,128)(2,1)S(1)}, u32[]{:S(2)}, u32[]{:S(2)}) collective-permute-start(bf16[176,256]{1,0:T(8,128)(2,1)S(1)} %collective-permute-done.4.refs_4_), channel_id=1, source_target_pairs={{0,1},{1,0},{2,3},{3,2},{4,5},{5,4},{6,7},{7,6},{8,9},{9,8},{10,11... | collective-permute-start | bytes 270344 | tf_op jit(solution)/shard_map/ppermute | solution.py:419

commit v3 on v2

--- a/solution.py
+++ b/solution.py
@@ -10,6 +10,8 @@
 norm_eps = 1e-05
 f32, bf16 = jnp.float32, jnp.bfloat16
 TH, TW, D, NH, NS = 4, 32, 256, 16, 64
+START_ORDER = (6, 4, 3, 1, 2, 7, 5)
+FORWARDED = {7: 6, 5: 4}
 HALO = 176
 
 
@@ -87,12 +89,13 @@
         copy.wait()
 
 
-def pack(loaded, partner, sent, far):
+def pack(loaded, partner, sent, short, far):
     lower = lax.axis_index("rows") == 1
     own = [loaded[TW * (i + 1) : TW * (i + 2), :] for i in range(4)]
     rows = [partner[jnp.where(lower, i, 3 - i)] for i in range(4)] + own
     for i in range(3, 8):
         sent[TW * (i - 3) : TW * (i - 2), :] = rows[i]
+        short[TW * (i - 3) : TW * (i - 2), :] = rows[i]
     for i in range(3):
         far[i * TW : (i + 1) * TW, :] = rows[i]
     wide = [part.astype(f32) for part in rows]
@@ -125,10 +128,27 @@
     return silu(total).astype(bf16)
 
 
+def filter_row(ref, count, q, columns, shifted, taps, bias):
+    def total(b, start, size):
+        rows = [a for a in range(3) if 0 <= q + a - 1 < count]
+        parts = [taps[a][b] * ref[q + a - 1, start : start + size, :] for a in rows]
+        return functools.reduce(jnp.add, parts)
+
+    for start in range(0, columns + 8, TW):
+        size = min(TW, columns + 8 - start)
+        shifted[0, start : start + size, :] = total(0, start, size)
+        shifted[1, start + 8 : start + 8 + size, :] = total(2, start + 8, size)
+    out = []
+    for start in range(8, columns + 8, TW):
+        moved = shifted[0, start - 1 : start - 1 + TW, :] + shifted[1, start + 1 : start + 1 + TW, :]
+        out.append(silu(moved + (total(1, start, TW) + bias)).astype(bf16))
+    return out
+
+
 def local(nb, count, sent, far, *refs):
     sides, refs = refs[:count], refs[count:]
     w_in, conv_w, conv_b, w_proj, dt_bias, a_rate, d_skip = refs[:7]
-    base_out, gate_out, reads_out, edge_out, strip = refs[7:]
+    base_out, gate_out, reads_out, edge_out, strip, shifted = refs[7:]
     row, col = lax.axis_index("rows"), lax.axis_index("cols")
     lower = row == 1
     w_x = w_in[:, :D]
@@ -147,12 +167,14 @@
     left = pre_conv(left) * jnp.where(col > 0, 1.0, 0.0)
     right = pre_conv(right) * jnp.where(col < nb - 1, 1.0, 0.0)
     far_pre, own_pre = pre_conv(far[...]), pre_conv(sent[0:160, :])
+    strip[:, 0:8, :] = jnp.zeros((8, 8, D), f32)
+    strip[:, 40:48, :] = jnp.zeros((8, 8, D), f32)
     for i in range(8):
         strip[i, 8:40, :] = far_pre[i * TW : (i + 1) * TW] if i < 3 else own_pre[(i - 3) * TW : (i - 2) * TW]
         strip[i, 7:8, :] = left[8 + i : 9 + i]
         strip[i, 40:41, :] = right[i : i + 1]
     taps, bias = direction_taps(conv_w, lower), conv_b[...]
-    strip_mixed = [filtered(strip, 8, q, 8, taps, bias) for q in range(8)]
+    strip_mixed = [filter_row(strip, 8, q, TW, shifted.at[q % 2], taps, bias)[0] for q in range(8)]
     own = jnp.concatenate(strip_mixed[4:], axis=0)
     column_tokens = jnp.concatenate(strip_mixed, axis=0)
     gate_out[...] = silu(dot(sent[TW:160, :], w_in[:, D:]))
@@ -169,6 +191,7 @@
     logs = [-steps[k] * a_rate[k : k + 1, :] for k in range(2)]
     write = [projected[k][:, NH : NH + NS].astype(bf16) for k in range(2)]
     read = [projected[k][:, NH + NS :].astype(bf16) for k in range(2)]
+    reach = [dot(read[k], w_proj[k, NH : NH + NS, :]).astype(bf16) for k in range(2)]
     from_edge = [
         dot_wide(jnp.exp(wide_dot(mask, logs[k])), expand) for k, mask in enumerate((upto, onward))
     ]
@@ -177,18 +200,20 @@
     spread = ones_where(pair_c // TW == pair_r)
     inner_r, inner_c = iotas(128, NH * TW)
     inner_u, inner_s = inner_r % TW, inner_c % TW
-    parts = []
-    for k, keep in enumerate((inner_u > inner_s, inner_u < inner_s)):
-        for part in split(logs[k]):
-            parts.append(jnp.where(keep, dot(part, spread), 0.0).astype(bf16))
-    step_parts = [jnp.where(inner_u == inner_s, dot_wide(steps[k], spread), 0.0) for k in range(2)]
+    stacked = [part for k in range(2) for part in split(logs[k])] + [part for k in range(2) for part in split(steps[k])]
+    wide = dot(jnp.concatenate(stacked, axis=0), spread)
+    wide = [wide[i * 128 : (i + 1) * 128] for i in range(8)]
+    parts = [
+        jnp.where(inner_u > inner_s if i < 2 else inner_u < inner_s, wide[i], 0.0).astype(bf16) for i in range(4)
+    ]
+    step_parts = [jnp.where(inner_u == inner_s, wide[4 + 2 * k] + wide[5 + 2 * k], 0.0) for k in range(2)]
     time_r, time_c = iotas(TW, TW)
     first, second = ones_where(time_c <= time_r), ones_where(time_c >= time_r)
     walk = jnp.concatenate([first, first, second, second], axis=1)
     local_t, local_s = iotas(TW, NH * TW)
     local_s = local_s % TW
     feature = lax.broadcasted_iota(jnp.int32, (TW, D), 1) // NH
-    zeros = jnp.zeros((TW, NS), bf16)
+    head_mask = [ones_where(feature == h) for h in range(NH)]
     across = []
     for q in range(4):
         rows = slice(q * TW, (q + 1) * TW)
@@ -201,17 +226,10 @@
         weights = (weights * jnp.exp(gaps)).astype(bf16)
         values = own[rows]
         spread_values = jnp.concatenate(
-            [jnp.where(feature == h, values, jnp.zeros_like(values)) for h in range(NH)], axis=0
+            [values * head_mask[h] for h in range(NH)], axis=0
         )
         result = dot(weights, spread_values)
-        reads = jnp.concatenate(
-            [
-                jnp.concatenate([read[0][rows], zeros], axis=1),
-                jnp.concatenate([zeros, read[1][rows]], axis=1),
-            ],
-            axis=0,
-        )
-        reads_out[q] = reads
+        reads_out[q] = jnp.concatenate([reach[0][rows], reach[1][rows]], axis=0)
         across.append(result)
     across = jnp.concatenate(across, axis=0)
 
@@ -274,7 +292,7 @@
     blocks, refs = refs[:count], refs[count:]
     base_in, gate_in, reads_in, edge_in = refs[:4]
     w_in, conv_w, conv_b, w_proj, dt_bias, a_rate, gain, w_out, out = refs[4:13]
-    pre, mixed, la_all, dt_all, totals, writes, scaled = refs[13:]
+    pre, mixed, la_all, dt_all, totals, attended, scaled = refs[13:]
     row, col = lax.axis_index("rows"), lax.axis_index("cols")
     lower = row == 1
     ng = nb // 8
@@ -312,23 +330,21 @@
     def first_pass(g):
         group = lane // NH + g * 8
         is_left = group < col
-        w_both = jnp.concatenate(
-            [jnp.where(g * 8 + j < col, w_proj[0, 0:NH, :], w_proj[1, 0:NH, :]) for j in range(8)]
-            + [w_proj[k, NH : NH + NS, :] for k in range(2)],
-            axis=0,
+        w_step = jnp.concatenate(
+            [jnp.where(g * 8 + j < col, w_proj[0, 0:NH, :], w_proj[1, 0:NH, :]) for j in range(8)], axis=0
         )
         raw = jnp.zeros((128, 128), f32)
         for j in range(8):
             base = g * (8 * TW) + (8 + TW * j)
             for q in range(1, 5):
                 mixed[g * 8 + j, (q - 1) * TW : q * TW, :] = filtered(pre, 5, q, base, taps, bias)
-            result = dot_t(mixed[g * 8 + j], w_both)
-            raw = jnp.where(lane // NH == j, result[:, :128], raw)
+            raw = jnp.where(lane // NH == j, dot_t(mixed[g * 8 + j], w_step), raw)
             block = g * 8 + j
-            keep = jnp.where(lane < NS, jnp.where(block < col, 1.0, 0.0), jnp.where(block > col, 1.0, 0.0))
-            vectors = (result[:, 128:] * keep).astype(bf16)
+            side = lax.broadcasted_iota(jnp.int32, (1, 2 * TW), 1) < TW
+            keep = jnp.where(side, jnp.where(block < col, 1.0, 0.0), jnp.where(block > col, 1.0, 0.0))
             for q in range(4):
-                writes[q, at(g, j), :] = vectors[q * TW : (q + 1) * TW]
+                tokens = mixed[g * 8 + j, q * TW : (q + 1) * TW, :]
+                attended[q, at(g, j), :] = (dot_t(tokens, reads_in[q]) * keep).astype(bf16)
         steps = softplus(raw + jnp.where(is_left, bias_2[0:1], bias_2[1:2]))
         steps = jnp.where(group == col, 0.0, steps)
         logs = -steps * jnp.where(is_left, rate_2[0:1], rate_2[1:2])
@@ -367,11 +383,14 @@
 
     each(ng, second_pass)
 
+    finish(lower, attended, 0, scaled, base_in, gate_in, edge_in, gain, w_out, out)
+
+
+def finish(lower, attended, axis, scaled, base_in, gate_in, edge_in, gain, w_out, out):
     entered = []
     for q in range(4):
         rows = slice(q * TW, (q + 1) * TW)
-        state = lax.dot_general(writes[q], scaled[q], (((0,), (0,)), ((), ())), preferred_element_type=f32)
-        both = wide_dot(reads_in[q], state)
+        both = lax.dot_general(attended[q], scaled[q], (((axis,), (0,)), ((), ())), preferred_element_type=f32)
         entered.append(both[:TW] * edge_in[0, rows, :] + both[TW:] * edge_in[1, rows, :])
     combined = base_in[...] + jnp.concatenate(entered, axis=0)
 
@@ -381,6 +400,110 @@
     result = dot(gated, w_out[...]).astype(bf16)
     for i in range(4):
         out[jnp.where(lower, i, 3 - i)] = result[i * TW : (i + 1) * TW]
+
+
+def early(sent, first, second, third, w_in, conv_w, conv_b, pre, mixed, shifted):
+    col = lax.axis_index("cols")
+    lower = lax.axis_index("rows") == 1
+    w_x = w_in[:, :D]
+    pre[:, 0:8, :] = jnp.zeros((5, 8, D), f32)
+    pre[:, 136:144, :] = jnp.zeros((5, 8, D), f32)
+    for step, block in enumerate((sent, first, second, third)):
+        place_rows(pre, block, w_x, (col & 3) ^ step)
+    taps, bias = direction_taps(conv_w, lower), conv_b[...]
+    for q in range(1, 5):
+        for j, part in enumerate(filter_row(pre, 5, q, 128, shifted.at[q % 2], taps, bias)):
+            mixed[q - 1, TW * j : TW * (j + 1), :] = part
+
+
+def place_rows(pre, block, w_x, position):
+    rows = dot(block[0:160, :], w_x).astype(bf16).astype(f32)
+    base = pl.multiple_of(position * TW + 8, 8)
+    for q in range(5):
+        pre[q, pl.ds(base, TW), :] = rows[q * TW : (q + 1) * TW]
+
+
+def late(*refs):
+    blocks, (half_pre, half_mixed, base_in, gate_in, reads_in, edge_in), refs = refs[:4], refs[4:10], refs[10:]
+    w_in, conv_w, conv_b, w_proj, dt_bias, a_rate, gain, w_out, out = refs[:9]
+    pre, mixed, attended, scaled, pick, shifted = refs[9:]
+    pre[:, 0:8, :] = jnp.zeros((5, 8, D), f32)
+    pre[:, 136:144, :] = jnp.zeros((5, 8, D), f32)
+    row, col = lax.axis_index("rows"), lax.axis_index("cols")
+    lower = row == 1
+    on_left = col < 4
+    w_x = w_in[:, :D]
+    for step, block in enumerate(blocks):
+        place_rows(pre, block, w_x, (col & 3) ^ step)
+    zero = jnp.zeros((1, D), f32)
+    for q in range(5):
+        pre[q, 7:8, :] = jnp.where(on_left, half_pre[q, 135:136, :], zero)
+        pre[q, 136:137, :] = jnp.where(on_left, zero, half_pre[q, 8:9, :])
+    taps, bias = direction_taps(conv_w, lower), conv_b[...]
+    for q in range(4):
+        for j, part in enumerate(filter_row(pre, 5, q + 1, 128, shifted.at[q % 2], taps, bias)):
+            mixed[q, 128 + TW * j : 128 + TW * (j + 1), :] = part
+    tile = lax.broadcasted_iota(jnp.int32, (16, D), 0)
+    low_place, high_place = jnp.where(on_left, 16, 0), jnp.where(on_left, 15, 16)
+    for q in range(4):
+        total = bias
+        for a in range(3):
+            if q + a < 5:
+                at_left = (half_pre[q + a, 134:135, :], half_pre[q + a, 135:136, :], pre[q + a, 8:9, :])
+                at_right = (pre[q + a, 135:136, :], half_pre[q + a, 8:9, :], half_pre[q + a, 9:10, :])
+                for b in range(3):
+                    total = total + taps[a][b] * jnp.where(on_left, at_left[b], at_right[b])
+        value = silu(total)
+        mixed[q, 16:112, :] = half_mixed[q, 16:112, :]
+        for start, place in ((0, low_place), (112, high_place)):
+            held = half_mixed[q, start : start + 16, :].astype(f32)
+            mixed[q, start : start + 16, :] = jnp.where(tile == place, value, held).astype(bf16)
+
+    turn = jnp.where(on_left, 0, 4)
+    head_lane = ones_where(iotas(NH, 128)[1] % NH == iotas(NH, 128)[0])
+    tok_r, tok_c = iotas(128, 128)
+    same_row = tok_r // TW == tok_c // TW
+    after = ones_where(same_row & (tok_c > tok_r))
+    before = ones_where(same_row & (tok_c < tok_r))
+    row_ones = ones_where(same_row)
+    lane = lax.broadcasted_iota(jnp.int32, (1, 128), 1)
+    group = (lane // NH) ^ turn
+    is_left = group < col
+    bias_2 = dot_wide(dt_bias[0:2, :], head_lane)
+    rate_2 = dot_wide(a_rate[0:2, :], head_lane)
+    w_step = jnp.concatenate(
+        [jnp.where((j ^ turn) < col, w_proj[0, 0:NH, :], w_proj[1, 0:NH, :]) for j in range(8)], axis=0
+    )
+    side, block = iotas(2 * TW, 256)
+    block = (block // TW) ^ turn
+    keep = jnp.where(side < TW, jnp.where(block < col, 1.0, 0.0), jnp.where(block > col, 1.0, 0.0))
+    raw = []
+    for q in range(4):
+        result = dot_t(mixed[q], w_step)
+        row_raw = result[0:TW]
+        for j in range(1, 8):
+            row_raw = jnp.where(lane // NH == j, result[TW * j : TW * (j + 1)], row_raw)
+        raw.append(row_raw)
+        attended[q] = (dot_t(reads_in[q], mixed[q]) * keep).astype(bf16)
+    raw = jnp.concatenate(raw, axis=0)
+    steps = softplus(raw + jnp.where(is_left, bias_2[0:1], bias_2[1:2]))
+    steps = jnp.where(group == col, 0.0, steps)
+    logs = -steps * jnp.where(is_left, rate_2[0:1], rate_2[1:2])
+    source, target = (tok_r // NH) ^ turn, (tok_c // NH) ^ turn
+    nearer = ((source > target) & (source < col)) | ((source < target) & (source > col))
+    reach = dot_wide(wide_dot(row_ones, logs), ones_where(nearer & (tok_r % NH == tok_c % NH)))
+    reach = reach + wide_dot(after, jnp.where(is_left, logs, 0.0)) + wide_dot(before, jnp.where(is_left, 0.0, logs))
+    weight = split(jnp.exp(reach) * steps)
+    pick[0:112, :] = jnp.zeros((112, D), bf16)
+    pick[112:128, :] = ones_where(iotas(NH, D)[1] // NH == iotas(NH, D)[0])
+    pick[128:240, :] = jnp.zeros((112, D), bf16)
+    for j in range(8):
+        mask = pick[112 - NH * j : 240 - NH * j, :]
+        factor = dot(weight[0], mask) + dot(weight[1], mask)
+        for q in range(4):
+            cells = slice(TW * j, TW * (j + 1))
+            scaled[q, cells, :] = (mixed[q, cells, :].astype(f32) * factor[q * TW : (q + 1) * TW]).astype(bf16)
+    finish(lower, attended, 1, scaled, base_in, gate_in, edge_in, gain, w_out, out)
 
 
 def shards(feats, w_in, conv_w, conv_b, w_proj, dt_bias, a_rate, d_skip, norm_gain, w_out):
@@ -405,11 +528,11 @@
         compiler_params=limit(8),
     )(*[pltpu.with_memory_space_constraint(part, pltpu.HBM) for part in (feats, *params)])
     w_in, conv_w, conv_b, w_proj, dt_bias, a_rate, d_skip, norm_gain, w_out = params
-    sent, far = pl.pallas_call(
+    sent, short, far = pl.pallas_call(
         pack,
-        out_shape=(shape(HALO, D, dtype=bf16), shape(96, D, dtype=bf16)),
+        out_shape=tuple(shape(count, D, dtype=bf16) for count in (HALO, 160, 96)),
         in_specs=[vmem] * 2,
-        out_specs=(vmem, vmem),
+        out_specs=(vmem,) * 3,
         input_output_aliases={0: 0},
         compiler_params=limit(4),
     )(loaded, partner)
@@ -419,37 +542,61 @@
             return lax.ppermute(part, "cols", [(i, i ^ step) for i in range(nb)])
 
         blocks = [sent] + [None] * 7
-        for step in (6, 4, 1, 3, 2):
-            blocks[step] = across(sent, step)
-        blocks[7] = across(blocks[6], 1)
-        blocks[5] = across(blocks[4], 1)
+        for block in START_ORDER:
+            source = FORWARDED.get(block)
+            own = short if block in (2, 4) else sent
+            blocks[block] = across(own, block) if source is None else across(blocks[source], block ^ source)
         sides = [blocks[1], blocks[3], blocks[7]]
     else:
         blocks = sides = [lax.all_gather(sent, "cols")]
     kept = pl.pallas_call(
         functools.partial(local, nb, len(sides)),
-        out_shape=(shape(128, D), shape(128, D), shape(4, 2 * TW, 2 * NS, dtype=bf16), shape(2, 128, D)),
+        out_shape=(shape(128, D), shape(128, D), shape(4, 2 * TW, D, dtype=bf16), shape(2, 128, D)),
         in_specs=[vmem] * (9 + len(sides)),
         out_specs=(vmem,) * 4,
-        scratch_shapes=[pltpu.VMEM((8, 48, D), f32)],
+        scratch_shapes=[pltpu.VMEM((8, 48, D), f32), pltpu.VMEM((2, 2, 48, D), f32)],
         compiler_params=limit(16 if direct else 40),
         cost_estimate=pl.CostEstimate(flops=1_000_000_000, bytes_accessed=4_000_000, transcendentals=1_000_000),
     )(sent, far, *sides, w_in, conv_w, conv_b, w_proj, dt_bias, a_rate, d_skip)
-    operands = [*blocks, *kept, w_in, conv_w, conv_b, w_proj, dt_bias, a_rate, norm_gain, w_out]
-    return pl.pallas_call(
-        functools.partial(final, nb, not direct),
-        out_shape=shape(TH, TW, D, dtype=bf16),
-        in_specs=[vmem] * len(operands),
-        out_specs=vmem,
-        scratch_shapes=[
+    tail = [w_in, conv_w, conv_b, w_proj, dt_bias, a_rate, norm_gain, w_out]
+    if direct:
+        half = pl.pallas_call(
+            early,
+            out_shape=(shape(5, 144, D), shape(4, 128, D, dtype=bf16)),
+            in_specs=[vmem] * 7,
+            out_specs=(vmem,) * 2,
+            scratch_shapes=[pltpu.VMEM((2, 2, 144, D), f32)],
+            compiler_params=limit(8),
+            cost_estimate=pl.CostEstimate(flops=200_000_000, bytes_accessed=1_500_000, transcendentals=200_000),
+        )(*blocks[:4], w_in, conv_w, conv_b)
+        operands = [*blocks[4:], *half, *kept, *tail]
+        body = late
+        scratch = [
+            pltpu.VMEM((5, 144, D), f32),
+            pltpu.VMEM((4, 256, D), bf16),
+            pltpu.VMEM((4, 2 * TW, 256), bf16),
+            pltpu.VMEM((4, 256, D), bf16),
+            pltpu.VMEM((240, D), bf16),
+            pltpu.VMEM((2, 2, 144, D), f32),
+        ]
+    else:
+        operands = [*blocks, *kept, *tail]
+        body = functools.partial(final, nb, True)
+        scratch = [
             pltpu.VMEM((5, nb * TW + 16, D), f32),
             pltpu.VMEM((nb, 128, D), bf16),
             pltpu.VMEM((nb // 8, 128, 128), f32),
             pltpu.VMEM((nb // 8, 128, 128), f32),
             pltpu.VMEM((nb // 8, 128, 128), f32),
-            pltpu.VMEM((4, nb * TW, 128), bf16),
+            pltpu.VMEM((4, nb * TW, 2 * TW), bf16),
             pltpu.VMEM((4, nb * TW, D), bf16),
-        ],
+        ]
+    return pl.pallas_call(
+        body,
+        out_shape=shape(TH, TW, D, dtype=bf16),
+        in_specs=[vmem] * len(operands),
+        out_specs=vmem,
+        scratch_shapes=scratch,
         compiler_params=limit(16 if direct else 48),
         cost_estimate=pl.CostEstimate(flops=1_000_000_000, bytes_accessed=4_000_000, transcendentals=1_000_000),
     )(*operands)

time: 24.1 us -> 23.6 us (0.979)
  starting transfers between devices: 13.5 us -> 11.3 us
  waiting for transfers between devices: 1.64 us -> 3.34 us
    ppermute x7, starting transfers between devices: 13 us -> 10.8 us  [across(): return lax.ppermute(part, 'cols', [(i, i ^ step) for i in range(nb)])]
    ppermute x7, waiting for transfers between devices: 1.64 us -> 3.34 us  [across(): return lax.ppermute(part, 'cols', [(i, i ^ step) for i in range(nb)])]
    pallas_call x2 -> x3, Pallas kernels: 3.86 us -> 3.84 us  [the longest x1 3.02 us: shards(): pl.pallas_call(body, out_shape=shape(TH, TW, D, dtype=bf16), in_specs=[vm...]
  transfers between devices with their start and end apart: 8 -> 8, of which waited for: 2 -> 2; matrix products, arithmetic and copies ran while one was open for 0% -> 0% of each run, Pallas kernels for 20% -> 24%
where the time goes in v3:
time: 23.6 us; the launch traced here: 23.4 us
  starting transfers between devices  11.3 us (48%)
  Pallas kernels  8.7 us (37%)
  waiting for transfers between devices  3.34 us (14%)
    ppermute x7, starting transfers between devices, across(): return lax.ppermute(part, 'cols', [(i, i ^ step) for i in range(nb)])  10.8 us
    pallas_call x1, Pallas kernels, shards(): pl.pallas_call(functools.partial(local, nb, len(sides)), out_shape=(shape...  3.55 us
    ppermute x7, waiting for transfers between devices, across(): return lax.ppermute(part, 'cols', [(i, i ^ step) for i in range(nb)])  3.34 us
    pallas_call x1, Pallas kernels, shards(): pl.pallas_call(body, out_shape=shape(TH, TW, D, dtype=bf16), in_specs=[vm...  3.02 us
    pallas_call x1, Pallas kernels, shards(): pl.pallas_call(load, out_shape=(shape(HALO, D, dtype=bf16), *[shape(*part...  1.3 us
    pallas_call x1, Pallas kernels, shards(): pl.pallas_call(early, out_shape=(shape(5, 144, D), shape(4, 128, D, dtype...  0.78 us
    ppermute x1, starting transfers between devices, shards(): partner = lax.ppermute(feats, 'rows', [(0, 1), (1, 0)])  0.49 us
  transfers between devices with their start and end apart: 8, of which 2 were waited for; matrix products, arithmetic and copies ran while one was open for 0% of the time, Pallas kernels for 24%

profile of v3, /device:TPU:0, one launch (start us, length us, event | category | flops | bytes accessed | tf_op | source)
XLA Modules:
  0.0 23.4 jit_solution(10399403327687249531)
XLA Ops:
  0.0 0.5 %collective-permute-start = (bf16[4,32,256]{2,1,0:T(8,128)(2,1)}, bf16[4,32,256]{2,1,0:T(8,128)(2,1)S(1)}, u32[]{:S(2)}, u32[]{:S(2)}) collective-permute-start(bf16[4,32,256]{2,1,0:T(8,128)(2,1)} %feats.1), channel_id=1, source_target_pairs={{0,8},{8,0},{1,9},{9,1},{2,10},{10,2},{3,11},{11,3},{4,12},{12,4},... | collective-permute-start | bytes 196616 | tf_op jit(solution)/shard_map/ppermute | solution.py:520
  0.5 1.3 %shard_map.100 = (bf16[176,256]{1,0:T(8,128)(2,1)S(1)}, bf16[256,512]{1,0:T(8,128)(2,1)S(1)}, f32[9,256]{1,0:T(8,128)S(1)}, f32[1,256]{1,0:T(1,128)S(1)}, bf16[4...) custom-call(bf16[4,32,256]{2,1,0:T(8,128)(2,1)} %feats.1, ...), custom_call_target="tpu_custom_call" | custom-call | tf_op jit(solution)/shard_map/pallas_call | solution.py:522
  1.8 0.0 collective-permute-done.partner
  1.9 4.8 %collective-permute-start.3 = (bf16[176,256]{1,0:T(8,128)(2,1)S(1)}, bf16[176,256]{1,0:T(8,128)(2,1)S(1)}, u32[]{:S(2)}, u32[]{:S(2)}) collective-permute-start(bf16[176,256]{1,0:T(8,128)(2,1)S(1)} %get-tuple-element.26.sent), channel_id=1, source_target_pairs={{0,6},{1,7},{2,4},{3,5},{4,2},{5,3},{6,0},{7,1},{8,14},{9,15},{10,... | collective-permute-start | bytes 270344 | tf_op jit(solution)/shard_map/ppermute | solution.py:542
  6.6 1.5 %collective-permute-start.5 = (bf16[176,256]{1,0:T(8,128)(2,1)S(1)}, bf16[176,256]{1,0:T(8,128)(2,1)S(1)}, u32[]{:S(2)}, u32[]{:S(2)}) collective-permute-start(bf16[176,256]{1,0:T(8,128)(2,1)S(1)} %get-tuple-element.26.sent), channel_id=1, source_target_pairs={{0,1},{1,0},{2,3},{3,2},{4,5},{5,4},{6,7},{7,6},{8,9},{9,8},{10,11... | collective-permute-start | bytes 270344 | tf_op jit(solution)/shard_map/ppermute | solution.py:542
  8.2 0.0 collective-permute-start.7
  8.2 0.6 %collective-permute-start.1 = (bf16[160,256]{1,0:T(8,128)(2,1)S(1)}, bf16[160,256]{1,0:T(8,128)(2,1)S(1)}, u32[]{:S(2)}, u32[]{:S(2)}) collective-permute-start(bf16[160,256]{1,0:T(8,128)(2,1)S(1)} %get-tuple-element.25), channel_id=1, source_target_pairs={{0,4},{1,5},{2,6},{3,7},{4,0},{5,1},{6,2},{7,3},{8,12},{9,13},{10,... | collective-permute-start | bytes 245768 | tf_op jit(solution)/shard_map/ppermute | solution.py:542
  8.8 1.4 %collective-permute-start.6 = (bf16[160,256]{1,0:T(8,128)(2,1)S(1)}, bf16[160,256]{1,0:T(8,128)(2,1)S(1)}, u32[]{:S(2)}, u32[]{:S(2)}) collective-permute-start(bf16[160,256]{1,0:T(8,128)(2,1)S(1)} %get-tuple-element.25), channel_id=1, source_target_pairs={{0,2},{1,3},{2,0},{3,1},{4,6},{5,7},{6,4},{7,5},{8,10},{9,11},{10,... | collective-permute-start | bytes 245768 | tf_op jit(solution)/shard_map/ppermute | solution.py:542
  10.1 0.0 collective-permute-done.3.refs_2_
  10.2 1.7 %collective-permute-start.4 = (bf16[176,256]{1,0:T(8,128)(2,1)S(1)}, bf16[176,256]{1,0:T(8,128)(2,1)S(1)}, u32[]{:S(2)}, u32[]{:S(2)}) collective-permute-start(bf16[176,256]{1,0:T(8,128)(2,1)S(1)} %collective-permute-done.3.refs_2_), channel_id=1, source_target_pairs={{0,1},{1,0},{2,3},{3,2},{4,5},{5,4},{6,7},{7,6},{8,9},{9,8},{10,11... | collective-permute-start | bytes 270344 | tf_op jit(solution)/shard_map/ppermute | solution.py:542
  11.8 2.8 %collective-permute-done.1.refs_0_ = bf16[160,256]{1,0:T(8,128)(2,1)S(1)} collective-permute-done((bf16[160,256]{1,0:T(8,128)(2,1)S(1)}, bf16[160,256]{1,0:T(8,128)(2,1)S(1)}, u32[]{:S(2)}, u32[]{:S(2)}) %collective-permute-start.1) | collective-permute-done | bytes 81952 | tf_op jit(solution)/shard_map/ppermute | solution.py:542
  14.7 0.8 %collective-permute-start.2 = (bf16[160,256]{1,0:T(8,128)(2,1)S(1)}, bf16[160,256]{1,0:T(8,128)(2,1)S(1)}, u32[]{:S(2)}, u32[]{:S(2)}) collective-permute-start(bf16[160,256]{1,0:T(8,128)(2,1)S(1)} %collective-permute-done.1.refs_0_), channel_id=1, source_target_pairs={{0,1},{1,0},{2,3},{3,2},{4,5},{5,4},{6,7},{7,6},{8,9},{9,8},{10,11... | collective-permute-start | bytes 245768 | tf_op jit(solution)/shard_map/ppermute | solution.py:542
  15.5 0.5 %collective-permute-done.6.second = bf16[160,256]{1,0:T(8,128)(2,1)S(1)} collective-permute-done((bf16[160,256]{1,0:T(8,128)(2,1)S(1)}, bf16[160,256]{1,0:T(8,128)(2,1)S(1)}, u32[]{:S(2)}, u32[]{:S(2)}) %collective-permute-start.6) | collective-permute-done | bytes 81952 | tf_op jit(solution)/shard_map/ppermute | solution.py:542
  16.0 0.0 collective-permute-done.5.first.refs_0_
  16.0 0.0 collective-permute-done.7.third.refs_1_
  16.0 0.8 %shard_map.102 = (f32[5,144,256]{2,1,0:T(8,128)S(1)}, bf16[4,128,256]{2,1,0:T(8,128)(2,1)S(1)}) custom-call(bf16[176,256]{1,0:T(8,128)(2,1)S(1)} %get-tuple-element.26.sent, bf16[176,256]{1,0:T(8,128)(2,1)S(1)} %collective-permute-done.5.first.refs_0_, bf16[160,256]{1,0:T(8,128)(2,1)S(1)} %collective-permute-done.6.second, ...), custom_call_target="tpu_custom_call" | custom-call | flops 200000000 | bytes 1500000 | tf_op jit(solution)/shard_map/pallas_call | solution.py:563
  16.8 0.0 collective-permute-done.4.refs_2_.refs_3_
  16.8 3.6 %shard_map.103 = (f32[128,256]{1,0:T(8,128)S(1)}, f32[128,256]{1,0:T(8,128)S(1)}, bf16[4,64,256]{2,1,0:T(8,128)(2,1)S(1)}, f32[2,128,256]{2,1,0:T(8,128)S(1)}) custom-call(bf16[176,256]{1,0:T(8,128)(2,1)S(1)} %get-tuple-element.26.sent, bf16[96,256]{1,0:T(8,128)(2,1)S(1)} %get-tuple-element.32.far, ...), custom_call_target="tpu_custom_call" | custom-call | flops 1000000000 | bytes 4000000 | tf_op jit(solution)/shard_map/pallas_call | solution.py:552
  20.3 0.0 collective-permute-done.2.refs_1_
  20.3 3.0 %shard_map.104 = bf16[4,32,256]{2,1,0:T(8,128)(2,1)} custom-call(bf16[160,256]{1,0:T(8,128)(2,1)S(1)} %collective-permute-done.1.refs_0_, bf16[160,256]{1,0:T(8,128)(2,1)S(1)} %collective-permute-done.2.refs_1_, bf16[176,256]{1,0:T(8,128)(2,1)S(1)} %collective-permute-done.3.refs_2_, bf16[176,256]{1,0:T(8,128)(2,1)S(1)} %collective-permute-done.4.refs_2_.refs_3_, ...), custom_call_target="tpu_custom_call" | custom-call | flops 1000000000 | bytes 4000000 | tf_op jit(solution)/shard_map/pallas_call | solution.py:594
  (1 shorter events, 0.0 us)
Async XLA Ops:
  0.0 1.8 %collective-permute-start = (bf16[4,32,256]{2,1,0:T(8,128)(2,1)}, bf16[4,32,256]{2,1,0:T(8,128)(2,1)S(1)}, u32[]{:S(2)}, u32[]{:S(2)}) collective-permute-start(bf16[4,32,256]{2,1,0:T(8,128)(2,1)} %feats.1), channel_id=1, source_target_pairs={{0,8},{8,0},{1,9},{9,1},{2,10},{10,2},{3,11},{11,3},{4,12},{12,4},... | collective-permute-start | bytes 196616 | tf_op jit(solution)/shard_map/ppermute | solution.py:520
  1.9 8.3 %collective-permute-start.3 = (bf16[176,256]{1,0:T(8,128)(2,1)S(1)}, bf16[176,256]{1,0:T(8,128)(2,1)S(1)}, u32[]{:S(2)}, u32[]{:S(2)}) collective-permute-start(bf16[176,256]{1,0:T(8,128)(2,1)S(1)} %get-tuple-element.26.sent), channel_id=1, source_target_pairs={{0,6},{1,7},{2,4},{3,5},{4,2},{5,3},{6,0},{7,1},{8,14},{9,15},{10,... | collective-permute-start | bytes 270344 | tf_op jit(solution)/shard_map/ppermute | solution.py:542
  6.6 9.3 %collective-permute-start.5 = (bf16[176,256]{1,0:T(8,128)(2,1)S(1)}, bf16[176,256]{1,0:T(8,128)(2,1)S(1)}, u32[]{:S(2)}, u32[]{:S(2)}) collective-permute-start(bf16[176,256]{1,0:T(8,128)(2,1)S(1)} %get-tuple-element.26.sent), channel_id=1, source_target_pairs={{0,1},{1,0},{2,3},{3,2},{4,5},{5,4},{6,7},{7,6},{8,9},{9,8},{10,11... | collective-permute-start | bytes 270344 | tf_op jit(solution)/shard_map/ppermute | solution.py:542
  8.2 7.8 %collective-permute-start.7 = (bf16[176,256]{1,0:T(8,128)(2,1)S(1)}, bf16[176,256]{1,0:T(8,128)(2,1)S(1)}, u32[]{:S(2)}, u32[]{:S(2)}) collective-permute-start(bf16[176,256]{1,0:T(8,128)(2,1)S(1)} %get-tuple-element.26.sent), channel_id=1, source_target_pairs={{0,3},{1,2},{2,1},{3,0},{4,7},{5,6},{6,5},{7,4},{8,11},{9,10},{10,... | collective-permute-start | bytes 270344 | tf_op jit(solution)/shard_map/ppermute | solution.py:542
  8.2 6.5 %collective-permute-start.1 = (bf16[160,256]{1,0:T(8,128)(2,1)S(1)}, bf16[160,256]{1,0:T(8,128)(2,1)S(1)}, u32[]{:S(2)}, u32[]{:S(2)}) collective-permute-start(bf16[160,256]{1,0:T(8,128)(2,1)S(1)} %get-tuple-element.25), channel_id=1, source_target_pairs={{0,4},{1,5},{2,6},{3,7},{4,0},{5,1},{6,2},{7,3},{8,12},{9,13},{10,... | collective-permute-start | bytes 245768 | tf_op jit(solution)/shard_map/ppermute | solution.py:542
  8.8 7.2 %collective-permute-start.6 = (bf16[160,256]{1,0:T(8,128)(2,1)S(1)}, bf16[160,256]{1,0:T(8,128)(2,1)S(1)}, u32[]{:S(2)}, u32[]{:S(2)}) collective-permute-start(bf16[160,256]{1,0:T(8,128)(2,1)S(1)} %get-tuple-element.25), channel_id=1, source_target_pairs={{0,2},{1,3},{2,0},{3,1},{4,6},{5,7},{6,4},{7,5},{8,10},{9,11},{10,... | collective-permute-start | bytes 245768 | tf_op jit(solution)/shard_map/ppermute | solution.py:542
  10.2 6.6 %collective-permute-start.4 = (bf16[176,256]{1,0:T(8,128)(2,1)S(1)}, bf16[176,256]{1,0:T(8,128)(2,1)S(1)}, u32[]{:S(2)}, u32[]{:S(2)}) collective-permute-start(bf16[176,256]{1,0:T(8,128)(2,1)S(1)} %collective-permute-done.3.refs_2_), channel_id=1, source_target_pairs={{0,1},{1,0},{2,3},{3,2},{4,5},{5,4},{6,7},{7,6},{8,9},{9,8},{10,11... | collective-permute-start | bytes 270344 | tf_op jit(solution)/shard_map/ppermute | solution.py:542
  14.7 5.7 %collective-permute-start.2 = (bf16[160,256]{1,0:T(8,128)(2,1)S(1)}, bf16[160,256]{1,0:T(8,128)(2,1)S(1)}, u32[]{:S(2)}, u32[]{:S(2)}) collective-permute-start(bf16[160,256]{1,0:T(8,128)(2,1)S(1)} %collective-permute-done.1.refs_0_), channel_id=1, source_target_pairs={{0,1},{1,0},{2,3},{3,2},{4,5},{5,4},{6,7},{7,6},{8,9},{9,8},{10,11... | collective-permute-start | bytes 245768 | tf_op jit(solution)/shard_map/ppermute | solution.py:542

commit v4 on v3

--- a/solution.py
+++ b/solution.py
@@ -145,10 +145,69 @@
     return out
 
 
-def local(nb, count, sent, far, *refs):
+def ahead(sent, far, w_in, w_proj, dt_bias, a_rate, *outs):
+    strip_pre, gate_out, triangle, spread_out, heads_out, select_out, same_out, walk_in, walk_out = outs[:9]
+    col = lax.axis_index("cols")
+    w_x = w_in[:, :D]
+    far_pre = dot(far[...], w_x).astype(bf16).astype(f32)
+    own_pre = dot(sent[0:160, :], w_x).astype(bf16).astype(f32)
+    for i in range(8):
+        strip_pre[i] = far_pre[i * TW : (i + 1) * TW] if i < 3 else own_pre[(i - 3) * TW : (i - 2) * TW]
+    gate_out[...] = silu(dot(sent[TW:160, :], w_in[:, D:]))
+    inner_u, inner_s = iotas(TW, NH * TW)
+    inner_s = inner_s % TW
+    for i, mask in enumerate((inner_u > inner_s, inner_u < inner_s, inner_u == inner_s)):
+        triangle[i] = jnp.where(mask, 1.0, 0.0)
+    pair_r, pair_c = iotas(NH, NH * TW)
+    spread_out[...] = ones_where(pair_c // TW == pair_r)
+    feature = iotas(TW, D)[1] // NH
+    for h in range(NH):
+        heads_out[h] = ones_where(feature == h)
+    source_r, source_c = iotas(256, 128)
+    select_out[...] = ones_where(source_r // TW == source_c // NH)
+    t_r, s_c = iotas(128, 256)
+    same_out[...] = jnp.where((t_r % TW) == (s_c % TW), 1.0, 0.0)
+    walk_r, walk_c = iotas(128, 512)
+    step, source, time = walk_r // NH, (walk_c % 128) // NH, walk_c // 128 + 4
+    same_head = walk_r % NH == walk_c % NH
+    walk_in[...] = ones_where(same_head & (source < step) & (step <= time))
+    walk_out[...] = ones_where(same_head & (time <= step) & (step < source))
+    if len(outs) == 9:
+        return
+    ordered, nearer_out, keep_out, pick, w_step, lanes = outs[9:]
+    turn = jnp.where(col < 4, 0, 4)
+    tok_r, tok_c = iotas(128, 128)
+    same_row = tok_r // TW == tok_c // TW
+    ordered[0] = ones_where(same_row & (tok_c > tok_r))
+    ordered[1] = ones_where(same_row & (tok_c < tok_r))
+    ordered[2] = ones_where(same_row)
+    source, target = (tok_r // NH) ^ turn, (tok_c // NH) ^ turn
+    nearer = ((source > target) & (source < col)) | ((source < target) & (source > col))
+    nearer_out[...] = ones_where(nearer & (tok_r % NH == tok_c % NH))
+    side, block = iotas(2 * TW, 256)
+    block = (block // TW) ^ turn
+    keep_out[...] = jnp.where(side < TW, jnp.where(block < col, 1.0, 0.0), jnp.where(block > col, 1.0, 0.0))
+    pick[0:112, :] = jnp.zeros((112, D), bf16)
+    pick[112:128, :] = ones_where(iotas(NH, D)[1] // NH == iotas(NH, D)[0])
+    pick[128:240, :] = jnp.zeros((112, D), bf16)
+    w_step[...] = jnp.concatenate(
+        [jnp.where((j ^ turn) < col, w_proj[0, 0:NH, :], w_proj[1, 0:NH, :]) for j in range(8)], axis=0
+    )
+    lane = lax.broadcasted_iota(jnp.int32, (1, 128), 1)
+    group = (lane // NH) ^ turn
+    head_lane = ones_where(iotas(NH, 128)[1] % NH == iotas(NH, 128)[0])
+    bias, rate = dot_wide(dt_bias[0:2, :], head_lane), dot_wide(a_rate[0:2, :], head_lane)
+    lanes[0:1, :] = jnp.where(group < col, bias[0:1], bias[1:2])
+    lanes[1:2, :] = jnp.where(group < col, rate[0:1], rate[1:2])
+    lanes[2:3, :] = jnp.where(group < col, 1.0, 0.0)
+    lanes[3:4, :] = jnp.where(group > col, 1.0, 0.0)
+
+
+def local(nb, count, *refs):
     sides, refs = refs[:count], refs[count:]
     w_in, conv_w, conv_b, w_proj, dt_bias, a_rate, d_skip = refs[:7]
-    base_out, gate_out, reads_out, edge_out, strip, shifted = refs[7:]
+    strip_pre, triangle, spread, heads, select, same_col, walk_in, walk_out = refs[7:15]
+    base_out, reads_out, edge_out, strip, shifted = refs[15:]
     row, col = lax.axis_index("rows"), lax.axis_index("cols")
     lower = row == 1
     w_x = w_in[:, :D]
@@ -166,18 +225,16 @@
         right = jnp.where(odd, jnp.where(col == 3, furthest, further), near)
     left = pre_conv(left) * jnp.where(col > 0, 1.0, 0.0)
     right = pre_conv(right) * jnp.where(col < nb - 1, 1.0, 0.0)
-    far_pre, own_pre = pre_conv(far[...]), pre_conv(sent[0:160, :])
     strip[:, 0:8, :] = jnp.zeros((8, 8, D), f32)
     strip[:, 40:48, :] = jnp.zeros((8, 8, D), f32)
     for i in range(8):
-        strip[i, 8:40, :] = far_pre[i * TW : (i + 1) * TW] if i < 3 else own_pre[(i - 3) * TW : (i - 2) * TW]
+        strip[i, 8:40, :] = strip_pre[i]
         strip[i, 7:8, :] = left[8 + i : 9 + i]
         strip[i, 40:41, :] = right[i : i + 1]
     taps, bias = direction_taps(conv_w, lower), conv_b[...]
     strip_mixed = [filter_row(strip, 8, q, TW, shifted.at[q % 2], taps, bias)[0] for q in range(8)]
     own = jnp.concatenate(strip_mixed[4:], axis=0)
     column_tokens = jnp.concatenate(strip_mixed, axis=0)
-    gate_out[...] = silu(dot(sent[TW:160, :], w_in[:, D:]))
 
     head_lane = ones_where(iotas(NH, 128)[1] % NH == iotas(NH, 128)[0])
     expand = ones_where(iotas(NH, D)[1] // NH == iotas(NH, D)[0])
@@ -196,37 +253,28 @@
         dot_wide(jnp.exp(wide_dot(mask, logs[k])), expand) for k, mask in enumerate((upto, onward))
     ]
     edge_out[0], edge_out[1] = from_edge
-    pair_r, pair_c = iotas(NH, NH * TW)
-    spread = ones_where(pair_c // TW == pair_r)
-    inner_r, inner_c = iotas(128, NH * TW)
-    inner_u, inner_s = inner_r % TW, inner_c % TW
     stacked = [part for k in range(2) for part in split(logs[k])] + [part for k in range(2) for part in split(steps[k])]
-    wide = dot(jnp.concatenate(stacked, axis=0), spread)
+    wide = dot(jnp.concatenate(stacked, axis=0), spread[...])
     wide = [wide[i * 128 : (i + 1) * 128] for i in range(8)]
-    parts = [
-        jnp.where(inner_u > inner_s if i < 2 else inner_u < inner_s, wide[i], 0.0).astype(bf16) for i in range(4)
-    ]
-    step_parts = [jnp.where(inner_u == inner_s, wide[4 + 2 * k] + wide[5 + 2 * k], 0.0) for k in range(2)]
+    later, sooner, equal = triangle[0], triangle[1], triangle[2]
     time_r, time_c = iotas(TW, TW)
     first, second = ones_where(time_c <= time_r), ones_where(time_c >= time_r)
     walk = jnp.concatenate([first, first, second, second], axis=1)
-    local_t, local_s = iotas(TW, NH * TW)
-    local_s = local_s % TW
-    feature = lax.broadcasted_iota(jnp.int32, (TW, D), 1) // NH
-    head_mask = [ones_where(feature == h) for h in range(NH)]
+    allowed = (later + equal, sooner + equal)
     across = []
     for q in range(4):
         rows = slice(q * TW, (q + 1) * TW)
-        gaps = dot(walk, jnp.concatenate([part[rows] for part in parts], axis=0))
+        parts = [(wide[i][rows] * (later if i < 2 else sooner)).astype(bf16) for i in range(4)]
+        gaps = dot(walk, jnp.concatenate(parts, axis=0))
         weights = jnp.zeros((TW, NH * TW), f32)
-        for k, keep in enumerate((local_s <= local_t, local_s >= local_t)):
+        for k, keep in enumerate(allowed):
             scores = dot_t(read[k][rows], jnp.concatenate([write[k][rows]] * NH, axis=0))
-            step_row = jnp.sum(step_parts[k][rows], axis=0, keepdims=True)
-            weights = weights + jnp.where(keep, scores * step_row, 0.0)
+            step_row = jnp.sum((wide[4 + 2 * k][rows] + wide[5 + 2 * k][rows]) * equal, axis=0, keepdims=True)
+            weights = weights + scores * step_row * keep
         weights = (weights * jnp.exp(gaps)).astype(bf16)
         values = own[rows]
         spread_values = jnp.concatenate(
-            [values * head_mask[h] for h in range(NH)], axis=0
+            [values * heads[h] for h in range(NH)], axis=0
         )
         result = dot(weights, spread_values)
         reads_out[q] = jnp.concatenate([reach[0][rows], reach[1][rows]], axis=0)
@@ -239,49 +287,42 @@
     def pick_row(ref, k):
         return jnp.where(k == 2, ref[2:3, :], ref[3:4, :])
 
-    project_in = dot_t(column_tokens, w_proj[k_in])
-    project_out = dot_t(own, w_proj[k_out])
-    steps_in = softplus(project_in[:, :NH] + pick_row(dt_bias, k_in))
-    steps_out = softplus(project_out[:, :NH] + pick_row(dt_bias, k_out))
-    logs_in = -steps_in * pick_row(a_rate, k_in)
-    logs_out = -steps_out * pick_row(a_rate, k_out)
-    write_in = project_in[:, NH : NH + NS].astype(bf16)
-    write_out = project_out[:, NH : NH + NS].astype(bf16)
-    read_in = project_in[128:, NH + NS :].astype(bf16)
-    read_out = project_out[:, NH + NS :].astype(bf16)
-    t_r, s_c = iotas(128, 256)
-    same_col = (t_r % TW) == (s_c % TW)
-    meet_in = ones_where(same_col)
-    walk_in = ones_where(same_col & (s_c // TW <= t_r // TW + 4))
-    meet_out = ones_where(tok_r % TW == tok_c % TW)
-    walk_out = ones_where((tok_r % TW == tok_c % TW) & (tok_c >= tok_r))
-    source_r, source_c = iotas(256, 128)
-    source_u, source_s = source_r // TW, source_c // NH
-    select = ones_where(source_u == source_s)
-    scores_in = dot_wide(jnp.where(same_col, dot_t(read_in, write_in), 0.0), select)
-    same_out = tok_r % TW == tok_c % TW
-    scores_out = dot_wide(jnp.where(same_out, dot_t(read_out, write_out), 0.0), select[128:])
-    out_u = tok_r // TW + 4
-    out_s = tok_c // NH
-    gap = jnp.zeros((128, 128), f32)
-    for part in split(logs_in):
-        gap = gap + dot(walk_in, jnp.where(source_u > source_s, dot(part, head_lane), 0.0).astype(bf16))
-    for part in split(logs_out):
-        gap = gap + dot(walk_out, jnp.where(out_u < out_s, dot(part, head_lane), 0.0).astype(bf16))
-    lane_in = jnp.zeros((128, 128), f32)
-    for part in split(steps_in):
-        lane_in = lane_in + dot(meet_in, jnp.where(source_u == source_s, dot(part, head_lane), 0.0).astype(bf16))
-    lane_out = jnp.zeros((128, 128), f32)
-    for part in split(steps_out):
-        lane_out = lane_out + dot(meet_out, jnp.where(out_u == out_s, dot(part, head_lane), 0.0).astype(bf16))
-    weights = jnp.where(out_s <= out_u, scores_in * lane_in, 0.0) + jnp.where(out_s >= out_u, scores_out * lane_out, 0.0)
-    weights = (weights * jnp.exp(gap)).astype(bf16)
+    lane = lax.broadcasted_iota(jnp.int32, (1, 128), 1) // NH
+    head_rows = [dot_wide(pick_row(ref, k), head_lane) for ref in (dt_bias, a_rate) for k in (k_in, k_out)]
+
+    def dense_steps(tokens, k, first, bias):
+        result = dot_t(tokens, jnp.concatenate([w_proj[k, 0:NH, :]] * 8, axis=0))
+        raw = result[0:TW]
+        for s in range(first + 1, 8):
+            raw = jnp.where(lane == s, result[(s - first) * TW : (s - first + 1) * TW], raw)
+        return softplus(raw + bias)
+
+    steps_in = dense_steps(column_tokens, k_in, 0, head_rows[0])
+    steps_out = dense_steps(own, k_out, 4, head_rows[1])
+    gap = dot(jnp.concatenate(split(-steps_in * head_rows[2]), axis=0), walk_in[...])
+    gap_out = dot(jnp.concatenate(split(-steps_out * head_rows[3]), axis=0), walk_out[...])
+    gap = (gap[:TW] + gap[TW:]) + (gap_out[:TW] + gap_out[TW:])
+    decay = jnp.exp(gap)
+    write_in = dot_t(column_tokens, w_proj[k_in, NH : NH + NS, :]).astype(bf16)
+    write_out = dot_t(own, w_proj[k_out, NH : NH + NS, :]).astype(bf16)
+    read_in = dot_t(own, w_proj[k_in, NH + NS :, :]).astype(bf16)
+    read_out = dot_t(own, w_proj[k_out, NH + NS :, :]).astype(bf16)
+    scores_in = dot_wide(dot_t(read_in, write_in) * same_col[...], select[...])
+    scores_out = dot_wide(dot_t(read_out, write_out) * same_col[:, :128], select[128:, :])
+    weights = []
+    for t in range(4):
+        rows = slice(t * TW, (t + 1) * TW)
+        sum_in = scores_in[rows] * (steps_in * jnp.where(lane <= t + 4, 1.0, 0.0))
+        sum_out = scores_out[rows] * (steps_out * jnp.where(lane >= t + 4, 1.0, 0.0))
+        weights.append((sum_in + sum_out) * decay[:, t * 128 : (t + 1) * 128])
+    weights = jnp.concatenate(weights, axis=0).astype(bf16)
     skips = dot_wide(d_skip[...], expand)
     own_wide = own.astype(f32)
     pick_r, pick_c = iotas(128, D)
+    pick_c = pick_c // NH
     vertical = (skips[2:3] + skips[3:4]) * own_wide
     for s in range(8):
-        factor = dot(weights, ones_where(pick_r == s * NH + pick_c // NH))
+        factor = dot(weights, ones_where(pick_r == s * NH + pick_c))
         values = strip_mixed[s].astype(f32)
         vertical = vertical + factor * jnp.concatenate([values] * 4, axis=0)
     base_out[...] = across + (skips[0:1] + skips[1:2]) * own_wide + vertical.astype(bf16).astype(f32)
@@ -290,7 +331,7 @@
 def final(nb, gathered, *refs):
     count = 1 if gathered else nb
     blocks, refs = refs[:count], refs[count:]
-    base_in, gate_in, reads_in, edge_in = refs[:4]
+    base_in, reads_in, edge_in, gate_in = refs[:4]
     w_in, conv_w, conv_b, w_proj, dt_bias, a_rate, gain, w_out, out = refs[4:13]
     pre, mixed, la_all, dt_all, totals, attended, scaled = refs[13:]
     row, col = lax.axis_index("rows"), lax.axis_index("cols")
@@ -424,9 +465,11 @@
 
 
 def late(*refs):
-    blocks, (half_pre, half_mixed, base_in, gate_in, reads_in, edge_in), refs = refs[:4], refs[4:10], refs[10:]
-    w_in, conv_w, conv_b, w_proj, dt_bias, a_rate, gain, w_out, out = refs[:9]
-    pre, mixed, attended, scaled, pick, shifted = refs[9:]
+    blocks, (half_pre, half_mixed, base_in, reads_in, edge_in, gate_in), refs = refs[:4], refs[4:10], refs[10:]
+    ordered, nearer, keep, pick, w_step, lanes = refs[:6]
+    refs = refs[6:]
+    w_in, conv_w, conv_b, _, _, _, gain, w_out, out = refs[:9]
+    pre, mixed, attended, scaled, shifted = refs[9:]
     pre[:, 0:8, :] = jnp.zeros((5, 8, D), f32)
     pre[:, 136:144, :] = jnp.zeros((5, 8, D), f32)
     row, col = lax.axis_index("rows"), lax.axis_index("cols")
@@ -459,44 +502,22 @@
             held = half_mixed[q, start : start + 16, :].astype(f32)
             mixed[q, start : start + 16, :] = jnp.where(tile == place, value, held).astype(bf16)
 
-    turn = jnp.where(on_left, 0, 4)
-    head_lane = ones_where(iotas(NH, 128)[1] % NH == iotas(NH, 128)[0])
-    tok_r, tok_c = iotas(128, 128)
-    same_row = tok_r // TW == tok_c // TW
-    after = ones_where(same_row & (tok_c > tok_r))
-    before = ones_where(same_row & (tok_c < tok_r))
-    row_ones = ones_where(same_row)
     lane = lax.broadcasted_iota(jnp.int32, (1, 128), 1)
-    group = (lane // NH) ^ turn
-    is_left = group < col
-    bias_2 = dot_wide(dt_bias[0:2, :], head_lane)
-    rate_2 = dot_wide(a_rate[0:2, :], head_lane)
-    w_step = jnp.concatenate(
-        [jnp.where((j ^ turn) < col, w_proj[0, 0:NH, :], w_proj[1, 0:NH, :]) for j in range(8)], axis=0
-    )
-    side, block = iotas(2 * TW, 256)
-    block = (block // TW) ^ turn
-    keep = jnp.where(side < TW, jnp.where(block < col, 1.0, 0.0), jnp.where(block > col, 1.0, 0.0))
     raw = []
     for q in range(4):
-        result = dot_t(mixed[q], w_step)
+        result = dot_t(mixed[q], w_step[...])
         row_raw = result[0:TW]
         for j in range(1, 8):
             row_raw = jnp.where(lane // NH == j, result[TW * j : TW * (j + 1)], row_raw)
         raw.append(row_raw)
-        attended[q] = (dot_t(reads_in[q], mixed[q]) * keep).astype(bf16)
+        attended[q] = (dot_t(reads_in[q], mixed[q]) * keep[...]).astype(bf16)
     raw = jnp.concatenate(raw, axis=0)
-    steps = softplus(raw + jnp.where(is_left, bias_2[0:1], bias_2[1:2]))
-    steps = jnp.where(group == col, 0.0, steps)
-    logs = -steps * jnp.where(is_left, rate_2[0:1], rate_2[1:2])
-    source, target = (tok_r // NH) ^ turn, (tok_c // NH) ^ turn
-    nearer = ((source > target) & (source < col)) | ((source < target) & (source > col))
-    reach = dot_wide(wide_dot(row_ones, logs), ones_where(nearer & (tok_r % NH == tok_c % NH)))
-    reach = reach + wide_dot(after, jnp.where(is_left, logs, 0.0)) + wide_dot(before, jnp.where(is_left, 0.0, logs))
+    left, right = lanes[2:3, :], lanes[3:4, :]
+    steps = softplus(raw + lanes[0:1, :]) * (left + right)
+    logs = -steps * lanes[1:2, :]
+    reach = dot_wide(wide_dot(ordered[2], logs), nearer[...])
+    reach = reach + wide_dot(ordered[0], logs * left) + wide_dot(ordered[1], logs * right)
     weight = split(jnp.exp(reach) * steps)
-    pick[0:112, :] = jnp.zeros((112, D), bf16)
-    pick[112:128, :] = ones_where(iotas(NH, D)[1] // NH == iotas(NH, D)[0])
-    pick[128:240, :] = jnp.zeros((112, D), bf16)
     for j in range(8):
         mask = pick[112 - NH * j : 240 - NH * j, :]
         factor = dot(weight[0], mask) + dot(weight[1], mask)
@@ -549,15 +570,44 @@
         sides = [blocks[1], blocks[3], blocks[7]]
     else:
         blocks = sides = [lax.all_gather(sent, "cols")]
+    outs = [
+        shape(8, TW, D),
+        shape(128, D),
+        shape(3, TW, NH * TW),
+        shape(NH, NH * TW, dtype=bf16),
+        shape(NH, TW, D, dtype=bf16),
+        shape(256, 128, dtype=bf16),
+        shape(128, 256),
+        shape(128, 512, dtype=bf16),
+        shape(128, 512, dtype=bf16),
+    ]
+    if direct:
+        outs += [
+            shape(3, 128, 128, dtype=bf16),
+            shape(128, 128, dtype=bf16),
+            shape(2 * TW, 256),
+            shape(240, D, dtype=bf16),
+            shape(128, D, dtype=bf16),
+            shape(8, 128),
+        ]
+    strip_pre, gate, *masks = pl.pallas_call(
+        ahead,
+        out_shape=tuple(outs),
+        in_specs=[vmem] * 6,
+        out_specs=(vmem,) * len(outs),
+        compiler_params=limit(8),
+        cost_estimate=pl.CostEstimate(flops=200_000_000, bytes_accessed=1_500_000, transcendentals=50_000),
+    )(sent, far, w_in, w_proj, dt_bias, a_rate)
     kept = pl.pallas_call(
         functools.partial(local, nb, len(sides)),
-        out_shape=(shape(128, D), shape(128, D), shape(4, 2 * TW, D, dtype=bf16), shape(2, 128, D)),
-        in_specs=[vmem] * (9 + len(sides)),
-        out_specs=(vmem,) * 4,
+        out_shape=(shape(128, D), shape(4, 2 * TW, D, dtype=bf16), shape(2, 128, D)),
+        in_specs=[vmem] * (15 + len(sides)),
+        out_specs=(vmem,) * 3,
         scratch_shapes=[pltpu.VMEM((8, 48, D), f32), pltpu.VMEM((2, 2, 48, D), f32)],
-        compiler_params=limit(16 if direct else 40),
+        compiler_params=limit(16 if direct else 32),
         cost_estimate=pl.CostEstimate(flops=1_000_000_000, bytes_accessed=4_000_000, transcendentals=1_000_000),
-    )(sent, far, *sides, w_in, conv_w, conv_b, w_proj, dt_bias, a_rate, d_skip)
+    )(*sides, w_in, conv_w, conv_b, w_proj, dt_bias, a_rate, d_skip, strip_pre, *masks[:7])
+    kept = [*kept, gate]
     tail = [w_in, conv_w, conv_b, w_proj, dt_bias, a_rate, norm_gain, w_out]
     if direct:
         half = pl.pallas_call(
@@ -569,14 +619,13 @@
             compiler_params=limit(8),
             cost_estimate=pl.CostEstimate(flops=200_000_000, bytes_accessed=1_500_000, transcendentals=200_000),
         )(*blocks[:4], w_in, conv_w, conv_b)
-        operands = [*blocks[4:], *half, *kept, *tail]
+        operands = [*blocks[4:], *half, *kept, *masks[7:], *tail]
         body = late
         scratch = [
             pltpu.VMEM((5, 144, D), f32),
             pltpu.VMEM((4, 256, D), bf16),
             pltpu.VMEM((4, 2 * TW, 256), bf16),
             pltpu.VMEM((4, 256, D), bf16),
-            pltpu.VMEM((240, D), bf16),
             pltpu.VMEM((2, 2, 144, D), f32),
         ]
     else:

time: 23.6 us -> 23 us (0.975)
  waiting for transfers between devices: 3.34 us -> 2.97 us
    pallas_call x1, Pallas kernels: 3.55 us -> 2.92 us  [shards(): pl.pallas_call(functools.partial(local, nb, len(sides)), out_shape=(shape...]
    ppermute x7, waiting for transfers between devices: 3.34 us -> 2.97 us  [across(): return lax.ppermute(part, 'cols', [(i, i ^ step) for i in range(nb)])]
    pallas_call x0 -> x1, Pallas kernels: none -> 0.37 us  [shards(): pl.pallas_call(ahead, out_shape=tuple(outs), in_specs=[vmem] * 6, out_spe...]
where the time goes in v4:
time: 23 us; the launch traced here: 22.8 us
  starting transfers between devices  11.3 us (49%)
  Pallas kernels  8.52 us (37%)
  waiting for transfers between devices  2.97 us (13%)
    ppermute x7, starting transfers between devices, across(): return lax.ppermute(part, 'cols', [(i, i ^ step) for i in range(nb)])  10.8 us
    pallas_call x1, Pallas kernels, shards(): pl.pallas_call(body, out_shape=shape(TH, TW, D, dtype=bf16), in_specs=[vm...  3.09 us
    ppermute x7, waiting for transfers between devices, across(): return lax.ppermute(part, 'cols', [(i, i ^ step) for i in range(nb)])  2.97 us
    pallas_call x1, Pallas kernels, shards(): pl.pallas_call(functools.partial(local, nb, len(sides)), out_shape=(shape...  2.92 us
    pallas_call x1, Pallas kernels, shards(): pl.pallas_call(load, out_shape=(shape(HALO, D, dtype=bf16), *[shape(*part...  1.3 us
    pallas_call x1, Pallas kernels, shards(): pl.pallas_call(early, out_shape=(shape(5, 144, D), shape(4, 128, D, dtype...  0.79 us
    ppermute x1, starting transfers between devices, shards(): partner = lax.ppermute(feats, 'rows', [(0, 1), (1, 0)])  0.49 us
  transfers between devices with their start and end apart: 8, of which 2 were waited for; matrix products, arithmetic and copies ran while one was open for 0% of the time, Pallas kernels for 24%

profile of v4, /device:TPU:0, one launch (start us, length us, event | category | flops | bytes accessed | tf_op | source)
XLA Modules:
  0.0 22.8 jit_solution(4972333224674705104)
XLA Ops:
  0.0 0.5 %collective-permute-start = (bf16[4,32,256]{2,1,0:T(8,128)(2,1)}, bf16[4,32,256]{2,1,0:T(8,128)(2,1)S(1)}, u32[]{:S(2)}, u32[]{:S(2)}) collective-permute-start(bf16[4,32,256]{2,1,0:T(8,128)(2,1)} %feats.1), channel_id=1, source_target_pairs={{0,8},{8,0},{1,9},{9,1},{2,10},{10,2},{3,11},{11,3},{4,12},{12,4},... | collective-permute-start | bytes 196616 | tf_op jit(solution)/shard_map/ppermute | solution.py:541
  0.5 1.3 %shard_map.100 = (bf16[176,256]{1,0:T(8,128)(2,1)S(1)}, bf16[256,512]{1,0:T(8,128)(2,1)S(1)}, f32[9,256]{1,0:T(8,128)S(1)}, f32[1,256]{1,0:T(1,128)S(1)}, bf16[4...) custom-call(bf16[4,32,256]{2,1,0:T(8,128)(2,1)} %feats.1, ...), custom_call_target="tpu_custom_call" | custom-call | tf_op jit(solution)/shard_map/pallas_call | solution.py:543
  1.8 0.0 collective-permute-done.partner
  1.9 4.8 %collective-permute-start.3 = (bf16[176,256]{1,0:T(8,128)(2,1)S(1)}, bf16[176,256]{1,0:T(8,128)(2,1)S(1)}, u32[]{:S(2)}, u32[]{:S(2)}) collective-permute-start(bf16[176,256]{1,0:T(8,128)(2,1)S(1)} %get-tuple-element.40.sent), channel_id=1, source_target_pairs={{0,6},{1,7},{2,4},{3,5},{4,2},{5,3},{6,0},{7,1},{8,14},{9,15},{10,... | collective-permute-start | bytes 270344 | tf_op jit(solution)/shard_map/ppermute | solution.py:563
  6.6 1.5 %collective-permute-start.5 = (bf16[176,256]{1,0:T(8,128)(2,1)S(1)}, bf16[176,256]{1,0:T(8,128)(2,1)S(1)}, u32[]{:S(2)}, u32[]{:S(2)}) collective-permute-start(bf16[176,256]{1,0:T(8,128)(2,1)S(1)} %get-tuple-element.40.sent), channel_id=1, source_target_pairs={{0,1},{1,0},{2,3},{3,2},{4,5},{5,4},{6,7},{7,6},{8,9},{9,8},{10,11... | collective-permute-start | bytes 270344 | tf_op jit(solution)/shard_map/ppermute | solution.py:563
  8.2 0.0 collective-permute-start.7
  8.2 0.6 %collective-permute-start.1 = (bf16[160,256]{1,0:T(8,128)(2,1)S(1)}, bf16[160,256]{1,0:T(8,128)(2,1)S(1)}, u32[]{:S(2)}, u32[]{:S(2)}) collective-permute-start(bf16[160,256]{1,0:T(8,128)(2,1)S(1)} %get-tuple-element.39), channel_id=1, source_target_pairs={{0,4},{1,5},{2,6},{3,7},{4,0},{5,1},{6,2},{7,3},{8,12},{9,13},{10,... | collective-permute-start | bytes 245768 | tf_op jit(solution)/shard_map/ppermute | solution.py:563
  8.8 1.4 %collective-permute-start.6 = (bf16[160,256]{1,0:T(8,128)(2,1)S(1)}, bf16[160,256]{1,0:T(8,128)(2,1)S(1)}, u32[]{:S(2)}, u32[]{:S(2)}) collective-permute-start(bf16[160,256]{1,0:T(8,128)(2,1)S(1)} %get-tuple-element.39), channel_id=1, source_target_pairs={{0,2},{1,3},{2,0},{3,1},{4,6},{5,7},{6,4},{7,5},{8,10},{9,11},{10,... | collective-permute-start | bytes 245768 | tf_op jit(solution)/shard_map/ppermute | solution.py:563
  10.1 0.0 collective-permute-done.3.refs_2_
  10.2 1.7 %collective-permute-start.4 = (bf16[176,256]{1,0:T(8,128)(2,1)S(1)}, bf16[176,256]{1,0:T(8,128)(2,1)S(1)}, u32[]{:S(2)}, u32[]{:S(2)}) collective-permute-start(bf16[176,256]{1,0:T(8,128)(2,1)S(1)} %collective-permute-done.3.refs_2_), channel_id=1, source_target_pairs={{0,1},{1,0},{2,3},{3,2},{4,5},{5,4},{6,7},{7,6},{8,9},{9,8},{10,11... | collective-permute-start | bytes 270344 | tf_op jit(solution)/shard_map/ppermute | solution.py:563
  11.8 0.4 %shard_map.103 = (f32[8,32,256]{2,1,0:T(8,128)S(1)}, f32[128,256]{1,0:T(8,128)S(1)}, f32[3,32,512]{2,1,0:T(8,128)S(1)}, bf16[16,512]{1,0:T(8,128)(2,1)S(1)}, bf1...) custom-call(bf16[176,256]{1,0:T(8,128)(2,1)S(1)} %get-tuple-element., ...), custom_call_target="tpu_custom_call" | custom-call | flops 200000000 | bytes 1500000 | tf_op jit(solution)/shard_map/pallas_call | solution.py:593
  12.2 2.5 %collective-permute-done.1.refs_0_ = bf16[160,256]{1,0:T(8,128)(2,1)S(1)} collective-permute-done((bf16[160,256]{1,0:T(8,128)(2,1)S(1)}, bf16[160,256]{1,0:T(8,128)(2,1)S(1)}, u32[]{:S(2)}, u32[]{:S(2)}) %collective-permute-start.1) | collective-permute-done | bytes 81952 | tf_op jit(solution)/shard_map/ppermute | solution.py:563
  14.7 0.8 %collective-permute-start.2 = (bf16[160,256]{1,0:T(8,128)(2,1)S(1)}, bf16[160,256]{1,0:T(8,128)(2,1)S(1)}, u32[]{:S(2)}, u32[]{:S(2)}) collective-permute-start(bf16[160,256]{1,0:T(8,128)(2,1)S(1)} %collective-permute-done.1.refs_0_), channel_id=1, source_target_pairs={{0,1},{1,0},{2,3},{3,2},{4,5},{5,4},{6,7},{7,6},{8,9},{9,8},{10,11... | collective-permute-start | bytes 245768 | tf_op jit(solution)/shard_map/ppermute | solution.py:563
  15.5 0.5 %collective-permute-done.6.second = bf16[160,256]{1,0:T(8,128)(2,1)S(1)} collective-permute-done((bf16[160,256]{1,0:T(8,128)(2,1)S(1)}, bf16[160,256]{1,0:T(8,128)(2,1)S(1)}, u32[]{:S(2)}, u32[]{:S(2)}) %collective-permute-start.6) | collective-permute-done | bytes 81952 | tf_op jit(solution)/shard_map/ppermute | solution.py:563
  16.0 0.0 collective-permute-done.5.first.refs_0_
  16.0 0.0 collective-permute-done.7.third.refs_1_
  16.0 0.8 %shard_map.102 = (f32[5,144,256]{2,1,0:T(8,128)S(1)}, bf16[4,128,256]{2,1,0:T(8,128)(2,1)S(1)}) custom-call(bf16[176,256]{1,0:T(8,128)(2,1)S(1)} %get-tuple-element.40.sent, bf16[176,256]{1,0:T(8,128)(2,1)S(1)} %collective-permute-done.5.first.refs_0_, bf16[160,256]{1,0:T(8,128)(2,1)S(1)} %collective-permute-done.6.second, ...), custom_call_target="tpu_custom_call" | custom-call | flops 200000000 | bytes 1500000 | tf_op jit(solution)/shard_map/pallas_call | solution.py:613
  16.8 0.0 collective-permute-done.4.refs_2_.refs_3_
  16.8 2.9 %shard_map.104 = (f32[128,256]{1,0:T(8,128)S(1)}, bf16[4,64,256]{2,1,0:T(8,128)(2,1)S(1)}, f32[2,128,256]{2,1,0:T(8,128)S(1)}) custom-call(bf16[176,256]{1,0:T(8,128)(2,1)S(1)} %collective-permute-done.5.first.refs_0_, bf16[176,256]{1,0:T(8,128)(2,1)S(1)} %collective-permute-done.7.third.refs_1_, ...), custom_call_target="tpu_custom_call" | custom-call | flops 1000000000 | bytes 4000000 | tf_op jit(solution)/shard_map/pallas_call | solution.py:601
  19.7 0.0 collective-permute-done.2.refs_1_
  19.7 3.1 %shard_map.105 = bf16[4,32,256]{2,1,0:T(8,128)(2,1)} custom-call(bf16[160,256]{1,0:T(8,128)(2,1)S(1)} %collective-permute-done.1.refs_0_, bf16[160,256]{1,0:T(8,128)(2,1)S(1)} %collective-permute-done.2.refs_1_, bf16[176,256]{1,0:T(8,128)(2,1)S(1)} %collective-permute-done.3.refs_2_, bf16[176,256]{1,0:T(8,128)(2,1)S(1)} %collective-permute-done.4.refs_2_.refs_3_, ...), custom_call_target="tpu_custom_call" | custom-call | flops 1000000000 | bytes 4000000 | tf_op jit(solution)/shard_map/pallas_call | solution.py:643
  (1 shorter events, 0.0 us)
Async XLA Ops:
  0.0 1.8 %collective-permute-start = (bf16[4,32,256]{2,1,0:T(8,128)(2,1)}, bf16[4,32,256]{2,1,0:T(8,128)(2,1)S(1)}, u32[]{:S(2)}, u32[]{:S(2)}) collective-permute-start(bf16[4,32,256]{2,1,0:T(8,128)(2,1)} %feats.1), channel_id=1, source_target_pairs={{0,8},{8,0},{1,9},{9,1},{2,10},{10,2},{3,11},{11,3},{4,12},{12,4},... | collective-permute-start | bytes 196616 | tf_op jit(solution)/shard_map/ppermute | solution.py:541
  1.9 8.3 %collective-permute-start.3 = (bf16[176,256]{1,0:T(8,128)(2,1)S(1)}, bf16[176,256]{1,0:T(8,128)(2,1)S(1)}, u32[]{:S(2)}, u32[]{:S(2)}) collective-permute-start(bf16[176,256]{1,0:T(8,128)(2,1)S(1)} %get-tuple-element.40.sent), channel_id=1, source_target_pairs={{0,6},{1,7},{2,4},{3,5},{4,2},{5,3},{6,0},{7,1},{8,14},{9,15},{10,... | collective-permute-start | bytes 270344 | tf_op jit(solution)/shard_map/ppermute | solution.py:563
  6.6 9.3 %collective-permute-start.5 = (bf16[176,256]{1,0:T(8,128)(2,1)S(1)}, bf16[176,256]{1,0:T(8,128)(2,1)S(1)}, u32[]{:S(2)}, u32[]{:S(2)}) collective-permute-start(bf16[176,256]{1,0:T(8,128)(2,1)S(1)} %get-tuple-element.40.sent), channel_id=1, source_target_pairs={{0,1},{1,0},{2,3},{3,2},{4,5},{5,4},{6,7},{7,6},{8,9},{9,8},{10,11... | collective-permute-start | bytes 270344 | tf_op jit(solution)/shard_map/ppermute | solution.py:563
  8.2 7.8 %collective-permute-start.7 = (bf16[176,256]{1,0:T(8,128)(2,1)S(1)}, bf16[176,256]{1,0:T(8,128)(2,1)S(1)}, u32[]{:S(2)}, u32[]{:S(2)}) collective-permute-start(bf16[176,256]{1,0:T(8,128)(2,1)S(1)} %get-tuple-element.40.sent), channel_id=1, source_target_pairs={{0,3},{1,2},{2,1},{3,0},{4,7},{5,6},{6,5},{7,4},{8,11},{9,10},{10,... | collective-permute-start | bytes 270344 | tf_op jit(solution)/shard_map/ppermute | solution.py:563
  8.2 6.5 %collective-permute-start.1 = (bf16[160,256]{1,0:T(8,128)(2,1)S(1)}, bf16[160,256]{1,0:T(8,128)(2,1)S(1)}, u32[]{:S(2)}, u32[]{:S(2)}) collective-permute-start(bf16[160,256]{1,0:T(8,128)(2,1)S(1)} %get-tuple-element.39), channel_id=1, source_target_pairs={{0,4},{1,5},{2,6},{3,7},{4,0},{5,1},{6,2},{7,3},{8,12},{9,13},{10,... | collective-permute-start | bytes 245768 | tf_op jit(solution)/shard_map/ppermute | solution.py:563
  8.8 7.2 %collective-permute-start.6 = (bf16[160,256]{1,0:T(8,128)(2,1)S(1)}, bf16[160,256]{1,0:T(8,128)(2,1)S(1)}, u32[]{:S(2)}, u32[]{:S(2)}) collective-permute-start(bf16[160,256]{1,0:T(8,128)(2,1)S(1)} %get-tuple-element.39), channel_id=1, source_target_pairs={{0,2},{1,3},{2,0},{3,1},{4,6},{5,7},{6,4},{7,5},{8,10},{9,11},{10,... | collective-permute-start | bytes 245768 | tf_op jit(solution)/shard_map/ppermute | solution.py:563
  10.2 6.6 %collective-permute-start.4 = (bf16[176,256]{1,0:T(8,128)(2,1)S(1)}, bf16[176,256]{1,0:T(8,128)(2,1)S(1)}, u32[]{:S(2)}, u32[]{:S(2)}) collective-permute-start(bf16[176,256]{1,0:T(8,128)(2,1)S(1)} %collective-permute-done.3.refs_2_), channel_id=1, source_target_pairs={{0,1},{1,0},{2,3},{3,2},{4,5},{5,4},{6,7},{7,6},{8,9},{9,8},{10,11... | collective-permute-start | bytes 270344 | tf_op jit(solution)/shard_map/ppermute | solution.py:563
  14.7 5.0 %collective-permute-start.2 = (bf16[160,256]{1,0:T(8,128)(2,1)S(1)}, bf16[160,256]{1,0:T(8,128)(2,1)S(1)}, u32[]{:S(2)}, u32[]{:S(2)}) collective-permute-start(bf16[160,256]{1,0:T(8,128)(2,1)S(1)} %collective-permute-done.1.refs_0_), channel_id=1, source_target_pairs={{0,1},{1,0},{2,3},{3,2},{4,5},{5,4},{6,7},{7,6},{8,9},{9,8},{10,11... | collective-permute-start | bytes 245768 | tf_op jit(solution)/shard_map/ppermute | solution.py:563

commit v5 on v4

--- a/solution.py
+++ b/solution.py
@@ -69,19 +69,24 @@
         lax.fori_loop(0, count, lambda i, carry: (body(i), carry)[1], 0)
 
 
-def load(feats, w_in, conv_w, conv_b, w_proj, dt_bias, a_rate, d_skip, gain, w_out, *refs):
+def load(feats, sent, sems):
     lower = lax.axis_index("rows") == 1
-    sent, outs, sems = refs[0], refs[1:-1], refs[-1]
     copies = [
         pltpu.make_async_copy(
             feats.at[jnp.where(lower, i, 3 - i)], sent.at[pl.ds(TW * (i + 1), TW), :], sems.at[i]
         )
         for i in range(4)
     ]
-    weights = (w_in, conv_w, conv_b, w_proj, dt_bias, a_rate, d_skip, gain, w_out)
-    copies += [
-        pltpu.make_async_copy(source, target, sems.at[4 + i])
-        for i, (source, target) in enumerate(zip(weights, outs))
+    for copy in copies:
+        copy.start()
+    for copy in copies:
+        copy.wait()
+
+
+def load_weights(*refs):
+    sources, targets, sems = refs[:9], refs[9:18], refs[18]
+    copies = [
+        pltpu.make_async_copy(source, target, sems.at[i]) for i, (source, target) in enumerate(zip(sources, targets))
     ]
     for copy in copies:
         copy.start()
@@ -145,8 +150,9 @@
     return out
 
 
-def ahead(sent, far, w_in, w_proj, dt_bias, a_rate, *outs):
-    strip_pre, gate_out, triangle, spread_out, heads_out, select_out, same_out, walk_in, walk_out = outs[:9]
+def ahead(nb, sent, far, w_in, w_proj, dt_bias, a_rate, *refs):
+    arrived, outs = (refs[:1], refs[1:]) if nb == 8 else ((), refs)
+    strip_pre, gate_out, triangle, spread_out, heads_out, select_out, same_out, walk_in, walk_out, row_masks, pick = outs[:11]
     col = lax.axis_index("cols")
     w_x = w_in[:, :D]
     far_pre = dot(far[...], w_x).astype(bf16).astype(f32)
@@ -172,24 +178,28 @@
     same_head = walk_r % NH == walk_c % NH
     walk_in[...] = ones_where(same_head & (source < step) & (step <= time))
     walk_out[...] = ones_where(same_head & (time <= step) & (step < source))
-    if len(outs) == 9:
-        return
-    ordered, nearer_out, keep_out, pick, w_step, lanes = outs[9:]
-    turn = jnp.where(col < 4, 0, 4)
     tok_r, tok_c = iotas(128, 128)
     same_row = tok_r // TW == tok_c // TW
-    ordered[0] = ones_where(same_row & (tok_c > tok_r))
-    ordered[1] = ones_where(same_row & (tok_c < tok_r))
-    ordered[2] = ones_where(same_row)
+    row_masks[0] = ones_where(same_row & (tok_c <= tok_r))
+    row_masks[1] = ones_where(same_row & (tok_c >= tok_r))
+    pick[0:112, :] = jnp.zeros((112, D), bf16)
+    pick[112:128, :] = ones_where(iotas(NH, D)[1] // NH == iotas(NH, D)[0])
+    pick[128:240, :] = jnp.zeros((112, D), bf16)
+    if len(outs) == 11:
+        return
+    ordered, nearer_out, keep_out, w_step, lanes, arrived_pre = outs[11:]
+    for i, block in enumerate(arrived):
+        arrived_pre[i] = dot(block[0:160, :], w_x).astype(bf16).astype(f32).reshape(5, TW, D)
+    turn = jnp.where(col < 4, 0, 4)
+    ordered[:, 0:128] = ones_where(same_row & (tok_c > tok_r))
+    ordered[:, 128:256] = ones_where(same_row & (tok_c < tok_r))
+    ordered[:, 256:384] = ones_where(same_row)
     source, target = (tok_r // NH) ^ turn, (tok_c // NH) ^ turn
     nearer = ((source > target) & (source < col)) | ((source < target) & (source > col))
     nearer_out[...] = ones_where(nearer & (tok_r % NH == tok_c % NH))
     side, block = iotas(2 * TW, 256)
     block = (block // TW) ^ turn
     keep_out[...] = jnp.where(side < TW, jnp.where(block < col, 1.0, 0.0), jnp.where(block > col, 1.0, 0.0))
-    pick[0:112, :] = jnp.zeros((112, D), bf16)
-    pick[112:128, :] = ones_where(iotas(NH, D)[1] // NH == iotas(NH, D)[0])
-    pick[128:240, :] = jnp.zeros((112, D), bf16)
     w_step[...] = jnp.concatenate(
         [jnp.where((j ^ turn) < col, w_proj[0, 0:NH, :], w_proj[1, 0:NH, :]) for j in range(8)], axis=0
     )
@@ -206,8 +216,8 @@
 def local(nb, count, *refs):
     sides, refs = refs[:count], refs[count:]
     w_in, conv_w, conv_b, w_proj, dt_bias, a_rate, d_skip = refs[:7]
-    strip_pre, triangle, spread, heads, select, same_col, walk_in, walk_out = refs[7:15]
-    base_out, reads_out, edge_out, strip, shifted = refs[15:]
+    strip_pre, triangle, spread, heads, select, same_col, walk_in, walk_out, row_masks, pick = refs[7:17]
+    base_out, reads_out, edge_out, strip, shifted = refs[17:]
     row, col = lax.axis_index("rows"), lax.axis_index("cols")
     lower = row == 1
     w_x = w_in[:, :D]
@@ -238,24 +248,52 @@
 
     head_lane = ones_where(iotas(NH, 128)[1] % NH == iotas(NH, 128)[0])
     expand = ones_where(iotas(NH, D)[1] // NH == iotas(NH, D)[0])
-    tok_r, tok_c = iotas(128, 128)
-    same_row = tok_r // TW == tok_c // TW
-    upto = ones_where(same_row & (tok_c <= tok_r))
-    onward = ones_where(same_row & (tok_c >= tok_r))
-
+    k_in = jnp.where(lower, 2, 3)
+    k_out = jnp.where(lower, 3, 2)
+
+    def pick_row(ref, k):
+        return jnp.where(k == 2, ref[2:3, :], ref[3:4, :])
+
+    lane = lax.broadcasted_iota(jnp.int32, (1, 128), 1) // NH
+    head_rows = [dot_wide(pick_row(ref, k), head_lane) for ref in (dt_bias, a_rate) for k in (k_in, k_out)]
+
+    def dense_steps(tokens, k, first, bias):
+        result = dot_t(tokens, jnp.concatenate([w_proj[k, 0:NH, :]] * 8, axis=0))
+        raw = result[0:TW]
+        for s in range(first + 1, 8):
+            raw = jnp.where(lane == s, result[(s - first) * TW : (s - first + 1) * TW], raw)
+        return softplus(raw + bias)
+
+    steps_in = dense_steps(column_tokens, k_in, 0, head_rows[0])
+    steps_out = dense_steps(own, k_out, 4, head_rows[1])
+    gap = dot(jnp.concatenate(split(-steps_in * head_rows[2]), axis=0), walk_in[...])
+    gap_out = dot(jnp.concatenate(split(-steps_out * head_rows[3]), axis=0), walk_out[...])
+    gap = (gap[:TW] + gap[TW:]) + (gap_out[:TW] + gap_out[TW:])
+    decay = jnp.exp(gap)
+    write_in = dot_t(column_tokens, w_proj[k_in, NH : NH + NS, :]).astype(bf16)
+    write_out = dot_t(own, w_proj[k_out, NH : NH + NS, :]).astype(bf16)
+    read_in = dot_t(own, w_proj[k_in, NH + NS :, :]).astype(bf16)
+    read_out = dot_t(own, w_proj[k_out, NH + NS :, :]).astype(bf16)
+    scores_in = dot((dot_t(read_in, write_in) * same_col[...]).astype(bf16), select[...])
+    scores_out = dot((dot_t(read_out, write_out) * same_col[:, :128]).astype(bf16), select[128:, :])
+    vertical_weights = []
+    for t in range(4):
+        rows = slice(t * TW, (t + 1) * TW)
+        sum_in = scores_in[rows] * (steps_in * jnp.where(lane <= t + 4, 1.0, 0.0))
+        sum_out = scores_out[rows] * (steps_out * jnp.where(lane >= t + 4, 1.0, 0.0))
+        vertical_weights.append((sum_in + sum_out) * decay[:, t * 128 : (t + 1) * 128])
+    vertical_weights = jnp.concatenate(vertical_weights, axis=0).astype(bf16)
     projected = [dot_t(own, w_proj[k]) for k in range(2)]
     steps = [softplus(projected[k][:, :NH] + dt_bias[k : k + 1, :]) for k in range(2)]
     logs = [-steps[k] * a_rate[k : k + 1, :] for k in range(2)]
     write = [projected[k][:, NH : NH + NS].astype(bf16) for k in range(2)]
     read = [projected[k][:, NH + NS :].astype(bf16) for k in range(2)]
     reach = [dot(read[k], w_proj[k, NH : NH + NS, :]).astype(bf16) for k in range(2)]
-    from_edge = [
-        dot_wide(jnp.exp(wide_dot(mask, logs[k])), expand) for k, mask in enumerate((upto, onward))
-    ]
-    edge_out[0], edge_out[1] = from_edge
-    stacked = [part for k in range(2) for part in split(logs[k])] + [part for k in range(2) for part in split(steps[k])]
+    for k in range(2):
+        edge_out[k] = dot(jnp.exp(wide_dot(row_masks[k], logs[k])).astype(bf16), expand)
+    stacked = [part for k in range(2) for part in split(logs[k])] + [steps[k].astype(bf16) for k in range(2)]
     wide = dot(jnp.concatenate(stacked, axis=0), spread[...])
-    wide = [wide[i * 128 : (i + 1) * 128] for i in range(8)]
+    wide = [wide[i * 128 : (i + 1) * 128] for i in range(6)]
     later, sooner, equal = triangle[0], triangle[1], triangle[2]
     time_r, time_c = iotas(TW, TW)
     first, second = ones_where(time_c <= time_r), ones_where(time_c >= time_r)
@@ -269,7 +307,7 @@
         weights = jnp.zeros((TW, NH * TW), f32)
         for k, keep in enumerate(allowed):
             scores = dot_t(read[k][rows], jnp.concatenate([write[k][rows]] * NH, axis=0))
-            step_row = jnp.sum((wide[4 + 2 * k][rows] + wide[5 + 2 * k][rows]) * equal, axis=0, keepdims=True)
+            step_row = jnp.sum(wide[4 + k][rows] * equal, axis=0, keepdims=True)
             weights = weights + scores * step_row * keep
         weights = (weights * jnp.exp(gaps)).astype(bf16)
         values = own[rows]
@@ -281,48 +319,11 @@
         across.append(result)
     across = jnp.concatenate(across, axis=0)
 
-    k_in = jnp.where(lower, 2, 3)
-    k_out = jnp.where(lower, 3, 2)
-
-    def pick_row(ref, k):
-        return jnp.where(k == 2, ref[2:3, :], ref[3:4, :])
-
-    lane = lax.broadcasted_iota(jnp.int32, (1, 128), 1) // NH
-    head_rows = [dot_wide(pick_row(ref, k), head_lane) for ref in (dt_bias, a_rate) for k in (k_in, k_out)]
-
-    def dense_steps(tokens, k, first, bias):
-        result = dot_t(tokens, jnp.concatenate([w_proj[k, 0:NH, :]] * 8, axis=0))
-        raw = result[0:TW]
-        for s in range(first + 1, 8):
-            raw = jnp.where(lane == s, result[(s - first) * TW : (s - first + 1) * TW], raw)
-        return softplus(raw + bias)
-
-    steps_in = dense_steps(column_tokens, k_in, 0, head_rows[0])
-    steps_out = dense_steps(own, k_out, 4, head_rows[1])
-    gap = dot(jnp.concatenate(split(-steps_in * head_rows[2]), axis=0), walk_in[...])
-    gap_out = dot(jnp.concatenate(split(-steps_out * head_rows[3]), axis=0), walk_out[...])
-    gap = (gap[:TW] + gap[TW:]) + (gap_out[:TW] + gap_out[TW:])
-    decay = jnp.exp(gap)
-    write_in = dot_t(column_tokens, w_proj[k_in, NH : NH + NS, :]).astype(bf16)
-    write_out = dot_t(own, w_proj[k_out, NH : NH + NS, :]).astype(bf16)
-    read_in = dot_t(own, w_proj[k_in, NH + NS :, :]).astype(bf16)
-    read_out = dot_t(own, w_proj[k_out, NH + NS :, :]).astype(bf16)
-    scores_in = dot_wide(dot_t(read_in, write_in) * same_col[...], select[...])
-    scores_out = dot_wide(dot_t(read_out, write_out) * same_col[:, :128], select[128:, :])
-    weights = []
-    for t in range(4):
-        rows = slice(t * TW, (t + 1) * TW)
-        sum_in = scores_in[rows] * (steps_in * jnp.where(lane <= t + 4, 1.0, 0.0))
-        sum_out = scores_out[rows] * (steps_out * jnp.where(lane >= t + 4, 1.0, 0.0))
-        weights.append((sum_in + sum_out) * decay[:, t * 128 : (t + 1) * 128])
-    weights = jnp.concatenate(weights, axis=0).astype(bf16)
     skips = dot_wide(d_skip[...], expand)
     own_wide = own.astype(f32)
-    pick_r, pick_c = iotas(128, D)
-    pick_c = pick_c // NH
     vertical = (skips[2:3] + skips[3:4]) * own_wide
     for s in range(8):
-        factor = dot(weights, ones_where(pick_r == s * NH + pick_c))
+        factor = dot(vertical_weights, pick[112 - NH * s : 240 - NH * s, :])
         values = strip_mixed[s].astype(f32)
         vertical = vertical + factor * jnp.concatenate([values] * 4, axis=0)
     base_out[...] = across + (skips[0:1] + skips[1:2]) * own_wide + vertical.astype(bf16).astype(f32)
@@ -443,14 +444,17 @@
         out[jnp.where(lower, i, 3 - i)] = result[i * TW : (i + 1) * TW]
 
 
-def early(sent, first, second, third, w_in, conv_w, conv_b, pre, mixed, shifted):
+def early(strip_pre, first, second, third, w_in, conv_w, conv_b, pre, mixed, shifted):
     col = lax.axis_index("cols")
     lower = lax.axis_index("rows") == 1
     w_x = w_in[:, :D]
     pre[:, 0:8, :] = jnp.zeros((5, 8, D), f32)
     pre[:, 136:144, :] = jnp.zeros((5, 8, D), f32)
-    for step, block in enumerate((sent, first, second, third)):
+    for step, block in ((1, first), (2, second), (3, third)):
         place_rows(pre, block, w_x, (col & 3) ^ step)
+    base = pl.multiple_of((col & 3) * TW + 8, 8)
+    for q in range(5):
+        pre[q, pl.ds(base, TW), :] = strip_pre[3 + q]
     taps, bias = direction_taps(conv_w, lower), conv_b[...]
     for q in range(1, 5):
         for j, part in enumerate(filter_row(pre, 5, q, 128, shifted.at[q % 2], taps, bias)):
@@ -465,8 +469,9 @@
 
 
 def late(*refs):
-    blocks, (half_pre, half_mixed, base_in, reads_in, edge_in, gate_in), refs = refs[:4], refs[4:10], refs[10:]
-    ordered, nearer, keep, pick, w_step, lanes = refs[:6]
+    blocks, arrived_pre, refs = (refs[0], refs[1], refs[3]), refs[2], refs[4:]
+    (half_pre, half_mixed, base_in, reads_in, edge_in, gate_in), refs = refs[:6], refs[6:]
+    pick, ordered, nearer, keep, w_step, lanes = refs[:6]
     refs = refs[6:]
     w_in, conv_w, conv_b, _, _, _, gain, w_out, out = refs[:9]
     pre, mixed, attended, scaled, shifted = refs[9:]
@@ -476,8 +481,11 @@
     lower = row == 1
     on_left = col < 4
     w_x = w_in[:, :D]
-    for step, block in enumerate(blocks):
+    for step, block in zip((0, 1, 3), blocks):
         place_rows(pre, block, w_x, (col & 3) ^ step)
+    base = pl.multiple_of(((col & 3) ^ 2) * TW + 8, 8)
+    for q in range(5):
+        pre[q, pl.ds(base, TW), :] = arrived_pre[0, q]
     zero = jnp.zeros((1, D), f32)
     for q in range(5):
         pre[q, 7:8, :] = jnp.where(on_left, half_pre[q, 135:136, :], zero)
@@ -515,12 +523,12 @@
     left, right = lanes[2:3, :], lanes[3:4, :]
     steps = softplus(raw + lanes[0:1, :]) * (left + right)
     logs = -steps * lanes[1:2, :]
-    reach = dot_wide(wide_dot(ordered[2], logs), nearer[...])
-    reach = reach + wide_dot(ordered[0], logs * left) + wide_dot(ordered[1], logs * right)
+    stacked = jnp.concatenate([logs * left, logs * right, dot_wide(logs, nearer[...])], axis=0)
+    reach = wide_dot(ordered[...], stacked)
     weight = split(jnp.exp(reach) * steps)
     for j in range(8):
         mask = pick[112 - NH * j : 240 - NH * j, :]
-        factor = dot(weight[0], mask) + dot(weight[1], mask)
+        factor = dot(weight[0], mask)
         for q in range(4):
             cells = slice(TW * j, TW * (j + 1))
             scaled[q, cells, :] = (mixed[q, cells, :].astype(f32) * factor[q * TW : (q + 1) * TW]).astype(bf16)
@@ -540,14 +548,22 @@
 
     partner = lax.ppermute(feats, "rows", [(0, 1), (1, 0)])
     params = [w_in, conv_w, conv_b[None], jnp.swapaxes(w_proj, 1, 2), dt_bias, a_rate, d_skip, norm_gain[None], w_out]
-    loaded, *params = pl.pallas_call(
+    loaded = pl.pallas_call(
         load,
-        out_shape=(shape(HALO, D, dtype=bf16), *[shape(*part.shape, dtype=part.dtype) for part in params]),
-        in_specs=[hbm] * 10,
-        out_specs=(vmem,) * 10,
-        scratch_shapes=[pltpu.SemaphoreType.DMA((13,))],
+        out_shape=shape(HALO, D, dtype=bf16),
+        in_specs=[hbm],
+        out_specs=vmem,
+        scratch_shapes=[pltpu.SemaphoreType.DMA((4,))],
         compiler_params=limit(8),
-    )(*[pltpu.with_memory_space_constraint(part, pltpu.HBM) for part in (feats, *params)])
+    )(pltpu.with_memory_space_constraint(feats, pltpu.HBM))
+    params = pl.pallas_call(
+        load_weights,
+        out_shape=tuple(shape(*part.shape, dtype=part.dtype) for part in params),
+        in_specs=[hbm] * 9,
+        out_specs=(vmem,) * 9,
+        scratch_shapes=[pltpu.SemaphoreType.DMA((9,))],
+        compiler_params=limit(8),
+    )(*[pltpu.with_memory_space_constraint(part, pltpu.HBM) for part in params])
     w_in, conv_w, conv_b, w_proj, dt_bias, a_rate, d_skip, norm_gain, w_out = params
     sent, short, far = pl.pallas_call(
         pack,
@@ -580,33 +596,35 @@
         shape(128, 256),
         shape(128, 512, dtype=bf16),
         shape(128, 512, dtype=bf16),
+        shape(2, 128, 128, dtype=bf16),
+        shape(240, D, dtype=bf16),
     ]
     if direct:
         outs += [
-            shape(3, 128, 128, dtype=bf16),
+            shape(128, 384, dtype=bf16),
             shape(128, 128, dtype=bf16),
             shape(2 * TW, 256),
-            shape(240, D, dtype=bf16),
             shape(128, D, dtype=bf16),
             shape(8, 128),
+            shape(1, 5, TW, D),
         ]
     strip_pre, gate, *masks = pl.pallas_call(
-        ahead,
+        functools.partial(ahead, nb),
         out_shape=tuple(outs),
-        in_specs=[vmem] * 6,
+        in_specs=[vmem] * (7 if direct else 6),
         out_specs=(vmem,) * len(outs),
         compiler_params=limit(8),
         cost_estimate=pl.CostEstimate(flops=200_000_000, bytes_accessed=1_500_000, transcendentals=50_000),
-    )(sent, far, w_in, w_proj, dt_bias, a_rate)
+    )(sent, far, w_in, w_proj, dt_bias, a_rate, *((blocks[6],) if direct else ()))
     kept = pl.pallas_call(
         functools.partial(local, nb, len(sides)),
         out_shape=(shape(128, D), shape(4, 2 * TW, D, dtype=bf16), shape(2, 128, D)),
-        in_specs=[vmem] * (15 + len(sides)),
+        in_specs=[vmem] * (17 + len(sides)),
         out_specs=(vmem,) * 3,
         scratch_shapes=[pltpu.VMEM((8, 48, D), f32), pltpu.VMEM((2, 2, 48, D), f32)],
         compiler_params=limit(16 if direct else 32),
         cost_estimate=pl.CostEstimate(flops=1_000_000_000, bytes_accessed=4_000_000, transcendentals=1_000_000),
-    )(*sides, w_in, conv_w, conv_b, w_proj, dt_bias, a_rate, d_skip, strip_pre, *masks[:7])
+    )(*sides, w_in, conv_w, conv_b, w_proj, dt_bias, a_rate, d_skip, strip_pre, *masks[:9])
     kept = [*kept, gate]
     tail = [w_in, conv_w, conv_b, w_proj, dt_bias, a_rate, norm_gain, w_out]
     if direct:
@@ -618,8 +636,8 @@
             scratch_shapes=[pltpu.VMEM((2, 2, 144, D), f32)],
             compiler_params=limit(8),
             cost_estimate=pl.CostEstimate(flops=200_000_000, bytes_accessed=1_500_000, transcendentals=200_000),
-        )(*blocks[:4], w_in, conv_w, conv_b)
-        operands = [*blocks[4:], *half, *kept, *masks[7:], *tail]
+        )(strip_pre, *blocks[1:4], w_in, conv_w, conv_b)
+        operands = [*blocks[4:6], masks[-1], blocks[7], *half, *kept, *masks[8:-1], *tail]
         body = late
         scratch = [
             pltpu.VMEM((5, 144, D), f32),

time: 23 us -> 22.7 us (0.987)
  waiting for transfers between devices: 2.97 us -> 1.59 us
  starting transfers between devices: 11.3 us -> 12.1 us
    ppermute x7, waiting for transfers between devices: 2.97 us -> 1.29 us  [across(): return lax.ppermute(part, 'cols', [(i, i ^ step) for i in range(nb)])]
    ppermute x7, starting transfers between devices: 10.8 us -> 11.6 us  [across(): return lax.ppermute(part, 'cols', [(i, i ^ step) for i in range(nb)])]
    pallas_call x2 -> x3, Pallas kernels: 1.68 us -> 2.45 us  [the longest x1 1.25 us: shards(): pl.pallas_call(load_weights, out_shape=tuple((shape(*part.shape, dtype=pa...]
    pallas_call x1, Pallas kernels: 3.09 us -> 2.71 us  [shards(): pl.pallas_call(body, out_shape=shape(TH, TW, D, dtype=bf16), in_specs=[vm...]
    ppermute x1, waiting for transfers between devices: 0.01 us -> 0.3 us  [shards(): partner = lax.ppermute(feats, 'rows', [(0, 1), (1, 0)])]
    pallas_call x1, Pallas kernels: 2.92 us -> 2.62 us  [shards(): pl.pallas_call(functools.partial(local, nb, len(sides)), out_shape=(shape...]
  transfers between devices with their start and end apart: 8 -> 8, of which waited for: 2 -> 3; matrix products, arithmetic and copies ran while one was open for 0% -> 0% of each run, Pallas kernels for 24% -> 26%
where the time goes in v5:
time: 22.7 us; the launch traced here: 22.4 us
  starting transfers between devices  12.1 us (53%)
  Pallas kernels  8.6 us (38%)
  waiting for transfers between devices  1.59 us (7%)
    ppermute x7, starting transfers between devices, across(): return lax.ppermute(part, 'cols', [(i, i ^ step) for i in range(nb)])  11.6 us
    pallas_call x1, Pallas kernels, shards(): pl.pallas_call(body, out_shape=shape(TH, TW, D, dtype=bf16), in_specs=[vm...  2.71 us
    pallas_call x1, Pallas kernels, shards(): pl.pallas_call(functools.partial(local, nb, len(sides)), out_shape=(shape...  2.62 us
    ppermute x7, waiting for transfers between devices, across(): return lax.ppermute(part, 'cols', [(i, i ^ step) for i in range(nb)])  1.29 us
    pallas_call x1, Pallas kernels, shards(): pl.pallas_call(load_weights, out_shape=tuple((shape(*part.shape, dtype=pa...  1.25 us
    pallas_call x1, Pallas kernels, shards(): pl.pallas_call(load, out_shape=shape(HALO, D, dtype=bf16), in_specs=[hbm]...  0.8 us
    pallas_call x1, Pallas kernels, shards(): pl.pallas_call(early, out_shape=(shape(5, 144, D), shape(4, 128, D, dtype...  0.79 us
    ppermute x1, starting transfers between devices, shards(): partner = lax.ppermute(feats, 'rows', [(0, 1), (1, 0)])  0.49 us
  transfers between devices with their start and end apart: 8, of which 3 were waited for; matrix products, arithmetic and copies ran while one was open for 0% of the time, Pallas kernels for 26%

profile of v5, /device:TPU:0, one launch (start us, length us, event | category | flops | bytes accessed | tf_op | source)
XLA Modules:
  0.0 22.4 jit_solution(16215810349488781842)
XLA Ops:
  0.0 0.5 %collective-permute-start = (bf16[4,32,256]{2,1,0:T(8,128)(2,1)}, bf16[4,32,256]{2,1,0:T(8,128)(2,1)S(1)}, u32[]{:S(2)}, u32[]{:S(2)}) collective-permute-start(bf16[4,32,256]{2,1,0:T(8,128)(2,1)} %feats.1), channel_id=1, source_target_pairs={{0,8},{8,0},{1,9},{9,1},{2,10},{10,2},{3,11},{11,3},{4,12},{12,4},... | collective-permute-start | bytes 196616 | tf_op jit(solution)/shard_map/ppermute | solution.py:549
  0.5 0.8 %shard_map.100.loaded = bf16[176,256]{1,0:T(8,128)(2,1)S(1)} custom-call(bf16[4,32,256]{2,1,0:T(8,128)(2,1)} %feats.1), custom_call_target="tpu_custom_call" | custom-call | tf_op jit(solution)/shard_map/pallas_call | solution.py:551
  1.3 0.3 %collective-permute-done.partner = bf16[4,32,256]{2,1,0:T(8,128)(2,1)S(1)} collective-permute-done((bf16[4,32,256]{2,1,0:T(8,128)(2,1)}, bf16[4,32,256]{2,1,0:T(8,128)(2,1)S(1)}, u32[]{:S(2)}, u32[]{:S(2)}) %collective-permute-start) | collective-permute-done | bytes 65568 | tf_op jit(solution)/shard_map/ppermute | solution.py:549
  1.6 5.0 %collective-permute-start.3 = (bf16[176,256]{1,0:T(8,128)(2,1)S(1)}, bf16[176,256]{1,0:T(8,128)(2,1)S(1)}, u32[]{:S(2)}, u32[]{:S(2)}) collective-permute-start(bf16[176,256]{1,0:T(8,128)(2,1)S(1)} %get-tuple-element.40.sent), channel_id=1, source_target_pairs={{0,6},{1,7},{2,4},{3,5},{4,2},{5,3},{6,0},{7,1},{8,14},{9,15},{10,... | collective-permute-start | bytes 270344 | tf_op jit(solution)/shard_map/ppermute | solution.py:579
  6.6 0.0 collective-permute-start.1
  6.6 1.5 %collective-permute-start.5 = (bf16[176,256]{1,0:T(8,128)(2,1)S(1)}, bf16[176,256]{1,0:T(8,128)(2,1)S(1)}, u32[]{:S(2)}, u32[]{:S(2)}) collective-permute-start(bf16[176,256]{1,0:T(8,128)(2,1)S(1)} %get-tuple-element.40.sent), channel_id=1, source_target_pairs={{0,1},{1,0},{2,3},{3,2},{4,5},{5,4},{6,7},{7,6},{8,9},{9,8},{10,11... | collective-permute-start | bytes 270344 | tf_op jit(solution)/shard_map/ppermute | solution.py:579
  8.2 0.6 %collective-permute-start.7 = (bf16[176,256]{1,0:T(8,128)(2,1)S(1)}, bf16[176,256]{1,0:T(8,128)(2,1)S(1)}, u32[]{:S(2)}, u32[]{:S(2)}) collective-permute-start(bf16[176,256]{1,0:T(8,128)(2,1)S(1)} %get-tuple-element.40.sent), channel_id=1, source_target_pairs={{0,3},{1,2},{2,1},{3,0},{4,7},{5,6},{6,5},{7,4},{8,11},{9,10},{10,... | collective-permute-start | bytes 270344 | tf_op jit(solution)/shard_map/ppermute | solution.py:579
  8.8 1.4 %collective-permute-start.6 = (bf16[160,256]{1,0:T(8,128)(2,1)S(1)}, bf16[160,256]{1,0:T(8,128)(2,1)S(1)}, u32[]{:S(2)}, u32[]{:S(2)}) collective-permute-start(bf16[160,256]{1,0:T(8,128)(2,1)S(1)} %get-tuple-element.39), channel_id=1, source_target_pairs={{0,2},{1,3},{2,0},{3,1},{4,6},{5,7},{6,4},{7,5},{8,10},{9,11},{10,... | collective-permute-start | bytes 245768 | tf_op jit(solution)/shard_map/ppermute | solution.py:579
  10.1 0.1 collective-permute-done.3.refs_0_
  10.2 1.6 %collective-permute-start.4 = (bf16[176,256]{1,0:T(8,128)(2,1)S(1)}, bf16[176,256]{1,0:T(8,128)(2,1)S(1)}, u32[]{:S(2)}, u32[]{:S(2)}) collective-permute-start(bf16[176,256]{1,0:T(8,128)(2,1)S(1)} %collective-permute-done.3.refs_0_), channel_id=1, source_target_pairs={{0,1},{1,0},{2,3},{3,2},{4,5},{5,4},{6,7},{7,6},{8,9},{9,8},{10,11... | collective-permute-start | bytes 270344 | tf_op jit(solution)/shard_map/ppermute | solution.py:579
  11.8 1.2 %shard_map.102 = (bf16[256,512]{1,0:T(8,128)(2,1)S(1)}, f32[9,256]{1,0:T(8,128)S(1)}, f32[1,256]{1,0:T(1,128)S(1)}, bf16[4,144,256]{2,1,0:T(8,128)(2,1)S(1)}, f3...) custom-call(bf16[256,512]{1,0:T(8,128)(2,1)} %refs_0_.1, ...), custom_call_target="tpu_custom_call" | custom-call | tf_op jit(solution)/shard_map/pallas_call | solution.py:559
  13.1 1.2 %collective-permute-done.1.refs_0_ = bf16[160,256]{1,0:T(8,128)(2,1)S(1)} collective-permute-done((bf16[160,256]{1,0:T(8,128)(2,1)S(1)}, bf16[160,256]{1,0:T(8,128)(2,1)S(1)}, u32[]{:S(2)}, u32[]{:S(2)}) %collective-permute-start.1) | collective-permute-done | bytes 81952 | tf_op jit(solution)/shard_map/ppermute | solution.py:579
  14.3 1.5 %collective-permute-start.2 = (bf16[160,256]{1,0:T(8,128)(2,1)S(1)}, bf16[160,256]{1,0:T(8,128)(2,1)S(1)}, u32[]{:S(2)}, u32[]{:S(2)}) collective-permute-start(bf16[160,256]{1,0:T(8,128)(2,1)S(1)} %collective-permute-done.1.refs_0_), channel_id=1, source_target_pairs={{0,1},{1,0},{2,3},{3,2},{4,5},{5,4},{6,7},{7,6},{8,9},{9,8},{10,11... | collective-permute-start | bytes 245768 | tf_op jit(solution)/shard_map/ppermute | solution.py:579
  15.8 0.4 %shard_map.103 = (f32[8,32,256]{2,1,0:T(8,128)S(1)}, f32[128,256]{1,0:T(8,128)S(1)}, f32[3,32,512]{2,1,0:T(8,128)S(1)}, bf16[16,512]{1,0:T(8,128)(2,1)S(1)}, bf1...) custom-call(bf16[176,256]{1,0:T(8,128)(2,1)S(1)} %get-tuple-element., ...), custom_call_target="tpu_custom_call" | custom-call | flops 200000000 | bytes 1500000 | tf_op jit(solution)/shard_map/pallas_call | solution.py:611
  16.2 0.0 collective-permute-done.6.second
  16.2 0.0 collective-permute-done.5.first.refs_0_
  16.2 0.0 collective-permute-done.7.third.refs_1_
  16.2 0.8 %shard_map.104 = (f32[5,144,256]{2,1,0:T(8,128)S(1)}, bf16[4,128,256]{2,1,0:T(8,128)(2,1)S(1)}) custom-call(f32[8,32,256]{2,1,0:T(8,128)S(1)} %get-tuple-element.47.strip_pre.refs_10_, bf16[176,256]{1,0:T(8,128)(2,1)S(1)} %collective-permute-done.5.first.refs_0_, bf16[160,256]{1,0:T(8,128)(2,1)S(1)} %collective-permute-done.6.second, ...), custom_call_target="tpu_custom_call" | custom-call | flops 200000000 | bytes 1500000 | tf_op jit(solution)/shard_map/pallas_call | solution.py:631
  17.0 0.0 collective-permute-done.4.refs_2_.refs_3_
  17.0 2.6 %shard_map.105 = (f32[128,256]{1,0:T(8,128)S(1)}, bf16[4,64,256]{2,1,0:T(8,128)(2,1)S(1)}, f32[2,128,256]{2,1,0:T(8,128)S(1)}) custom-call(bf16[176,256]{1,0:T(8,128)(2,1)S(1)} %collective-permute-done.5.first.refs_0_, bf16[176,256]{1,0:T(8,128)(2,1)S(1)} %collective-permute-done.7.third.refs_1_, ...), custom_call_target="tpu_custom_call" | custom-call | flops 1000000000 | bytes 4000000 | tf_op jit(solution)/shard_map/pallas_call | solution.py:619
  19.7 0.0 collective-permute-done.2.refs_1_
  19.7 2.7 %shard_map.106 = bf16[4,32,256]{2,1,0:T(8,128)(2,1)} custom-call(bf16[160,256]{1,0:T(8,128)(2,1)S(1)} %collective-permute-done.1.refs_0_, bf16[160,256]{1,0:T(8,128)(2,1)S(1)} %collective-permute-done.2.refs_1_, f32[1,5,32,256]{3,2,1,0:T(8,128)S(1)} %get-tuple-element.46.refs_2_, bf16[176,256]{1,0:T(8,128)(2,1)S(1)} %collective-permute-done.4.refs_2_.refs_3_, ...), custom_call_target="tpu_custom_call" | custom-call | flops 1000000000 | bytes 4000000 | tf_op jit(solution)/shard_map/pallas_call | solution.py:661
  (1 shorter events, 0.0 us)
Async XLA Ops:
  0.0 1.6 %collective-permute-start = (bf16[4,32,256]{2,1,0:T(8,128)(2,1)}, bf16[4,32,256]{2,1,0:T(8,128)(2,1)S(1)}, u32[]{:S(2)}, u32[]{:S(2)}) collective-permute-start(bf16[4,32,256]{2,1,0:T(8,128)(2,1)} %feats.1), channel_id=1, source_target_pairs={{0,8},{8,0},{1,9},{9,1},{2,10},{10,2},{3,11},{11,3},{4,12},{12,4},... | collective-permute-start | bytes 196616 | tf_op jit(solution)/shard_map/ppermute | solution.py:549
  1.6 8.6 %collective-permute-start.3 = (bf16[176,256]{1,0:T(8,128)(2,1)S(1)}, bf16[176,256]{1,0:T(8,128)(2,1)S(1)}, u32[]{:S(2)}, u32[]{:S(2)}) collective-permute-start(bf16[176,256]{1,0:T(8,128)(2,1)S(1)} %get-tuple-element.40.sent), channel_id=1, source_target_pairs={{0,6},{1,7},{2,4},{3,5},{4,2},{5,3},{6,0},{7,1},{8,14},{9,15},{10,... | collective-permute-start | bytes 270344 | tf_op jit(solution)/shard_map/ppermute | solution.py:579
  6.6 7.6 %collective-permute-start.1 = (bf16[160,256]{1,0:T(8,128)(2,1)S(1)}, bf16[160,256]{1,0:T(8,128)(2,1)S(1)}, u32[]{:S(2)}, u32[]{:S(2)}) collective-permute-start(bf16[160,256]{1,0:T(8,128)(2,1)S(1)} %get-tuple-element.39), channel_id=1, source_target_pairs={{0,4},{1,5},{2,6},{3,7},{4,0},{5,1},{6,2},{7,3},{8,12},{9,13},{10,... | collective-permute-start | bytes 245768 | tf_op jit(solution)/shard_map/ppermute | solution.py:579
  6.6 9.6 %collective-permute-start.5 = (bf16[176,256]{1,0:T(8,128)(2,1)S(1)}, bf16[176,256]{1,0:T(8,128)(2,1)S(1)}, u32[]{:S(2)}, u32[]{:S(2)}) collective-permute-start(bf16[176,256]{1,0:T(8,128)(2,1)S(1)} %get-tuple-element.40.sent), channel_id=1, source_target_pairs={{0,1},{1,0},{2,3},{3,2},{4,5},{5,4},{6,7},{7,6},{8,9},{9,8},{10,11... | collective-permute-start | bytes 270344 | tf_op jit(solution)/shard_map/ppermute | solution.py:579
  8.2 8.0 %collective-permute-start.7 = (bf16[176,256]{1,0:T(8,128)(2,1)S(1)}, bf16[176,256]{1,0:T(8,128)(2,1)S(1)}, u32[]{:S(2)}, u32[]{:S(2)}) collective-permute-start(bf16[176,256]{1,0:T(8,128)(2,1)S(1)} %get-tuple-element.40.sent), channel_id=1, source_target_pairs={{0,3},{1,2},{2,1},{3,0},{4,7},{5,6},{6,5},{7,4},{8,11},{9,10},{10,... | collective-permute-start | bytes 270344 | tf_op jit(solution)/shard_map/ppermute | solution.py:579
  8.8 7.5 %collective-permute-start.6 = (bf16[160,256]{1,0:T(8,128)(2,1)S(1)}, bf16[160,256]{1,0:T(8,128)(2,1)S(1)}, u32[]{:S(2)}, u32[]{:S(2)}) collective-permute-start(bf16[160,256]{1,0:T(8,128)(2,1)S(1)} %get-tuple-element.39), channel_id=1, source_target_pairs={{0,2},{1,3},{2,0},{3,1},{4,6},{5,7},{6,4},{7,5},{8,10},{9,11},{10,... | collective-permute-start | bytes 245768 | tf_op jit(solution)/shard_map/ppermute | solution.py:579
  10.2 6.8 %collective-permute-start.4 = (bf16[176,256]{1,0:T(8,128)(2,1)S(1)}, bf16[176,256]{1,0:T(8,128)(2,1)S(1)}, u32[]{:S(2)}, u32[]{:S(2)}) collective-permute-start(bf16[176,256]{1,0:T(8,128)(2,1)S(1)} %collective-permute-done.3.refs_0_), channel_id=1, source_target_pairs={{0,1},{1,0},{2,3},{3,2},{4,5},{5,4},{6,7},{7,6},{8,9},{9,8},{10,11... | collective-permute-start | bytes 270344 | tf_op jit(solution)/shard_map/ppermute | solution.py:579
  14.3 5.4 %collective-permute-start.2 = (bf16[160,256]{1,0:T(8,128)(2,1)S(1)}, bf16[160,256]{1,0:T(8,128)(2,1)S(1)}, u32[]{:S(2)}, u32[]{:S(2)}) collective-permute-start(bf16[160,256]{1,0:T(8,128)(2,1)S(1)} %collective-permute-done.1.refs_0_), channel_id=1, source_target_pairs={{0,1},{1,0},{2,3},{3,2},{4,5},{5,4},{6,7},{7,6},{8,9},{9,8},{10,11... | collective-permute-start | bytes 245768 | tf_op jit(solution)/shard_map/ppermute | solution.py:579

commit v6 on v5

--- a/solution.py
+++ b/solution.py
@@ -295,6 +295,7 @@
     wide = dot(jnp.concatenate(stacked, axis=0), spread[...])
     wide = [wide[i * 128 : (i + 1) * 128] for i in range(6)]
     later, sooner, equal = triangle[0], triangle[1], triangle[2]
+    masks = (later.astype(bf16), sooner.astype(bf16))
     time_r, time_c = iotas(TW, TW)
     first, second = ones_where(time_c <= time_r), ones_where(time_c >= time_r)
     walk = jnp.concatenate([first, first, second, second], axis=1)
@@ -302,7 +303,7 @@
     across = []
     for q in range(4):
         rows = slice(q * TW, (q + 1) * TW)
-        parts = [(wide[i][rows] * (later if i < 2 else sooner)).astype(bf16) for i in range(4)]
+        parts = [wide[i][rows].astype(bf16) * masks[i // 2] for i in range(4)]
         gaps = dot(walk, jnp.concatenate(parts, axis=0))
         weights = jnp.zeros((TW, NH * TW), f32)
         for k, keep in enumerate(allowed):
@@ -528,10 +529,10 @@
     weight = split(jnp.exp(reach) * steps)
     for j in range(8):
         mask = pick[112 - NH * j : 240 - NH * j, :]
-        factor = dot(weight[0], mask)
+        factor = dot(weight[0], mask).astype(bf16)
         for q in range(4):
             cells = slice(TW * j, TW * (j + 1))
-            scaled[q, cells, :] = (mixed[q, cells, :].astype(f32) * factor[q * TW : (q + 1) * TW]).astype(bf16)
+            scaled[q, cells, :] = mixed[q, cells, :] * factor[q * TW : (q + 1) * TW]
     finish(lower, attended, 1, scaled, base_in, gate_in, edge_in, gain, w_out, out)
 
 

time: 22.7 us -> 22.7 us (level)
  no operation moved by 1% of the time
where the time goes in v6:
time: 22.7 us; the launch traced here: 22.4 us
  starting transfers between devices  12.1 us (53%)
  Pallas kernels  8.6 us (38%)
  waiting for transfers between devices  1.59 us (7%)
    ppermute x7, starting transfers between devices, across(): return lax.ppermute(part, 'cols', [(i, i ^ step) for i in range(nb)])  11.6 us
    pallas_call x1, Pallas kernels, shards(): pl.pallas_call(body, out_shape=shape(TH, TW, D, dtype=bf16), in_specs=[vm...  2.71 us
    pallas_call x1, Pallas kernels, shards(): pl.pallas_call(functools.partial(local, nb, len(sides)), out_shape=(shape...  2.62 us
    ppermute x7, waiting for transfers between devices, across(): return lax.ppermute(part, 'cols', [(i, i ^ step) for i in range(nb)])  1.29 us
    pallas_call x1, Pallas kernels, shards(): pl.pallas_call(load_weights, out_shape=tuple((shape(*part.shape, dtype=pa...  1.25 us
    pallas_call x1, Pallas kernels, shards(): pl.pallas_call(load, out_shape=shape(HALO, D, dtype=bf16), in_specs=[hbm]...  0.8 us
    pallas_call x1, Pallas kernels, shards(): pl.pallas_call(early, out_shape=(shape(5, 144, D), shape(4, 128, D, dtype...  0.79 us
    ppermute x1, starting transfers between devices, shards(): partner = lax.ppermute(feats, 'rows', [(0, 1), (1, 0)])  0.49 us
  transfers between devices with their start and end apart: 8, of which 3 were waited for; matrix products, arithmetic and copies ran while one was open for 0% of the time, Pallas kernels for 26%

profile of v6, /device:TPU:0, one launch (start us, length us, event | category | flops | bytes accessed | tf_op | source)
XLA Modules:
  0.0 22.4 jit_solution(18352582217497383056)
XLA Ops:
  0.0 0.5 %collective-permute-start = (bf16[4,32,256]{2,1,0:T(8,128)(2,1)}, bf16[4,32,256]{2,1,0:T(8,128)(2,1)S(1)}, u32[]{:S(2)}, u32[]{:S(2)}) collective-permute-start(bf16[4,32,256]{2,1,0:T(8,128)(2,1)} %feats.1), channel_id=1, source_target_pairs={{0,8},{8,0},{1,9},{9,1},{2,10},{10,2},{3,11},{11,3},{4,12},{12,4},... | collective-permute-start | bytes 196616 | tf_op jit(solution)/shard_map/ppermute | solution.py:550
  0.5 0.8 %shard_map.100.loaded = bf16[176,256]{1,0:T(8,128)(2,1)S(1)} custom-call(bf16[4,32,256]{2,1,0:T(8,128)(2,1)} %feats.1), custom_call_target="tpu_custom_call" | custom-call | tf_op jit(solution)/shard_map/pallas_call | solution.py:552
  1.3 0.3 %collective-permute-done.partner = bf16[4,32,256]{2,1,0:T(8,128)(2,1)S(1)} collective-permute-done((bf16[4,32,256]{2,1,0:T(8,128)(2,1)}, bf16[4,32,256]{2,1,0:T(8,128)(2,1)S(1)}, u32[]{:S(2)}, u32[]{:S(2)}) %collective-permute-start) | collective-permute-done | bytes 65568 | tf_op jit(solution)/shard_map/ppermute | solution.py:550
  1.6 5.0 %collective-permute-start.3 = (bf16[176,256]{1,0:T(8,128)(2,1)S(1)}, bf16[176,256]{1,0:T(8,128)(2,1)S(1)}, u32[]{:S(2)}, u32[]{:S(2)}) collective-permute-start(bf16[176,256]{1,0:T(8,128)(2,1)S(1)} %get-tuple-element.40.sent), channel_id=1, source_target_pairs={{0,6},{1,7},{2,4},{3,5},{4,2},{5,3},{6,0},{7,1},{8,14},{9,15},{10,... | collective-permute-start | bytes 270344 | tf_op jit(solution)/shard_map/ppermute | solution.py:580
  6.6 0.0 collective-permute-start.1
  6.6 1.5 %collective-permute-start.5 = (bf16[176,256]{1,0:T(8,128)(2,1)S(1)}, bf16[176,256]{1,0:T(8,128)(2,1)S(1)}, u32[]{:S(2)}, u32[]{:S(2)}) collective-permute-start(bf16[176,256]{1,0:T(8,128)(2,1)S(1)} %get-tuple-element.40.sent), channel_id=1, source_target_pairs={{0,1},{1,0},{2,3},{3,2},{4,5},{5,4},{6,7},{7,6},{8,9},{9,8},{10,11... | collective-permute-start | bytes 270344 | tf_op jit(solution)/shard_map/ppermute | solution.py:580
  8.2 0.6 %collective-permute-start.7 = (bf16[176,256]{1,0:T(8,128)(2,1)S(1)}, bf16[176,256]{1,0:T(8,128)(2,1)S(1)}, u32[]{:S(2)}, u32[]{:S(2)}) collective-permute-start(bf16[176,256]{1,0:T(8,128)(2,1)S(1)} %get-tuple-element.40.sent), channel_id=1, source_target_pairs={{0,3},{1,2},{2,1},{3,0},{4,7},{5,6},{6,5},{7,4},{8,11},{9,10},{10,... | collective-permute-start | bytes 270344 | tf_op jit(solution)/shard_map/ppermute | solution.py:580
  8.8 1.4 %collective-permute-start.6 = (bf16[160,256]{1,0:T(8,128)(2,1)S(1)}, bf16[160,256]{1,0:T(8,128)(2,1)S(1)}, u32[]{:S(2)}, u32[]{:S(2)}) collective-permute-start(bf16[160,256]{1,0:T(8,128)(2,1)S(1)} %get-tuple-element.39), channel_id=1, source_target_pairs={{0,2},{1,3},{2,0},{3,1},{4,6},{5,7},{6,4},{7,5},{8,10},{9,11},{10,... | collective-permute-start | bytes 245768 | tf_op jit(solution)/shard_map/ppermute | solution.py:580
  10.1 0.1 collective-permute-done.3.refs_0_
  10.2 1.6 %collective-permute-start.4 = (bf16[176,256]{1,0:T(8,128)(2,1)S(1)}, bf16[176,256]{1,0:T(8,128)(2,1)S(1)}, u32[]{:S(2)}, u32[]{:S(2)}) collective-permute-start(bf16[176,256]{1,0:T(8,128)(2,1)S(1)} %collective-permute-done.3.refs_0_), channel_id=1, source_target_pairs={{0,1},{1,0},{2,3},{3,2},{4,5},{5,4},{6,7},{7,6},{8,9},{9,8},{10,11... | collective-permute-start | bytes 270344 | tf_op jit(solution)/shard_map/ppermute | solution.py:580
  11.8 1.2 %shard_map.102 = (bf16[256,512]{1,0:T(8,128)(2,1)S(1)}, f32[9,256]{1,0:T(8,128)S(1)}, f32[1,256]{1,0:T(1,128)S(1)}, bf16[4,144,256]{2,1,0:T(8,128)(2,1)S(1)}, f3...) custom-call(bf16[256,512]{1,0:T(8,128)(2,1)} %refs_0_.1, ...), custom_call_target="tpu_custom_call" | custom-call | tf_op jit(solution)/shard_map/pallas_call | solution.py:560
  13.1 1.2 %collective-permute-done.1.refs_0_ = bf16[160,256]{1,0:T(8,128)(2,1)S(1)} collective-permute-done((bf16[160,256]{1,0:T(8,128)(2,1)S(1)}, bf16[160,256]{1,0:T(8,128)(2,1)S(1)}, u32[]{:S(2)}, u32[]{:S(2)}) %collective-permute-start.1) | collective-permute-done | bytes 81952 | tf_op jit(solution)/shard_map/ppermute | solution.py:580
  14.3 1.5 %collective-permute-start.2 = (bf16[160,256]{1,0:T(8,128)(2,1)S(1)}, bf16[160,256]{1,0:T(8,128)(2,1)S(1)}, u32[]{:S(2)}, u32[]{:S(2)}) collective-permute-start(bf16[160,256]{1,0:T(8,128)(2,1)S(1)} %collective-permute-done.1.refs_0_), channel_id=1, source_target_pairs={{0,1},{1,0},{2,3},{3,2},{4,5},{5,4},{6,7},{7,6},{8,9},{9,8},{10,11... | collective-permute-start | bytes 245768 | tf_op jit(solution)/shard_map/ppermute | solution.py:580
  15.8 0.4 %shard_map.103 = (f32[8,32,256]{2,1,0:T(8,128)S(1)}, f32[128,256]{1,0:T(8,128)S(1)}, f32[3,32,512]{2,1,0:T(8,128)S(1)}, bf16[16,512]{1,0:T(8,128)(2,1)S(1)}, bf1...) custom-call(bf16[176,256]{1,0:T(8,128)(2,1)S(1)} %get-tuple-element., ...), custom_call_target="tpu_custom_call" | custom-call | flops 200000000 | bytes 1500000 | tf_op jit(solution)/shard_map/pallas_call | solution.py:612
  16.2 0.0 collective-permute-done.6.second
  16.2 0.0 collective-permute-done.5.first.refs_0_
  16.2 0.0 collective-permute-done.7.third.refs_1_
  16.2 0.8 %shard_map.104 = (f32[5,144,256]{2,1,0:T(8,128)S(1)}, bf16[4,128,256]{2,1,0:T(8,128)(2,1)S(1)}) custom-call(f32[8,32,256]{2,1,0:T(8,128)S(1)} %get-tuple-element.47.strip_pre.refs_10_, bf16[176,256]{1,0:T(8,128)(2,1)S(1)} %collective-permute-done.5.first.refs_0_, bf16[160,256]{1,0:T(8,128)(2,1)S(1)} %collective-permute-done.6.second, ...), custom_call_target="tpu_custom_call" | custom-call | flops 200000000 | bytes 1500000 | tf_op jit(solution)/shard_map/pallas_call | solution.py:632
  17.0 0.0 collective-permute-done.4.refs_2_.refs_3_
  17.0 2.6 %shard_map.105 = (f32[128,256]{1,0:T(8,128)S(1)}, bf16[4,64,256]{2,1,0:T(8,128)(2,1)S(1)}, f32[2,128,256]{2,1,0:T(8,128)S(1)}) custom-call(bf16[176,256]{1,0:T(8,128)(2,1)S(1)} %collective-permute-done.5.first.refs_0_, bf16[176,256]{1,0:T(8,128)(2,1)S(1)} %collective-permute-done.7.third.refs_1_, ...), custom_call_target="tpu_custom_call" | custom-call | flops 1000000000 | bytes 4000000 | tf_op jit(solution)/shard_map/pallas_call | solution.py:620
  19.7 0.0 collective-permute-done.2.refs_1_
  19.7 2.7 %shard_map.106 = bf16[4,32,256]{2,1,0:T(8,128)(2,1)} custom-call(bf16[160,256]{1,0:T(8,128)(2,1)S(1)} %collective-permute-done.1.refs_0_, bf16[160,256]{1,0:T(8,128)(2,1)S(1)} %collective-permute-done.2.refs_1_, f32[1,5,32,256]{3,2,1,0:T(8,128)S(1)} %get-tuple-element.46.refs_2_, bf16[176,256]{1,0:T(8,128)(2,1)S(1)} %collective-permute-done.4.refs_2_.refs_3_, ...), custom_call_target="tpu_custom_call" | custom-call | flops 1000000000 | bytes 4000000 | tf_op jit(solution)/shard_map/pallas_call | solution.py:662
  (1 shorter events, 0.0 us)
Async XLA Ops:
  0.0 1.6 %collective-permute-start = (bf16[4,32,256]{2,1,0:T(8,128)(2,1)}, bf16[4,32,256]{2,1,0:T(8,128)(2,1)S(1)}, u32[]{:S(2)}, u32[]{:S(2)}) collective-permute-start(bf16[4,32,256]{2,1,0:T(8,128)(2,1)} %feats.1), channel_id=1, source_target_pairs={{0,8},{8,0},{1,9},{9,1},{2,10},{10,2},{3,11},{11,3},{4,12},{12,4},... | collective-permute-start | bytes 196616 | tf_op jit(solution)/shard_map/ppermute | solution.py:550
  1.6 8.6 %collective-permute-start.3 = (bf16[176,256]{1,0:T(8,128)(2,1)S(1)}, bf16[176,256]{1,0:T(8,128)(2,1)S(1)}, u32[]{:S(2)}, u32[]{:S(2)}) collective-permute-start(bf16[176,256]{1,0:T(8,128)(2,1)S(1)} %get-tuple-element.40.sent), channel_id=1, source_target_pairs={{0,6},{1,7},{2,4},{3,5},{4,2},{5,3},{6,0},{7,1},{8,14},{9,15},{10,... | collective-permute-start | bytes 270344 | tf_op jit(solution)/shard_map/ppermute | solution.py:580
  6.6 7.6 %collective-permute-start.1 = (bf16[160,256]{1,0:T(8,128)(2,1)S(1)}, bf16[160,256]{1,0:T(8,128)(2,1)S(1)}, u32[]{:S(2)}, u32[]{:S(2)}) collective-permute-start(bf16[160,256]{1,0:T(8,128)(2,1)S(1)} %get-tuple-element.39), channel_id=1, source_target_pairs={{0,4},{1,5},{2,6},{3,7},{4,0},{5,1},{6,2},{7,3},{8,12},{9,13},{10,... | collective-permute-start | bytes 245768 | tf_op jit(solution)/shard_map/ppermute | solution.py:580
  6.6 9.6 %collective-permute-start.5 = (bf16[176,256]{1,0:T(8,128)(2,1)S(1)}, bf16[176,256]{1,0:T(8,128)(2,1)S(1)}, u32[]{:S(2)}, u32[]{:S(2)}) collective-permute-start(bf16[176,256]{1,0:T(8,128)(2,1)S(1)} %get-tuple-element.40.sent), channel_id=1, source_target_pairs={{0,1},{1,0},{2,3},{3,2},{4,5},{5,4},{6,7},{7,6},{8,9},{9,8},{10,11... | collective-permute-start | bytes 270344 | tf_op jit(solution)/shard_map/ppermute | solution.py:580
  8.2 8.0 %collective-permute-start.7 = (bf16[176,256]{1,0:T(8,128)(2,1)S(1)}, bf16[176,256]{1,0:T(8,128)(2,1)S(1)}, u32[]{:S(2)}, u32[]{:S(2)}) collective-permute-start(bf16[176,256]{1,0:T(8,128)(2,1)S(1)} %get-tuple-element.40.sent), channel_id=1, source_target_pairs={{0,3},{1,2},{2,1},{3,0},{4,7},{5,6},{6,5},{7,4},{8,11},{9,10},{10,... | collective-permute-start | bytes 270344 | tf_op jit(solution)/shard_map/ppermute | solution.py:580
  8.8 7.5 %collective-permute-start.6 = (bf16[160,256]{1,0:T(8,128)(2,1)S(1)}, bf16[160,256]{1,0:T(8,128)(2,1)S(1)}, u32[]{:S(2)}, u32[]{:S(2)}) collective-permute-start(bf16[160,256]{1,0:T(8,128)(2,1)S(1)} %get-tuple-element.39), channel_id=1, source_target_pairs={{0,2},{1,3},{2,0},{3,1},{4,6},{5,7},{6,4},{7,5},{8,10},{9,11},{10,... | collective-permute-start | bytes 245768 | tf_op jit(solution)/shard_map/ppermute | solution.py:580
  10.2 6.8 %collective-permute-start.4 = (bf16[176,256]{1,0:T(8,128)(2,1)S(1)}, bf16[176,256]{1,0:T(8,128)(2,1)S(1)}, u32[]{:S(2)}, u32[]{:S(2)}) collective-permute-start(bf16[176,256]{1,0:T(8,128)(2,1)S(1)} %collective-permute-done.3.refs_0_), channel_id=1, source_target_pairs={{0,1},{1,0},{2,3},{3,2},{4,5},{5,4},{6,7},{7,6},{8,9},{9,8},{10,11... | collective-permute-start | bytes 270344 | tf_op jit(solution)/shard_map/ppermute | solution.py:580
  14.3 5.4 %collective-permute-start.2 = (bf16[160,256]{1,0:T(8,128)(2,1)S(1)}, bf16[160,256]{1,0:T(8,128)(2,1)S(1)}, u32[]{:S(2)}, u32[]{:S(2)}) collective-permute-start(bf16[160,256]{1,0:T(8,128)(2,1)S(1)} %collective-permute-done.1.refs_0_), channel_id=1, source_target_pairs={{0,1},{1,0},{2,3},{3,2},{4,5},{5,4},{6,7},{7,6},{8,9},{9,8},{10,11... | collective-permute-start | bytes 245768 | tf_op jit(solution)/shard_map/ppermute | solution.py:580
